TPU v7x, 128 devices: a whole 4x4x4 slice. The times are simulated.
128 devices in a mesh: dp: 8 (over x_hi, z), cent: 16 (over x_lo, y, core).
Axes of the slice: x: 4 (x_hi: 2, x_lo: 2; x = x_hi * 2 + x_lo), y: 4, z: 4, core: 2. Of those that a mesh axis runs over, the one named last changes fastest.
Arguments:
- points: bfloat16 [16384, 1024], P(('dp', 'cent')), may hold values from -6 to 6
- centroids: bfloat16 [32768, 1024], P('cent'), may hold values from -6 to 6
Outputs:
- centroids_next: float32 [1024, 32768], P('dp', 'cent')
All inputs are finite; a program needn't handle non-finite values.
Results may differ from a plain program's by a relative error of at most 0.007.
Values may be sent and summed in bfloat16 or wider, within the bound.
No kernel may reach another device: no remote copies, remote signals or barrier semaphores. Data moves between devices by JAX's collectives and lax.ppermute only.
A program may use at most 128 MiB of HBM per device.

v0:
```python
import jax
import jax.numpy as jnp
from jax import lax
from jax.sharding import PartitionSpec as P

BETA_GAIN = 4.0
PRIOR = 0.5


def local(points, centroids):
    features = points.shape[1]
    sharpness = BETA_GAIN * features ** (-0.5)
    gathered = lax.all_gather(points, "cent", axis=0, tiled=True)
    sqnorm = jnp.sum(jnp.square(centroids.astype(jnp.float32)), axis=1)
    total_rows = gathered.shape[0]
    block_rows = min(512, total_rows)
    blocks = gathered.reshape(total_rows // block_rows, block_rows, features)
    shard_cents = centroids.shape[0]

    def logits_of(xblock):
        dots = lax.dot_general(
            xblock, centroids, (((1,), (1,)), ((), ())), preferred_element_type=jnp.float32
        )
        return sharpness * (dots - 0.5 * sqnorm[None, :])

    def resp_of(logits, row_top, row_total):
        return (jnp.exp(logits - row_top[:, None]) / row_total[:, None]).astype(jnp.bfloat16)

    logits = lax.map(logits_of, blocks)
    local_max = jnp.max(logits, axis=-1)
    local_sum = jnp.sum(jnp.exp(logits - local_max[..., None]), axis=-1)
    row_top = lax.pmax(local_max, "cent")
    row_total = lax.psum(local_sum * jnp.exp(local_max - row_top), "cent")
    resp = jax.vmap(resp_of)(logits, row_top, row_total)
    resp = resp.reshape(total_rows, shard_cents)
    counts = jnp.sum(resp.astype(jnp.float32), axis=0)
    dp_count = lax.axis_size("dp")
    dp_index = lax.axis_index("dp")
    column_share = features // dp_count
    numer = lax.psum_scatter(
        lax.dot_general(
            gathered, resp, (((0,), (0,)), ((), ())), preferred_element_type=jnp.float32
        ).astype(jnp.bfloat16),
        "dp",
        scatter_dimension=0,
        tiled=True,
    ).astype(jnp.float32)
    counts_all = lax.psum(counts, "dp")
    own_cols = (
        lax.dynamic_slice_in_dim(centroids, dp_index * column_share, column_share, 1)
        .astype(jnp.float32)
        .T
    )
    result = (numer + PRIOR * own_cols) / (counts_all[None, :] + PRIOR)
    return result


def solution(mesh):
    return jax.shard_map(
        local,
        mesh=mesh,
        in_specs=(P(("dp", "cent"), None), P("cent", None)),
        out_specs=P("dp", "cent"),
        check_vma=False,
    )
```

profile of v0, /device:TPU:1, one launch (start us, length us, event | category | flops | bytes accessed | tf_op | source)
XLA Modules:
  0.0 268.4 jit_solution(6856425457871237441)
XLA Ops:
  6.5 0.0 all-gather.2.cloned.1.call-start
  6.5 0.7 all-gather.2.cloned.1.call-update
  7.3 0.0 reduce-scatter.4.cloned.1.call-start
  7.3 3.1 %multiply_reduce_fusion = f32[2048]{0:T(1024)S(1)} fusion(bf16[2048,1024]{1,0:T(8,128)(2,1)} %param.5), kind=kLoop, calls=%fused_computation.8 | loop fusion | flops 6289408 | bytes 4202496 | tf_op jit(solution)/shard_map/reduce_sum | solution.py:14
  10.4 39.7 %all-gather.2.cloned.1.call-done = bf16[2048,1024]{1,0:T(8,128)(2,1)} async-done(((bf16[128,1024]{1,0:T(8,128)(2,1)}), bf16[2048,1024]{1,0:T(8,128)(2,1)}) %all-gather.2.cloned.1.call-update) | async-done | bytes 4194320 | tf_op jit(solution)/shard_map/all_gather | solution.py:13
  50.1 27.4 %while.10 = (s32[]{:T(128)}, f32[4,512,2048]{2,1,0:T(8,128)}, bf16[4,512,1024]{2,1,0:T(8,128)(2,1)}, bf16[2048,1024]{1,0:T(8,128)(2,1)}, f32[2048]{0:T(1024)S(1)}, /*index=5*/s32[]{:T(128)}) while((s32[]{:T(128)}, f32[4,512,2048]{2,1,0:T(8,128)}, bf16[4,512,1024]{2,1,0:T(8,128)(2,1)}, bf16[2048,1024]{1,0:T(8,128)(2,1)}, f32[2048]{0:T(1024)S(1)}, ...), condition=%wide.region_2.3_spmd, body=%wide.region_1.2_spmd.sunk | while | flops 2149582848 | bytes 9462853 | solution.py:29
  50.1 6.8 %bitcast_dynamic-update-slice_fusion.2 = f32[4,512,2048]{2,1,0:T(8,128)} fusion(f32[4,512,2048]{2,1,0:T(8,128)} %get-tuple-element.83, s32[]{:T(128)} %get-tuple-element.82, bf16[2048,1024]{1,0:T(8,128)(2,1)} %get-tuple-element.91, f32[2048]{0:T(1024)S(1)} %broadcast_multiply_fusion.2, bf16[4,512,1024]{2,1,0:T(8,128)(2,1)} %get-tuple-element.90), kind=kOutput, calls=%fused_computation.clone.1 | convolution fusion | flops 2149580800 | bytes 9446400 | tf_op jit(solution)/shard_map/while/body/eval_jaxpr/dot_general | solution.py:21
  56.9 6.9 %bitcast_dynamic-update-slice_fusion.2 = f32[4,512,2048]{2,1,0:T(8,128)} fusion(f32[4,512,2048]{2,1,0:T(8,128)} %get-tuple-element.83, s32[]{:T(128)} %get-tuple-element.82, bf16[2048,1024]{1,0:T(8,128)(2,1)} %get-tuple-element.91, f32[2048]{0:T(1024)S(1)} %broadcast_multiply_fusion.2, bf16[4,512,1024]{2,1,0:T(8,128)(2,1)} %get-tuple-element.90), kind=kOutput, calls=%fused_computation.clone.1 | convolution fusion | flops 2149580800 | bytes 9446400 | tf_op jit(solution)/shard_map/while/body/eval_jaxpr/dot_general | solution.py:21
  63.7 6.9 %bitcast_dynamic-update-slice_fusion.2 = f32[4,512,2048]{2,1,0:T(8,128)} fusion(f32[4,512,2048]{2,1,0:T(8,128)} %get-tuple-element.83, s32[]{:T(128)} %get-tuple-element.82, bf16[2048,1024]{1,0:T(8,128)(2,1)} %get-tuple-element.91, f32[2048]{0:T(1024)S(1)} %broadcast_multiply_fusion.2, bf16[4,512,1024]{2,1,0:T(8,128)(2,1)} %get-tuple-element.90), kind=kOutput, calls=%fused_computation.clone.1 | convolution fusion | flops 2149580800 | bytes 9446400 | tf_op jit(solution)/shard_map/while/body/eval_jaxpr/dot_general | solution.py:21
  70.6 6.8 %bitcast_dynamic-update-slice_fusion.2 = f32[4,512,2048]{2,1,0:T(8,128)} fusion(f32[4,512,2048]{2,1,0:T(8,128)} %get-tuple-element.83, s32[]{:T(128)} %get-tuple-element.82, bf16[2048,1024]{1,0:T(8,128)(2,1)} %get-tuple-element.91, f32[2048]{0:T(1024)S(1)} %broadcast_multiply_fusion.2, bf16[4,512,1024]{2,1,0:T(8,128)(2,1)} %get-tuple-element.90), kind=kOutput, calls=%fused_computation.clone.1 | convolution fusion | flops 2149580800 | bytes 9446400 | tf_op jit(solution)/shard_map/while/body/eval_jaxpr/dot_general | solution.py:21
  77.4 6.6 %reduce_max.9 = f32[4,512]{1,0:T(4,128)S(1)} reduce(f32[4,512,2048]{2,1,0:T(8,128)} %get-tuple-element.32, f32[]{:T(128)} %constant.20.clone.1), dimensions={2}, to_apply=%region_3.4 | reduce | flops 4192256 | bytes 16785412 | tf_op jit(solution)/shard_map/reduce_max | solution.py:30
  84.0 8.1 %exponential_reduce_fusion = f32[4,512]{1,0:T(4,128)S(1)} fusion(f32[4,512,2048]{2,1,0:T(8,128)} %get-tuple-element.32, f32[4,512]{1,0:T(4,128)S(1)} %reduce_max.9), kind=kLoop, calls=%fused_computation.7 | loop fusion | flops 8386560 | bytes 16793600 | tf_op jit(solution)/shard_map/reduce_sum | solution.py:31
  92.1 27.2 %pmax.7 = f32[4,512]{1,0:T(4,128)S(1)} all-reduce(f32[4,512]{1,0:T(4,128)S(1)} %reduce_max.9), channel_id=1, replica_groups=mesh['dp'=8,'cent'=16] {'cent'}, use_global_device_ids=true, to_apply=%region_4.5 | all-reduce | flops 2048 | bytes 16384 | tf_op jit(solution)/shard_map/pmax | solution.py:32
  119.4 29.8 %psum.14 = f32[4,512]{1,0:T(4,128)S(1)} all-reduce(f32[4,512]{1,0:T(4,128)S(1)} %exponential_multiply_fusion), channel_id=1, replica_groups=mesh['dp'=8,'cent'=16] {'cent'}, use_global_device_ids=true, to_apply=%region_6.7 | all-reduce | flops 2048 | bytes 16384 | tf_op jit(solution)/shard_map/psum | solution.py:33
  149.2 0.0 copy-start
  149.3 8.0 %convert_reduce_fusion = (f32[2048]{0:T(1024)S(1)}, bf16[4,512,2048]{2,1,0:T(8,128)(2,1)S(1)}) fusion(f32[4,512]{1,0:T(4,128)S(1)} %psum.14, f32[4,512,2048]{2,1,0:T(8,128)} %get-tuple-element.32, f32[4,512]{1,0:T(4,128)S(1)} %pmax.7), kind=kLoop, calls=%fused_computation.5 | loop fusion | flops 20969472 | bytes 25190400 | tf_op jit(solution)/shard_map/reduce_sum | solution.py:36
  157.3 0.0 copy-done
  157.3 10.9 %convert_bitcast_fusion = bf16[1024,2048]{0,1:T(8,128)(2,1)} fusion(bf16[2048,2048]{1,0:T(8,128)(2,1)S(1)} %bitcast.23, bf16[2048,1024]{1,0:T(8,128)(2,1)S(1)} %bitcast.25), kind=kOutput, calls=%fused_computation.9 | convolution fusion | flops 8592031744 | bytes 16777216 | tf_op jit(solution)/shard_map/dot_general | solution.py:41
  168.2 6.5 %copy.5 = bf16[1024,2048]{1,0:T(8,128)(2,1)} copy(bf16[1024,2048]{0,1:T(8,128)(2,1)} %convert_bitcast_fusion) | data formatting | bytes 8388608
  174.7 0.0 reduce-scatter.4.cloned.1.call-update
  174.8 20.7 %psum.15 = f32[2048]{0:T(1024)S(1)} all-reduce(f32[2048]{0:T(1024)S(1)} %get-tuple-element.43), channel_id=1, replica_groups=mesh['dp'=8,'cent'=16] {'dp'}, use_global_device_ids=true, to_apply=%region_9.10 | all-reduce | flops 2048 | bytes 16384 | tf_op jit(solution)/shard_map/psum | solution.py:48
  195.5 62.0 %reduce-scatter.4.cloned.1.call-done = bf16[128,2048]{1,0:T(8,128)(2,1)} async-done(((bf16[1024,2048]{1,0:T(8,128)(2,1)}), bf16[128,2048]{1,0:T(8,128)(2,1)}) %reduce-scatter.4.cloned.1.call-update) | async-done | bytes 524304
  257.5 1.3 copy.6
  258.8 1.4 fusion.3
  260.2 1.3 copy.4
  (7 shorter events, 0.0 us)
Async XLA Ops:
  6.5 43.5 %all-gather.2.cloned.1.call-start = ((), (), s32[]{:S(2)}) async-start(), calls=%async_computation.1 | async-start | bytes 4456448 | tf_op jit(solution)/shard_map/all_gather | solution.py:13
  7.3 250.2 %reduce-scatter.4.cloned.1.call-start = ((), (), s32[]{:S(2)}) async-start(), calls=%async_computation.2 | async-start | bytes 4718592
  149.2 8.1 %copy-start = (bf16[4,512,1024]{2,1,0:T(8,128)(2,1)S(1)}, bf16[4,512,1024]{2,1,0:T(8,128)(2,1)}, u32[]{:S(2)}) copy-start(bf16[4,512,1024]{2,1,0:T(8,128)(2,1)} %get-tuple-element.103) | copy-start | bytes 12582916
Sparse Core Ops, SparseCore 0:
  9.1 40.9 all-gather.1
  174.9 82.5 reduce-scatter.3
where the time goes:
time: 269 us; the launch traced here: 268 us
  waiting for transfers between devices  102 us (38%)
  blocking collectives  77.8 us (29%)
  matrix products  38.3 us (14%)
  other arithmetic  27.2 us (10%)
  between operations  13.5 us (5%)
  local copies, waits for them, and re-layouts  9.11 us (3%)
    unnamed x3, waiting for transfers between devices  62.7 us
    all_gather x1, waiting for transfers between devices, local(): gathered = lax.all_gather(points, 'cent', axis=0, tiled=True)  39.7 us
    psum x1, blocking collectives, local(): row_total = lax.psum(local_sum * jnp.exp(local_max - row_top), 'cent')  29.8 us
    dot_general x4, matrix products, logits_of(): lax.dot_general(xblock, centroids, (((1,), (1,)), ((), ())), preferred_el...  27.4 us
    pmax x1, blocking collectives, local(): row_top = lax.pmax(local_max, 'cent')  27.2 us
    psum x1, blocking collectives, local(): counts_all = lax.psum(counts, 'dp')  20.7 us
    dot_general x1, matrix products, local(): lax.dot_general(gathered, resp, (((0,), (0,)), ((), ())), preferred_eleme...  10.9 us
    reduce_sum x1, other arithmetic, local(): local_sum = jnp.sum(jnp.exp(logits - local_max[..., None]), axis=-1)  8.12 us
  transfers between devices with their start and end apart: 2, of which 2 were waited for; matrix products, arithmetic and copies ran while one was open for 1% of the time, Pallas kernels for 0%

commit v1 on v0

v1 whole, which is shorter than its diff:
```python
import functools
import math

import jax
import jax.numpy as jnp
from jax import lax
from jax.experimental import pallas as pl
from jax.experimental.pallas import tpu as pltpu
from jax.sharding import PartitionSpec as P

BETA_GAIN = 4.0
PRIOR = 0.5
F32 = jnp.float32
BF16 = jnp.bfloat16

NX, NY, NZ = 4, 4, 4
AXES = ("dp", "cent")
COUNT_ROWS = 32
GROUPS = ((2, 1), (3, 0))


def _send(a, move):
    pairs = []
    for xh in range(2):
        for z in range(NZ):
            for xl in range(2):
                for y in range(NY):
                    for core in range(2):
                        src = (xh * 4 + z) * 16 + (xl * 4 + y) * 2 + core
                        x2, y2, z2, core2 = move(xh * 2 + xl, y, z, core)
                        x2, y2, z2 = x2 % NX, y2 % NY, z2 % NZ
                        dst = ((x2 // 2) * 4 + z2) * 16 + ((x2 % 2) * 4 + y2) * 2 + core2
                        pairs.append((src, dst))
    return lax.ppermute(a, AXES, pairs)


def send_first(a, d):
    return _send(a, lambda x, y, z, c: (x, y + d, z, c) if c == 0 else (x + d, y, z, c))


def send_second(a, d):
    return _send(a, lambda x, y, z, c: (x + d, y, z, c) if c == 0 else (x, y + d, z, c))


def send_core(a):
    return _send(a, lambda x, y, z, c: (x, y, z, 1 - c))


def send_owner(a, dxh, dz):
    return _send(a, lambda x, y, z, c: (x + 2 * dxh, y, z + dz, c))


def _full(shape):
    return pl.BlockSpec(shape, lambda *_: (0,) * len(shape))


def _norm_kernel(a_ref, b_ref, o_ref):
    for i, r in enumerate((a_ref, b_ref)):
        v = r[...].astype(F32)
        s = 0.5 * jnp.sum(v * v, axis=1, keepdims=True)
        o_ref[i] = jnp.broadcast_to(s, (s.shape[0], 128))


def half_norms(own, sib):
    k, d = own.shape
    step = 256
    return pl.pallas_call(
        _norm_kernel,
        out_shape=jax.ShapeDtypeStruct((2, k, 128), F32),
        grid=(k // step,),
        in_specs=[pl.BlockSpec((step, d), lambda i: (i, 0))] * 2,
        out_specs=pl.BlockSpec((2, step, 128), lambda i: (0, i, 0)),
        name="half_norms",
    )(own, sib)


def _score_kernel(gain, x_ref, own_ref, sib_ref, h_ref, w_ref, st_ref, u_ref):
    x = x_ref[...]
    rb = x.shape[0]
    k = own_ref.shape[0]
    kb = 256
    maxima = []
    for b, c_ref in enumerate((own_ref, sib_ref)):
        m = None
        for j in range(k // kb):
            rows = slice(j * kb, (j + 1) * kb)
            dots = lax.dot_general(
                c_ref[rows, :], x, (((1,), (1,)), ((), ())), preferred_element_type=F32
            )
            u = dots - jnp.tile(h_ref[b, rows, :], (1, rb // 128))
            u_ref[b, rows, :] = u
            mj = jnp.max(u, axis=0, keepdims=True)
            m = mj if m is None else jnp.maximum(m, mj)
        maxima.append(m)
    for b in range(2):
        m = maxima[b]
        s = None
        for j in range(k // kb):
            rows = slice(j * kb, (j + 1) * kb)
            w = jnp.exp2((u_ref[b, rows, :] - m) * gain)
            sj = jnp.sum(w, axis=0, keepdims=True)
            s = sj if s is None else s + sj
            w_ref[b, rows, :] = w.astype(BF16)
        st_ref[2 * b : 2 * b + 1, :] = m
        st_ref[2 * b + 1 : 2 * b + 2, :] = s
    st_ref[4:8, :] = jnp.zeros((4, rb), F32)


def score(x, own, sib, h, gain):
    r, d = x.shape
    k = own.shape[0]
    rb = min(256, r)
    return pl.pallas_call(
        functools.partial(_score_kernel, gain),
        out_shape=(
            jax.ShapeDtypeStruct((2, k, r), BF16),
            jax.ShapeDtypeStruct((8, r), F32),
        ),
        grid=(r // rb,),
        in_specs=[
            pl.BlockSpec((rb, d), lambda i: (i, 0)),
            _full((k, d)),
            _full((k, d)),
            _full((2, k, 128)),
        ],
        out_specs=(
            pl.BlockSpec((2, k, rb), lambda i: (0, 0, i)),
            pl.BlockSpec((8, rb), lambda i: (0, i)),
        ),
        scratch_shapes=[pltpu.VMEM((2, k, rb), F32)],
        compiler_params=pltpu.CompilerParams(vmem_limit_bytes=40 << 20),
        cost_estimate=pl.CostEstimate(
            flops=4 * r * k * d, bytes_accessed=4 * k * d + 2 * r * d + 4 * r * k,
            transcendentals=2 * r * k,
        ),
        name="score",
    )(x, own, sib, h)


def _sum_kernel(half, n_arr, n_blk, stacked, has_add, fb_ref, *refs):
    w_refs = refs[:n_arr]
    x_refs = refs[n_arr : n_arr + n_arr * n_blk]
    pos = n_arr + n_arr * n_blk
    sc_ref = refs[pos]
    pos += 1
    add_ref = None
    if has_add:
        add_ref = refs[pos]
        pos += 1
    n_out = 1 if stacked else n_blk
    outs = refs[pos : pos + n_out]
    xb_ref, cnt_ref = refs[pos + n_out :]
    i = pl.program_id(0)
    steps = pl.num_programs(0)
    kb = w_refs[0].shape[1]
    r = w_refs[0].shape[2]
    k = outs[0].shape[-2] - COUNT_ROWS

    @pl.when(i == 0)
    def _():
        for a in range(n_arr):
            for f in range(n_blk):
                xb_ref[a * r : (a + 1) * r, f * 128 : (f + 1) * 128] = x_refs[a * n_blk + f][...]

    acc = None
    lanes = None
    for a in range(n_arr):
        sc = sc_ref[half : half + 1, a * r : (a + 1) * r]
        w = (w_refs[a][0].astype(F32) * sc).astype(BF16)
        wf = w.astype(F32)
        for t in range(r // 128):
            part = wf[:, t * 128 : (t + 1) * 128]
            lanes = part if lanes is None else lanes + part
        d = jnp.dot(w, xb_ref[a * r : (a + 1) * r, :], preferred_element_type=F32)
        acc = d if acc is None else acc + d
    col = jnp.sum(lanes.T, axis=0, keepdims=True)
    per = kb // 128
    rows = jnp.concatenate([col[:, t * 128 : (t + 1) * 128] for t in range(per)], axis=0)
    for j in range(k // kb):

        @pl.when(i == j)
        def _():
            cnt_ref[j * per : (j + 1) * per, :] = rows

    row0 = pl.multiple_of(i * kb, kb)
    for f in range(n_blk):
        v = acc[:, f * 128 : (f + 1) * 128]
        if has_add:
            v = v + add_ref[f, pl.ds(row0, kb), :].astype(F32)
        v = v.astype(BF16)
        if stacked:
            outs[0][f, pl.ds(row0, kb), :] = v
        else:
            outs[f][pl.ds(row0, kb), :] = v

    @pl.when(i == steps - 1)
    def _():
        c = cnt_ref[...]
        if has_add:
            t = add_ref[0, k : k + COUNT_ROWS, :].astype(F32)
            c = c + ((t[0:8] + t[8:16]) + t[16:24])
        hi = c.astype(BF16).astype(F32)
        mid = (c - hi).astype(BF16).astype(F32)
        lo = (c - hi) - mid
        packed = jnp.concatenate([hi, mid, lo, jnp.zeros_like(lo)], axis=0).astype(BF16)
        for f in range(n_blk):
            if stacked:
                outs[0][f, k : k + COUNT_ROWS, :] = packed
            else:
                outs[f][k : k + COUNT_ROWS, :] = packed


def weighted_sums(half, ws, xs, scales, blocks, add=None, stacked=False):
    n_arr, n_blk = len(ws), blocks.shape[0]
    k, r = ws[0].shape[1:]
    kb = 256
    rows = k + COUNT_ROWS
    in_specs = [pl.BlockSpec((1, kb, r), lambda i, fb: (half, i, 0)) for _ in ws]
    for _ in xs:
        for f in range(n_blk):
            in_specs.append(pl.BlockSpec((r, 128), lambda i, fb, f=f: (0, fb[f])))
    in_specs.append(_full(scales.shape))
    operands = list(ws)
    for x in xs:
        operands += [x] * n_blk
    operands.append(scales)
    if add is not None:
        in_specs.append(_full(add.shape))
        operands.append(add)
    if stacked:
        out_shape = [jax.ShapeDtypeStruct((n_blk, rows, 128), BF16)]
        out_specs = [_full((n_blk, rows, 128))]
    else:
        out_shape = [jax.ShapeDtypeStruct((rows, 128), BF16)] * n_blk
        out_specs = [_full((rows, 128))] * n_blk
    return pl.pallas_call(
        functools.partial(_sum_kernel, half, n_arr, n_blk, stacked, add is not None),
        out_shape=out_shape,
        grid_spec=pltpu.PrefetchScalarGridSpec(
            num_scalar_prefetch=1,
            grid=(k // kb,),
            in_specs=in_specs,
            out_specs=out_specs,
            scratch_shapes=[
                pltpu.VMEM((n_arr * r, n_blk * 128), BF16),
                pltpu.VMEM((8, 128), F32),
            ],
        ),
        compiler_params=pltpu.CompilerParams(vmem_limit_bytes=40 << 20),
        cost_estimate=pl.CostEstimate(
            flops=2 * k * n_arr * r * n_blk * 128,
            bytes_accessed=2 * n_arr * r * (k + n_blk * 128),
            transcendentals=0,
        ),
        name="sums_sib" if add is None else "sums_own",
    )(blocks, *operands)


def _final_kernel(n, idx_ref, *refs):
    parts = (refs[:n], refs[n : 2 * n])
    c_ref, o_ref = refs[2 * n :]
    k = c_ref.shape[0] // 2
    for j in range(2):
        side = idx_ref[0] if j == 0 else 1 - idx_ref[0]
        off = pl.multiple_of(side * k, k)
        total = None
        for p in parts[j]:
            v = p[...].astype(F32)
            total = v if total is None else total + v
        t = total[k : k + 24]
        c = (t[0:8] + t[8:16]) + t[16:24]
        cnt = jnp.concatenate([c[q : q + 1, :] for q in range(k // 128)], axis=1)
        top = total[:k] + PRIOR * c_ref[pl.ds(off, k), :].astype(F32)
        o_ref[:, pl.ds(off, k)] = top.T / (cnt + PRIOR)


def finish(idx, mine, other, centroids):
    rows = mine[0].shape[0]
    k2 = centroids.shape[0]
    return pl.pallas_call(
        functools.partial(_final_kernel, len(mine)),
        out_shape=jax.ShapeDtypeStruct((128, k2), F32),
        grid_spec=pltpu.PrefetchScalarGridSpec(
            num_scalar_prefetch=1,
            grid=(1,),
            in_specs=[_full((rows, 128))] * (2 * len(mine))
            + [pl.BlockSpec((k2, 128), lambda i, idx: (0, idx[1]))],
            out_specs=_full((128, k2)),
        ),
        compiler_params=pltpu.CompilerParams(vmem_limit_bytes=40 << 20),
        name="finish",
    )(idx, *mine, *other, centroids)


def _merge(pairs, gain):
    m = functools.reduce(jnp.maximum, [p[0] for p in pairs])
    s = sum(p[1] * jnp.exp2((p[0] - m) * gain) for p in pairs)
    return m, s


def local(points, centroids):
    features = points.shape[1]
    gain = BETA_GAIN * features ** (-0.5) * math.log2(math.e)
    dp = lax.axis_index("dp")
    xh, z = dp // NZ, dp % NZ
    half_cents = centroids.shape[0] // 2

    got = [points] + [send_first(points, d) for d in (1, 2, 3)]
    own = lax.dynamic_slice_in_dim(centroids, xh * half_cents, half_cents, 0)
    sib = send_core(own)
    line = jnp.concatenate(got, axis=0)
    xs = [line] + [send_second(line, d) for d in (1, 2, 3)]
    h = half_norms(own, sib)

    ws, stats = [None] * 4, [None] * 4
    for k in (0, 1, 3, 2):
        ws[k], stats[k] = score(xs[k], own, sib, h, gain)
    st = jnp.stack(stats)
    mb, sb = st[:, 0:4:2, :], st[:, 1:4:2, :]
    m, s = _merge([(mb[:, b], sb[:, b]) for b in range(2)], gain)
    pack = jnp.stack([m, s]).reshape(2, 4, 4, -1)
    every = [pack] + [jnp.roll(send_first(pack, d), d, axis=2) for d in (1, 2, 3)]
    pack = jnp.stack(_merge([(e[0], e[1]) for e in every], gain))
    every = [pack] + [jnp.roll(send_second(pack, d), d, axis=1) for d in (1, 2, 3)]
    top, total = _merge([(e[0], e[1]) for e in every], gain)
    top, total = top.reshape(4, 1, -1), total.reshape(4, 1, -1)
    scales = jnp.exp2((mb - top) * gain) / total
    scales = scales.transpose(1, 0, 2).reshape(2, -1)

    mine, other = [], []
    for group in GROUPS:
        blocks = jnp.stack(
            [((xh + dxh) % 2) * NZ + (z + dz) % NZ for dz in group for dxh in (1, 0)]
        ).astype(jnp.int32)
        (part,) = weighted_sums(1, ws, xs, scales, blocks, stacked=True)
        part = send_core(part)
        sums = weighted_sums(0, ws, xs, scales, blocks, add=part)
        for n, (dz, dxh) in enumerate((dz, dxh) for dz in group for dxh in (1, 0)):
            if dxh == 0:
                mine.append(sums[n] if dz == 0 else send_owner(sums[n], 0, dz))
            else:
                other.append(send_owner(sums[n], 1, dz))
    idx = jnp.stack([xh, dp]).astype(jnp.int32)
    return finish(idx, mine, other, centroids)


def solution(mesh):
    return jax.shard_map(
        local,
        mesh=mesh,
        in_specs=(P(("dp", "cent"), None), P("cent", None)),
        out_specs=P("dp", "cent"),
        check_vma=False,
    )
```

time: 269 us -> 144 us (0.54)
  blocking collectives: 77.8 us -> 0 us
  waiting for transfers between devices: 102 us -> 39.6 us
  Pallas kernels: 0 us -> 51 us
  matrix products: 38.3 us -> 0 us
  starting transfers between devices: 0.04 us -> 35.7 us
  other arithmetic: 27.2 us -> 0.54 us
  between operations: 13.5 us -> 0.28 us
  local copies, waits for them, and re-layouts: 9.11 us -> 16.6 us
    unnamed x3 -> x0, waiting for transfers between devices: 62.7 us -> none
    pallas_call x0 -> x10, Pallas kernels: none -> 51 us  [the longest x4 23.6 us: weighted_sums(): pl.pallas_call(functools.partial(_sum_kernel, half, n_arr, n_blk, stacked...]
    psum x2 -> x0, blocking collectives: 50.6 us -> none  [the longest x1 29.8 us: local(): row_total = lax.psum(local_sum * jnp.exp(local_max - row_top), 'cent')]
    all_gather x1 -> x0, waiting for transfers between devices: 39.7 us -> none  [local(): gathered = lax.all_gather(points, 'cent', axis=0, tiled=True)]
    ppermute x0 -> x22, waiting for transfers between devices: none -> 39.6 us  [_send(): return lax.ppermute(a, AXES, pairs)]
    dot_general x5 -> x0, matrix products: 38.3 us -> none  [the longest x4 27.4 us: logits_of(): lax.dot_general(xblock, centroids, (((1,), (1,)), ((), ())), preferred_el...]
    ppermute x0 -> x22, starting transfers between devices: none -> 35.7 us  [_send(): return lax.ppermute(a, AXES, pairs)]
    pmax x1 -> x0, blocking collectives: 27.2 us -> none  [local(): row_top = lax.pmax(local_max, 'cent')]
  transfers between devices with their start and end apart: 2 -> 22, of which waited for: 2 -> 10; matrix products, arithmetic and copies ran while one was open for 1% -> 0% of each run, Pallas kernels for 0% -> 26%
where the time goes in v1:
time: 144 us
  Pallas kernels  51 us (35%)
  waiting for transfers between devices  39.6 us (28%)
  starting transfers between devices  35.7 us (25%)
  local copies, waits for them, and re-layouts  16.6 us (12%)
    ppermute x22, waiting for transfers between devices, _send(): return lax.ppermute(a, AXES, pairs)  39.6 us
    ppermute x22, starting transfers between devices, _send(): return lax.ppermute(a, AXES, pairs)  35.7 us
    pallas_call x4, Pallas kernels, weighted_sums(): pl.pallas_call(functools.partial(_sum_kernel, half, n_arr, n_blk, stacked...  23.6 us
    pallas_call x4, Pallas kernels, score(): pl.pallas_call(functools.partial(_score_kernel, gain), out_shape=(jax.Sha...  20.9 us
    unnamed x30, local copies, waits for them, and re-layouts  14.6 us
    pallas_call x1, Pallas kernels, half_norms(): pl.pallas_call(_norm_kernel, out_shape=jax.ShapeDtypeStruct((2, k, 128),...  4.43 us
  transfers between devices with their start and end apart: 22, of which 10 were waited for; matrix products, arithmetic and copies ran while one was open for 0% of the time, Pallas kernels for 26%

profile of v1, /device:TPU:1, one launch (start us, length us, event | category | flops | bytes accessed | tf_op | source)
XLA Modules:
  0.0 143.8 jit_solution(7070003264987377697)
XLA Ops:
  0.0 1.8 %constant_dynamic-slice_fusion.a_ref.own_ref = bf16[1024,1024]{1,0:T(8,128)(2,1)S(1)} fusion(bf16[2048,1024]{1,0:T(8,128)(2,1)} %refs_8_.1, s32[]{:T(128)S(6)} %select_n.64), kind=kLoop, calls=%fused_computation.43 | loop fusion | bytes 4194308 | tf_op jit(solution)/shard_map/dynamic_slice | solution.py:309
  1.8 1.5 %collective-permute-start.3 = (bf16[1024,1024]{1,0:T(8,128)(2,1)S(1)}, bf16[1024,1024]{1,0:T(8,128)(2,1)}, u32[]{:S(2)}, u32[]{:S(2)}) collective-permute-start(bf16[1024,1024]{1,0:T(8,128)(2,1)S(1)} %constant_dynamic-slice_fusion.a_ref.own_ref), channel_id=1, source_target_pairs={{0,1},{1,0},{2,3},{3,2},{4,5},{5,4},{6,7},{7,6},{8,9},{9,8},{10,11... | collective-permute-start | bytes 6291464 | tf_op jit(solution)/shard_map/ppermute | solution.py:34
  3.3 1.3 collective-permute-start
  4.6 2.5 %collective-permute-start.1 = (bf16[128,1024]{1,0:T(8,128)(2,1)S(1)}, bf16[128,1024]{1,0:T(8,128)(2,1)S(1)}, u32[]{:S(2)}, u32[]{:S(2)}) collective-permute-start(bf16[128,1024]{1,0:T(8,128)(2,1)S(1)} %copy-done.12), channel_id=1, source_target_pairs={{0,4},{1,65},{2,6},{3,67},{4,0},{5,69},{6,2},{7,71},{8,12},{9,73},... | collective-permute-start | bytes 786440 | tf_op jit(solution)/shard_map/ppermute | solution.py:34
  7.1 1.2 collective-permute-start.2
  8.2 1.8 %collective-permute-done = bf16[128,1024]{1,0:T(8,128)(2,1)S(1)} collective-permute-done((bf16[128,1024]{1,0:T(8,128)(2,1)S(1)}, bf16[128,1024]{1,0:T(8,128)(2,1)S(1)}, u32[]{:S(2)}, u32[]{:S(2)}) %collective-permute-start) | collective-permute-done | bytes 262176 | tf_op jit(solution)/shard_map/ppermute | solution.py:34
  10.1 3.9 %collective-permute-done.1 = bf16[128,1024]{1,0:T(8,128)(2,1)S(1)} collective-permute-done((bf16[128,1024]{1,0:T(8,128)(2,1)S(1)}, bf16[128,1024]{1,0:T(8,128)(2,1)S(1)}, u32[]{:S(2)}, u32[]{:S(2)}) %collective-permute-start.1) | collective-permute-done | bytes 262176 | tf_op jit(solution)/shard_map/ppermute | solution.py:34
  14.0 2.5 %collective-permute-start.6 = (bf16[512,1024]{1,0:T(8,128)(2,1)S(1)}, bf16[512,1024]{1,0:T(8,128)(2,1)S(1)}, u32[]{:S(2)}, u32[]{:S(2)}) collective-permute-start(bf16[512,1024]{1,0:T(8,128)(2,1)S(1)} %constant_dynamic-update-slice_fusion.x_ref.refs_4_.refs_5_.refs_6_.refs_7_), channel_id=1, source_target_pairs={{0,72},{1,7},{2,74},{3,1},{4,76},{5,3},{6,78},{7,5},{8,0},{9,15},{... | collective-permute-start | bytes 3145736 | tf_op jit(solution)/shard_map/ppermute | solution.py:34
  16.9 0.7 collective-permute-start.4
  17.5 4.4 %half_norms.1.h_ref = f32[2,1024,128]{2,1,0:T(8,128)} custom-call(bf16[1024,1024]{1,0:T(8,128)(2,1)} %copy-done.9, bf16[1024,1024]{1,0:T(8,128)(2,1)} %collective-permute-done.3.b_ref.sib_ref), custom_call_target="tpu_custom_call" | custom-call | tf_op jit(solution)/shard_map/half_norms/pallas_call | solution.py:67
  22.0 1.6 %copy-done.10 = bf16[1024,1024]{1,0:T(8,128)(2,1)S(1)} copy-done((bf16[1024,1024]{1,0:T(8,128)(2,1)S(1)}, bf16[1024,1024]{1,0:T(8,128)(2,1)}, u32[]{:S(2)}) %copy-start.10) | copy-done | bytes 2097176
  23.6 1.2 copy-done.11
  24.8 5.2 %score.4 = (bf16[2,1024,512]{2,1,0:T(8,128)(2,1)S(1)}, f32[8,512]{1,0:T(8,128)S(1)}) custom-call(bf16[512,1024]{1,0:T(8,128)(2,1)S(1)} %constant_dynamic-update-slice_fusion.x_ref.refs_4_.refs_5_.refs_6_.refs_7_, bf16[1024,1024]{1,0:T(8,128)(2,1)S(1)} %copy-done.10, bf16[1024,1024]{1,0:T(8,128)(2,1)} %collective-permute-done.3.b_ref.sib_ref, ...), custom_call_target="tpu_custom_call" | custom-call | flops 2147483648 | bytes 7340032 | tf_op jit(solution)/shard_map/score/pallas_call | solution.py:113
  30.0 1.3 copy-done
  31.3 8.2 %collective-permute-done.6.x_ref.refs_16_.refs_17_.refs_18_.refs_19_ = bf16[512,1024]{1,0:T(8,128)(2,1)S(1)} collective-permute-done((bf16[512,1024]{1,0:T(8,128)(2,1)S(1)}, bf16[512,1024]{1,0:T(8,128)(2,1)S(1)}, u32[]{:S(2)}, u32[]{:S(2)}) %collective-permute-start.6) | collective-permute-done | bytes 1048608 | tf_op jit(solution)/shard_map/ppermute | solution.py:34
  39.5 5.2 %score.7 = (bf16[2,1024,512]{2,1,0:T(8,128)(2,1)S(1)}, f32[8,512]{1,0:T(8,128)S(1)}) custom-call(bf16[512,1024]{1,0:T(8,128)(2,1)S(1)} %collective-permute-done.6.x_ref.refs_16_.refs_17_.refs_18_.refs_19_, bf16[1024,1024]{1,0:T(8,128)(2,1)S(1)} %copy-done.10, bf16[1024,1024]{1,0:T(8,128)(2,1)} %collective-permute-done.3.b_ref.sib_ref, ...), custom_call_target="tpu_custom_call" | custom-call | flops 2147483648 | bytes 7340032 | tf_op jit(solution)/shard_map/score/pallas_call | solution.py:113
  44.7 1.3 copy-done.2
  46.0 5.2 %score.6 = (bf16[2,1024,512]{2,1,0:T(8,128)(2,1)S(1)}, f32[8,512]{1,0:T(8,128)S(1)}) custom-call(bf16[512,1024]{1,0:T(8,128)(2,1)S(1)} %collective-permute-done.5.x_ref.refs_12_.refs_13_.refs_14_.refs_15_, bf16[1024,1024]{1,0:T(8,128)(2,1)S(1)} %copy-done.10, bf16[1024,1024]{1,0:T(8,128)(2,1)} %collective-permute-done.3.b_ref.sib_ref, ...), custom_call_target="tpu_custom_call" | custom-call | flops 2147483648 | bytes 7340032 | tf_op jit(solution)/shard_map/score/pallas_call | solution.py:113
  51.2 1.4 copy-done.4
  52.6 5.4 %score.5 = (bf16[2,1024,512]{2,1,0:T(8,128)(2,1)S(1)}, f32[8,512]{1,0:T(8,128)S(1)}) custom-call(bf16[512,1024]{1,0:T(8,128)(2,1)} %collective-permute-done.4.x_ref.refs_8_.refs_9_.refs_10_.refs_11_, bf16[1024,1024]{1,0:T(8,128)(2,1)S(1)} %copy-done.10, bf16[1024,1024]{1,0:T(8,128)(2,1)} %collective-permute-done.3.b_ref.sib_ref, f32[2,1024,128]{2,1,0:T(8,128)S(1)} %copy-done.11), custom_call_target="tpu_custom_call" | custom-call | flops 2147483648 | bytes 7340032 | tf_op jit(solution)/shard_map/score/pallas_call | solution.py:113
  57.9 1.4 copy-done.6
  59.5 2.7 %collective-permute-start.8 = (f32[2,4,4,128]{3,2,1,0:T(4,128)S(1)}, f32[2,4,4,128]{3,2,1,0:T(4,128)S(1)}, u32[]{:S(2)}, u32[]{:S(2)}) collective-permute-start(f32[2,4,4,128]{3,2,1,0:T(4,128)S(1)} %pad_maximum_fusion.1), channel_id=1, source_target_pairs={{0,4},{1,65},{2,6},{3,67},{4,0},{5,69},{6,2},{7,71},{8,12},{9,73},... | collective-permute-start | bytes 49160 | tf_op jit(solution)/shard_map/ppermute | solution.py:34
  62.2 1.1 collective-permute-start.9
  63.2 0.4 collective-permute-start.7
  63.7 1.1 collective-permute-done.9
  64.8 2.2 %collective-permute-done.7 = f32[2,4,4,128]{3,2,1,0:T(4,128)S(1)} collective-permute-done((f32[2,4,4,128]{3,2,1,0:T(4,128)S(1)}, f32[2,4,4,128]{3,2,1,0:T(4,128)S(1)}, u32[]{:S(2)}, u32[]{:S(2)}) %collective-permute-start.7) | collective-permute-done | bytes 16416 | tf_op jit(solution)/shard_map/ppermute | solution.py:34
  67.1 3.3 %collective-permute-start.12 = (f32[2,4,4,128]{3,2,1,0:T(4,128)S(1)}, f32[2,4,4,128]{3,2,1,0:T(4,128)S(1)}, u32[]{:S(2)}, u32[]{:S(2)}) collective-permute-start(f32[2,4,4,128]{3,2,1,0:T(4,128)S(1)} %pad_maximum_fusion.2), channel_id=1, source_target_pairs={{0,72},{1,7},{2,74},{3,1},{4,76},{5,3},{6,78},{7,5},{8,0},{9,15},{... | collective-permute-start | bytes 49160 | tf_op jit(solution)/shard_map/ppermute | solution.py:34
  70.6 0.6 collective-permute-start.10
  71.3 3.4 %collective-permute-done.11 = f32[2,4,4,128]{3,2,1,0:T(4,128)S(1)} collective-permute-done((f32[2,4,4,128]{3,2,1,0:T(4,128)S(1)}, f32[2,4,4,128]{3,2,1,0:T(4,128)S(1)}, u32[]{:S(2)}, u32[]{:S(2)}) %collective-permute-start.11) | collective-permute-done | bytes 16416 | tf_op jit(solution)/shard_map/ppermute | solution.py:34
  75.0 1.6 %copy-done.1 = bf16[2,1024,512]{2,1,0:T(8,128)(2,1)S(1)} copy-done((bf16[2,1024,512]{2,1,0:T(8,128)(2,1)S(1)}, bf16[2,1024,512]{2,1,0:T(8,128)(2,1)}, u32[]{:S(2)}) %copy-start.1) | copy-done | bytes 2097176
  76.6 1.6 %copy-done.3 = bf16[2,1024,512]{2,1,0:T(8,128)(2,1)S(1)} copy-done((bf16[2,1024,512]{2,1,0:T(8,128)(2,1)S(1)}, bf16[2,1024,512]{2,1,0:T(8,128)(2,1)}, u32[]{:S(2)}) %copy-start.3) | copy-done | bytes 2097176
  78.2 1.6 %copy-done.5 = bf16[2,1024,512]{2,1,0:T(8,128)(2,1)S(1)} copy-done((bf16[2,1024,512]{2,1,0:T(8,128)(2,1)S(1)}, bf16[2,1024,512]{2,1,0:T(8,128)(2,1)}, u32[]{:S(2)}) %copy-start.5) | copy-done | bytes 2097176
  79.8 1.6 %copy-done.7 = bf16[2,1024,512]{2,1,0:T(8,128)(2,1)S(1)} copy-done((bf16[2,1024,512]{2,1,0:T(8,128)(2,1)S(1)}, bf16[2,1024,512]{2,1,0:T(8,128)(2,1)}, u32[]{:S(2)}) %copy-start.7) | copy-done | bytes 2097176
  81.4 5.8 %sums_sib.2 = bf16[4,1056,128]{2,1,0:T(8,128)(2,1)S(1)} custom-call(s32[4]{0:T(128)S(1)} %pad_add_fusion.1.fb_ref, bf16[2,1024,512]{2,1,0:T(8,128)(2,1)S(1)} %copy-done.1, bf16[2,1024,512]{2,1,0:T(8,128)(2,1)S(1)} %copy-done.7, bf16[2,1024,512]{2,1,0:T(8,128)(2,1)S(1)} %copy-done.5, bf16[2,1024,512]{2,1,0:T(8,128)(2,1)S(1)} %copy-done.3, ...), custom_call_target="tpu_custom_call" | custom-call | flops 2147483648 | bytes 6291456 | tf_op jit(solution)/shard_map/sums_sib/pallas_call | solution.py:236
  87.2 5.5 %collective-permute-start.13 = (bf16[4,1056,128]{2,1,0:T(8,128)(2,1)S(1)}, bf16[4,1056,128]{2,1,0:T(8,128)(2,1)S(1)}, u32[]{:S(2)}, u32[]{:S(2)}) collective-permute-start(bf16[4,1056,128]{2,1,0:T(8,128)(2,1)S(1)} %sums_sib.2), channel_id=1, source_target_pairs={{0,1},{1,0},{2,3},{3,2},{4,5},{5,4},{6,7},{7,6},{8,9},{9,8},{10,11... | collective-permute-start | bytes 3244040 | tf_op jit(solution)/shard_map/ppermute | solution.py:34
  92.7 5.7 %sums_sib.3 = bf16[4,1056,128]{2,1,0:T(8,128)(2,1)S(1)} custom-call(s32[4]{0:T(128)S(1)} %pad_add_fusion.2.fb_ref, bf16[2,1024,512]{2,1,0:T(8,128)(2,1)S(1)} %copy-done.1, bf16[2,1024,512]{2,1,0:T(8,128)(2,1)S(1)} %copy-done.7, bf16[2,1024,512]{2,1,0:T(8,128)(2,1)S(1)} %copy-done.5, bf16[2,1024,512]{2,1,0:T(8,128)(2,1)S(1)} %copy-done.3, ...), custom_call_target="tpu_custom_call" | custom-call | flops 2147483648 | bytes 6291456 | tf_op jit(solution)/shard_map/sums_sib/pallas_call | solution.py:236
  98.6 6.0 %sums_own.2 = (bf16[1056,128]{1,0:T(8,128)(2,1)S(1)}, bf16[1056,128]{1,0:T(8,128)(2,1)S(1)}, bf16[1056,128]{1,0:T(8,128)(2,1)S(1)}, bf16[1056,128]{1,0:T(8,128)(2,1)S(1)}) custom-call(s32[4]{0:T(128)S(1)} %pad_add_fusion.1.fb_ref, bf16[2,1024,512]{2,1,0:T(8,128)(2,1)S(1)} %copy-done.1, bf16[2,1024,512]{2,1,0:T(8,128)(2,1)S(1)} %copy-done.7, ...), custom_call_target="tpu_custom_call" | custom-call | flops 2147483648 | bytes 6291456 | tf_op jit(solution)/shard_map/sums_own/pallas_call | solution.py:236
  104.6 3.7 %collective-permute-start.14 = (bf16[1056,128]{1,0:T(8,128)(2,1)S(1)}, bf16[1056,128]{1,0:T(8,128)(2,1)S(1)}, u32[]{:S(2)}, u32[]{:S(2)}) collective-permute-start(bf16[1056,128]{1,0:T(8,128)(2,1)S(1)} %get-tuple-element.29), channel_id=1, source_target_pairs={{0,32},{1,33},{2,34},{3,35},{4,36},{5,37},{6,38},{7,39},{8,40},{9,... | collective-permute-start | bytes 811016 | tf_op jit(solution)/shard_map/ppermute | solution.py:34
  108.3 0.8 collective-permute-start.15
  109.0 2.2 %collective-permute-start.18 = (bf16[1056,128]{1,0:T(8,128)(2,1)S(1)}, bf16[1056,128]{1,0:T(8,128)(2,1)S(1)}, u32[]{:S(2)}, u32[]{:S(2)}) collective-permute-start(bf16[1056,128]{1,0:T(8,128)(2,1)S(1)} %get-tuple-element.33), channel_id=1, source_target_pairs={{0,96},{1,97},{2,98},{3,99},{4,100},{5,101},{6,102},{7,103},{8,104... | collective-permute-start | bytes 811016 | tf_op jit(solution)/shard_map/ppermute | solution.py:34
  111.2 2.7 %collective-permute-start.19 = (bf16[1056,128]{1,0:T(8,128)(2,1)S(1)}, bf16[1056,128]{1,0:T(8,128)(2,1)S(1)}, u32[]{:S(2)}, u32[]{:S(2)}) collective-permute-start(bf16[1056,128]{1,0:T(8,128)(2,1)S(1)} %get-tuple-element.34), channel_id=1, source_target_pairs={{0,80},{1,81},{2,82},{3,83},{4,84},{5,85},{6,86},{7,87},{8,88},{9,... | collective-permute-start | bytes 811016 | tf_op jit(solution)/shard_map/ppermute | solution.py:34
  113.9 6.1 %sums_own.3 = (bf16[1056,128]{1,0:T(8,128)(2,1)S(1)}, bf16[1056,128]{1,0:T(8,128)(2,1)S(1)}, bf16[1056,128]{1,0:T(8,128)(2,1)S(1)}, bf16[1056,128]{1,0:T(8,128)(2,1)S(1)}) custom-call(s32[4]{0:T(128)S(1)} %pad_add_fusion.2.fb_ref, bf16[2,1024,512]{2,1,0:T(8,128)(2,1)S(1)} %copy-done.1, bf16[2,1024,512]{2,1,0:T(8,128)(2,1)S(1)} %copy-done.7, ...), custom_call_target="tpu_custom_call" | custom-call | flops 2147483648 | bytes 6291456 | tf_op jit(solution)/shard_map/sums_own/pallas_call | solution.py:236
  120.1 1.1 collective-permute-start.17
  121.2 4.0 %collective-permute-done.14.refs_0_ = bf16[1056,128]{1,0:T(8,128)(2,1)S(1)} collective-permute-done((bf16[1056,128]{1,0:T(8,128)(2,1)S(1)}, bf16[1056,128]{1,0:T(8,128)(2,1)S(1)}, u32[]{:S(2)}, u32[]{:S(2)}) %collective-permute-start.14) | collective-permute-done | bytes 270368 | tf_op jit(solution)/shard_map/ppermute | solution.py:34
  125.2 7.4 %collective-permute-done.15.refs_1_ = bf16[1056,128]{1,0:T(8,128)(2,1)S(1)} collective-permute-done((bf16[1056,128]{1,0:T(8,128)(2,1)S(1)}, bf16[1056,128]{1,0:T(8,128)(2,1)S(1)}, u32[]{:S(2)}, u32[]{:S(2)}) %collective-permute-start.15) | collective-permute-done | bytes 270368 | tf_op jit(solution)/shard_map/ppermute | solution.py:34
  132.6 1.6 %collective-permute-start.21 = (bf16[1056,128]{1,0:T(8,128)(2,1)S(1)}, bf16[1056,128]{1,0:T(8,128)(2,1)S(1)}, u32[]{:S(2)}, u32[]{:S(2)}) collective-permute-start(bf16[1056,128]{1,0:T(8,128)(2,1)S(1)} %get-tuple-element.36), channel_id=1, source_target_pairs={{0,64},{1,65},{2,66},{3,67},{4,68},{5,69},{6,70},{7,71},{8,72},{9,... | collective-permute-start | bytes 811016 | tf_op jit(solution)/shard_map/ppermute | solution.py:34
  134.3 7.4 %collective-permute-done.21.refs_7_ = bf16[1056,128]{1,0:T(8,128)(2,1)S(1)} collective-permute-done((bf16[1056,128]{1,0:T(8,128)(2,1)S(1)}, bf16[1056,128]{1,0:T(8,128)(2,1)S(1)}, u32[]{:S(2)}, u32[]{:S(2)}) %collective-permute-start.21) | collective-permute-done | bytes 270368 | tf_op jit(solution)/shard_map/ppermute | solution.py:34
  141.7 2.1 %finish.1 = f32[128,2048]{1,0:T(8,128)} custom-call(s32[2]{0:T(128)S(1)} %pad_add_fusion.idx_ref, bf16[1056,128]{1,0:T(8,128)(2,1)S(1)} %collective-permute-done.14.refs_0_, bf16[1056,128]{1,0:T(8,128)(2,1)S(1)} %collective-permute-done.15.refs_1_, bf16[1056,128]{1,0:T(8,128)(2,1)S(1)} %collective-permute-done.17.refs_2_, ...), custom_call_target="tpu_custom_call" | custom-call | tf_op jit(solution)/shard_map/finish/pallas_call | solution.py:280
  (65 shorter events, 1.5 us)
Async XLA Ops:
  0.0 3.3 %copy-start.12 = (bf16[128,1024]{1,0:T(8,128)(2,1)S(1)}, bf16[128,1024]{1,0:T(8,128)(2,1)}, u32[]{:S(2)}) copy-start(bf16[128,1024]{1,0:T(8,128)(2,1)} %param.2) | copy-start | bytes 786436
  1.8 14.7 %copy-start.9 = (bf16[1024,1024]{1,0:T(8,128)(2,1)}, bf16[1024,1024]{1,0:T(8,128)(2,1)S(1)}, u32[]{:S(2)}) copy-start(bf16[1024,1024]{1,0:T(8,128)(2,1)S(1)} %constant_dynamic-slice_fusion.a_ref.own_ref) | copy-start | bytes 6291460
  1.8 15.7 %collective-permute-start.3 = (bf16[1024,1024]{1,0:T(8,128)(2,1)S(1)}, bf16[1024,1024]{1,0:T(8,128)(2,1)}, u32[]{:S(2)}, u32[]{:S(2)}) collective-permute-start(bf16[1024,1024]{1,0:T(8,128)(2,1)S(1)} %constant_dynamic-slice_fusion.a_ref.own_ref), channel_id=1, source_target_pairs={{0,1},{1,0},{2,3},{3,2},{4,5},{5,4},{6,7},{7,6},{8,9},{9,8},{10,11... | collective-permute-start | bytes 6291464 | tf_op jit(solution)/shard_map/ppermute | solution.py:34
  3.3 6.7 %collective-permute-start = (bf16[128,1024]{1,0:T(8,128)(2,1)S(1)}, bf16[128,1024]{1,0:T(8,128)(2,1)S(1)}, u32[]{:S(2)}, u32[]{:S(2)}) collective-permute-start(bf16[128,1024]{1,0:T(8,128)(2,1)S(1)} %copy-done.12), channel_id=1, source_target_pairs={{0,2},{1,9},{2,4},{3,11},{4,6},{5,13},{6,0},{7,15},{8,10},{9,65},{... | collective-permute-start | bytes 786440 | tf_op jit(solution)/shard_map/ppermute | solution.py:34
  4.6 9.3 %collective-permute-start.1 = (bf16[128,1024]{1,0:T(8,128)(2,1)S(1)}, bf16[128,1024]{1,0:T(8,128)(2,1)S(1)}, u32[]{:S(2)}, u32[]{:S(2)}) collective-permute-start(bf16[128,1024]{1,0:T(8,128)(2,1)S(1)} %copy-done.12), channel_id=1, source_target_pairs={{0,4},{1,65},{2,6},{3,67},{4,0},{5,69},{6,2},{7,71},{8,12},{9,73},... | collective-permute-start | bytes 786440 | tf_op jit(solution)/shard_map/ppermute | solution.py:34
  7.1 6.9 %collective-permute-start.2 = (bf16[128,1024]{1,0:T(8,128)(2,1)S(1)}, bf16[128,1024]{1,0:T(8,128)(2,1)S(1)}, u32[]{:S(2)}, u32[]{:S(2)}) collective-permute-start(bf16[128,1024]{1,0:T(8,128)(2,1)S(1)} %copy-done.12), channel_id=1, source_target_pairs={{0,6},{1,73},{2,0},{3,75},{4,2},{5,77},{6,4},{7,79},{8,14},{9,1},{... | collective-permute-start | bytes 786440 | tf_op jit(solution)/shard_map/ppermute | solution.py:34
  14.0 25.5 %collective-permute-start.6 = (bf16[512,1024]{1,0:T(8,128)(2,1)S(1)}, bf16[512,1024]{1,0:T(8,128)(2,1)S(1)}, u32[]{:S(2)}, u32[]{:S(2)}) collective-permute-start(bf16[512,1024]{1,0:T(8,128)(2,1)S(1)} %constant_dynamic-update-slice_fusion.x_ref.refs_4_.refs_5_.refs_6_.refs_7_), channel_id=1, source_target_pairs={{0,72},{1,7},{2,74},{3,1},{4,76},{5,3},{6,78},{7,5},{8,0},{9,15},{... | collective-permute-start | bytes 3145736 | tf_op jit(solution)/shard_map/ppermute | solution.py:34
  16.5 29.5 %collective-permute-start.5 = (bf16[512,1024]{1,0:T(8,128)(2,1)S(1)}, bf16[512,1024]{1,0:T(8,128)(2,1)S(1)}, u32[]{:S(2)}, u32[]{:S(2)}) collective-permute-start(bf16[512,1024]{1,0:T(8,128)(2,1)S(1)} %constant_dynamic-update-slice_fusion.x_ref.refs_4_.refs_5_.refs_6_.refs_7_), channel_id=1, source_target_pairs={{0,64},{1,5},{2,66},{3,7},{4,68},{5,1},{6,70},{7,3},{8,72},{9,13},... | collective-permute-start | bytes 3145736 | tf_op jit(solution)/shard_map/ppermute | solution.py:34
  16.9 35.7 %collective-permute-start.4 = (bf16[512,1024]{1,0:T(8,128)(2,1)S(1)}, bf16[512,1024]{1,0:T(8,128)(2,1)}, u32[]{:S(2)}, u32[]{:S(2)}) collective-permute-start(bf16[512,1024]{1,0:T(8,128)(2,1)S(1)} %constant_dynamic-update-slice_fusion.x_ref.refs_4_.refs_5_.refs_6_.refs_7_), channel_id=1, source_target_pairs={{0,8},{1,3},{2,10},{3,5},{4,12},{5,7},{6,14},{7,1},{8,64},{9,11},{... | collective-permute-start | bytes 3145736 | tf_op jit(solution)/shard_map/ppermute | solution.py:34
  22.0 1.6 %copy-start.10 = (bf16[1024,1024]{1,0:T(8,128)(2,1)S(1)}, bf16[1024,1024]{1,0:T(8,128)(2,1)}, u32[]{:S(2)}) copy-start(bf16[1024,1024]{1,0:T(8,128)(2,1)} %copy-done.9) | copy-start | bytes 6291460
  23.6 1.2 copy-start.11
  30.0 1.3 copy-start
  44.7 1.3 copy-start.2
  51.2 1.4 copy-start.4
  57.9 1.4 copy-start.6
  59.5 4.2 %collective-permute-start.8 = (f32[2,4,4,128]{3,2,1,0:T(4,128)S(1)}, f32[2,4,4,128]{3,2,1,0:T(4,128)S(1)}, u32[]{:S(2)}, u32[]{:S(2)}) collective-permute-start(f32[2,4,4,128]{3,2,1,0:T(4,128)S(1)} %pad_maximum_fusion.1), channel_id=1, source_target_pairs={{0,4},{1,65},{2,6},{3,67},{4,0},{5,69},{6,2},{7,71},{8,12},{9,73},... | collective-permute-start | bytes 49160 | tf_op jit(solution)/shard_map/ppermute | solution.py:34
  62.2 2.6 %collective-permute-start.9 = (f32[2,4,4,128]{3,2,1,0:T(4,128)S(1)}, f32[2,4,4,128]{3,2,1,0:T(4,128)S(1)}, u32[]{:S(2)}, u32[]{:S(2)}) collective-permute-start(f32[2,4,4,128]{3,2,1,0:T(4,128)S(1)} %pad_maximum_fusion.1), channel_id=1, source_target_pairs={{0,6},{1,73},{2,0},{3,75},{4,2},{5,77},{6,4},{7,79},{8,14},{9,1},{... | collective-permute-start | bytes 49160 | tf_op jit(solution)/shard_map/ppermute | solution.py:34
  63.2 3.8 %collective-permute-start.7 = (f32[2,4,4,128]{3,2,1,0:T(4,128)S(1)}, f32[2,4,4,128]{3,2,1,0:T(4,128)S(1)}, u32[]{:S(2)}, u32[]{:S(2)}) collective-permute-start(f32[2,4,4,128]{3,2,1,0:T(4,128)S(1)} %pad_maximum_fusion.1), channel_id=1, source_target_pairs={{0,2},{1,9},{2,4},{3,11},{4,6},{5,13},{6,0},{7,15},{8,10},{9,65},{... | collective-permute-start | bytes 49160 | tf_op jit(solution)/shard_map/ppermute | solution.py:34
  67.1 4.2 %collective-permute-start.12 = (f32[2,4,4,128]{3,2,1,0:T(4,128)S(1)}, f32[2,4,4,128]{3,2,1,0:T(4,128)S(1)}, u32[]{:S(2)}, u32[]{:S(2)}) collective-permute-start(f32[2,4,4,128]{3,2,1,0:T(4,128)S(1)} %pad_maximum_fusion.2), channel_id=1, source_target_pairs={{0,72},{1,7},{2,74},{3,1},{4,76},{5,3},{6,78},{7,5},{8,0},{9,15},{... | collective-permute-start | bytes 49160 | tf_op jit(solution)/shard_map/ppermute | solution.py:34
  70.5 4.2 %collective-permute-start.11 = (f32[2,4,4,128]{3,2,1,0:T(4,128)S(1)}, f32[2,4,4,128]{3,2,1,0:T(4,128)S(1)}, u32[]{:S(2)}, u32[]{:S(2)}) collective-permute-start(f32[2,4,4,128]{3,2,1,0:T(4,128)S(1)} %pad_maximum_fusion.2), channel_id=1, source_target_pairs={{0,64},{1,5},{2,66},{3,7},{4,68},{5,1},{6,70},{7,3},{8,72},{9,13},... | collective-permute-start | bytes 49160 | tf_op jit(solution)/shard_map/ppermute | solution.py:34
  70.6 4.2 %collective-permute-start.10 = (f32[2,4,4,128]{3,2,1,0:T(4,128)S(1)}, f32[2,4,4,128]{3,2,1,0:T(4,128)S(1)}, u32[]{:S(2)}, u32[]{:S(2)}) collective-permute-start(f32[2,4,4,128]{3,2,1,0:T(4,128)S(1)} %pad_maximum_fusion.2), channel_id=1, source_target_pairs={{0,8},{1,3},{2,10},{3,5},{4,12},{5,7},{6,14},{7,1},{8,64},{9,11},{... | collective-permute-start | bytes 49160 | tf_op jit(solution)/shard_map/ppermute | solution.py:34
  75.0 1.6 %copy-start.1 = (bf16[2,1024,512]{2,1,0:T(8,128)(2,1)S(1)}, bf16[2,1024,512]{2,1,0:T(8,128)(2,1)}, u32[]{:S(2)}) copy-start(bf16[2,1024,512]{2,1,0:T(8,128)(2,1)} %copy-done) | copy-start | bytes 6291460
  76.6 1.6 %copy-start.3 = (bf16[2,1024,512]{2,1,0:T(8,128)(2,1)S(1)}, bf16[2,1024,512]{2,1,0:T(8,128)(2,1)}, u32[]{:S(2)}) copy-start(bf16[2,1024,512]{2,1,0:T(8,128)(2,1)} %copy-done.2) | copy-start | bytes 6291460
  78.2 1.6 %copy-start.5 = (bf16[2,1024,512]{2,1,0:T(8,128)(2,1)S(1)}, bf16[2,1024,512]{2,1,0:T(8,128)(2,1)}, u32[]{:S(2)}) copy-start(bf16[2,1024,512]{2,1,0:T(8,128)(2,1)} %copy-done.4) | copy-start | bytes 6291460
  79.8 1.6 %copy-start.7 = (bf16[2,1024,512]{2,1,0:T(8,128)(2,1)S(1)}, bf16[2,1024,512]{2,1,0:T(8,128)(2,1)}, u32[]{:S(2)}) copy-start(bf16[2,1024,512]{2,1,0:T(8,128)(2,1)} %copy-done.6) | copy-start | bytes 6291460
  87.2 11.4 %collective-permute-start.13 = (bf16[4,1056,128]{2,1,0:T(8,128)(2,1)S(1)}, bf16[4,1056,128]{2,1,0:T(8,128)(2,1)S(1)}, u32[]{:S(2)}, u32[]{:S(2)}) collective-permute-start(bf16[4,1056,128]{2,1,0:T(8,128)(2,1)S(1)} %sums_sib.2), channel_id=1, source_target_pairs={{0,1},{1,0},{2,3},{3,2},{4,5},{5,4},{6,7},{7,6},{8,9},{9,8},{10,11... | collective-permute-start | bytes 3244040 | tf_op jit(solution)/shard_map/ppermute | solution.py:34
  98.5 15.5 %collective-permute-start.16 = (bf16[4,1056,128]{2,1,0:T(8,128)(2,1)S(1)}, bf16[4,1056,128]{2,1,0:T(8,128)(2,1)S(1)}, u32[]{:S(2)}, u32[]{:S(2)}) collective-permute-start(bf16[4,1056,128]{2,1,0:T(8,128)(2,1)S(1)} %sums_sib.3), channel_id=1, source_target_pairs={{0,1},{1,0},{2,3},{3,2},{4,5},{5,4},{6,7},{7,6},{8,9},{9,8},{10,11... | collective-permute-start | bytes 3244040 | tf_op jit(solution)/shard_map/ppermute | solution.py:34
  104.6 20.6 %collective-permute-start.14 = (bf16[1056,128]{1,0:T(8,128)(2,1)S(1)}, bf16[1056,128]{1,0:T(8,128)(2,1)S(1)}, u32[]{:S(2)}, u32[]{:S(2)}) collective-permute-start(bf16[1056,128]{1,0:T(8,128)(2,1)S(1)} %get-tuple-element.29), channel_id=1, source_target_pairs={{0,32},{1,33},{2,34},{3,35},{4,36},{5,37},{6,38},{7,39},{8,40},{9,... | collective-permute-start | bytes 811016 | tf_op jit(solution)/shard_map/ppermute | solution.py:34
  108.3 24.3 %collective-permute-start.15 = (bf16[1056,128]{1,0:T(8,128)(2,1)S(1)}, bf16[1056,128]{1,0:T(8,128)(2,1)S(1)}, u32[]{:S(2)}, u32[]{:S(2)}) collective-permute-start(bf16[1056,128]{1,0:T(8,128)(2,1)S(1)} %get-tuple-element.30), channel_id=1, source_target_pairs={{0,16},{1,17},{2,18},{3,19},{4,20},{5,21},{6,22},{7,23},{8,24},{9,... | collective-permute-start | bytes 811016 | tf_op jit(solution)/shard_map/ppermute | solution.py:34
  109.0 25.2 %collective-permute-start.18 = (bf16[1056,128]{1,0:T(8,128)(2,1)S(1)}, bf16[1056,128]{1,0:T(8,128)(2,1)S(1)}, u32[]{:S(2)}, u32[]{:S(2)}) collective-permute-start(bf16[1056,128]{1,0:T(8,128)(2,1)S(1)} %get-tuple-element.33), channel_id=1, source_target_pairs={{0,96},{1,97},{2,98},{3,99},{4,100},{5,101},{6,102},{7,103},{8,104... | collective-permute-start | bytes 811016 | tf_op jit(solution)/shard_map/ppermute | solution.py:34
  111.2 23.0 %collective-permute-start.19 = (bf16[1056,128]{1,0:T(8,128)(2,1)S(1)}, bf16[1056,128]{1,0:T(8,128)(2,1)S(1)}, u32[]{:S(2)}, u32[]{:S(2)}) collective-permute-start(bf16[1056,128]{1,0:T(8,128)(2,1)S(1)} %get-tuple-element.34), channel_id=1, source_target_pairs={{0,80},{1,81},{2,82},{3,83},{4,84},{5,85},{6,86},{7,87},{8,88},{9,... | collective-permute-start | bytes 811016 | tf_op jit(solution)/shard_map/ppermute | solution.py:34
  113.9 27.7 %copy-start.8 = (bf16[2048,1024]{1,0:T(8,128)(2,1)S(1)}, bf16[2048,1024]{1,0:T(8,128)(2,1)}, u32[]{:S(2)}) copy-start(bf16[2048,1024]{1,0:T(8,128)(2,1)} %refs_8_.1) | copy-start | bytes 12582916
  120.1 14.2 %collective-permute-start.17 = (bf16[1056,128]{1,0:T(8,128)(2,1)S(1)}, bf16[1056,128]{1,0:T(8,128)(2,1)S(1)}, u32[]{:S(2)}, u32[]{:S(2)}) collective-permute-start(bf16[1056,128]{1,0:T(8,128)(2,1)S(1)} %get-tuple-element.31), channel_id=1, source_target_pairs={{0,48},{1,49},{2,50},{3,51},{4,52},{5,53},{6,54},{7,55},{8,56},{9,... | collective-permute-start | bytes 811016 | tf_op jit(solution)/shard_map/ppermute | solution.py:34
  125.2 9.1 %collective-permute-start.20 = (bf16[1056,128]{1,0:T(8,128)(2,1)S(1)}, bf16[1056,128]{1,0:T(8,128)(2,1)S(1)}, u32[]{:S(2)}, u32[]{:S(2)}) collective-permute-start(bf16[1056,128]{1,0:T(8,128)(2,1)S(1)} %get-tuple-element.35), channel_id=1, source_target_pairs={{0,112},{1,113},{2,114},{3,115},{4,116},{5,117},{6,118},{7,119},{8... | collective-permute-start | bytes 811016 | tf_op jit(solution)/shard_map/ppermute | solution.py:34
  132.6 9.1 %collective-permute-start.21 = (bf16[1056,128]{1,0:T(8,128)(2,1)S(1)}, bf16[1056,128]{1,0:T(8,128)(2,1)S(1)}, u32[]{:S(2)}, u32[]{:S(2)}) collective-permute-start(bf16[1056,128]{1,0:T(8,128)(2,1)S(1)} %get-tuple-element.36), channel_id=1, source_target_pairs={{0,64},{1,65},{2,66},{3,67},{4,68},{5,69},{6,70},{7,71},{8,72},{9,... | collective-permute-start | bytes 811016 | tf_op jit(solution)/shard_map/ppermute | solution.py:34

commit v2 on v0

v2 whole, which is shorter than its diff:
```python
import functools
import math

import jax
import jax.numpy as jnp
from jax import lax
from jax.experimental import pallas as pl
from jax.experimental.pallas import tpu as pltpu
from jax.sharding import PartitionSpec as P

BETA_GAIN = 4.0
PRIOR = 0.5
F32 = jnp.float32
BF16 = jnp.bfloat16

NX, NY, NZ = 4, 4, 4
AXES = ("dp", "cent")
COUNT_ROWS = 32
SHIFTS = (2, 1, 3, 0)
VMEM = pl.BlockSpec(memory_space=pltpu.VMEM)
SMEM = pl.BlockSpec(memory_space=pltpu.SMEM)


def _send(a, move):
    pairs = []
    for xh in range(2):
        for z in range(NZ):
            for xl in range(2):
                for y in range(NY):
                    for core in range(2):
                        src = (xh * 4 + z) * 16 + (xl * 4 + y) * 2 + core
                        x2, y2, z2, core2 = move(xh * 2 + xl, y, z, core)
                        x2, y2, z2 = x2 % NX, y2 % NY, z2 % NZ
                        dst = ((x2 // 2) * 4 + z2) * 16 + ((x2 % 2) * 4 + y2) * 2 + core2
                        pairs.append((src, dst))
    return lax.ppermute(a, AXES, pairs)


def send_first(a, d):
    return _send(a, lambda x, y, z, c: (x, y + d, z, c) if c == 0 else (x + d, y, z, c))


def send_second(a, d):
    return _send(a, lambda x, y, z, c: (x + d, y, z, c) if c == 0 else (x, y + d, z, c))


def send_core(a):
    return _send(a, lambda x, y, z, c: (x, y, z, 1 - c))


def send_z(a, d):
    return _send(a, lambda x, y, z, c: (x, y, z + d, c))


def send_far(a):
    return _send(a, lambda x, y, z, c: (x + 2, y, z, c))


def _params(mib):
    return pltpu.CompilerParams(vmem_limit_bytes=mib << 20)


def _norm_kernel(idx_ref, c_ref, o_ref):
    k = o_ref.shape[0]
    step = 128
    for j in range(k // step):
        v = c_ref[pl.ds(pl.multiple_of(idx_ref[0] * k + j * step, step), step), :].astype(F32)
        s = 0.5 * jnp.sum(v * v, axis=1, keepdims=True)
        o_ref[j * step : (j + 1) * step, :] = jnp.broadcast_to(s, (step, 128))


def half_norms(idx, cents):
    k, d = cents.shape
    return pl.pallas_call(
        _norm_kernel,
        out_shape=jax.ShapeDtypeStruct((k // 2, 128), F32),
        in_specs=[SMEM, VMEM],
        out_specs=VMEM,
        compiler_params=_params(8),
        cost_estimate=pl.CostEstimate(
            flops=k * d, bytes_accessed=k * d * 2, transcendentals=0
        ),
        name="half_norms",
    )(idx, cents)


def _score_kernel(gain, n_x, idx_ref, *refs):
    x_refs = refs[:n_x]
    c_refs, h_refs = refs[n_x : n_x + 2], refs[n_x + 2 : n_x + 4]
    w_ref, st_ref, xp_ref, u_ref, xt_ref = refs[-5:]
    k = h_refs[0].shape[0]
    r = w_ref.shape[2]
    kb = 256
    base = idx_ref[0] * k
    pos = 0
    for x_ref in x_refs:
        n = x_ref.shape[0]
        xt_ref[:, pos : pos + n] = x_ref[...].T
        pos += n

    def dots(b, j):
        rows = slice(j * kb, (j + 1) * kb)
        c = c_refs[b][pl.ds(pl.multiple_of(base + j * kb, kb), kb), :]
        u = jnp.dot(c, xt_ref[...], preferred_element_type=F32)
        u = u - jnp.tile(h_refs[b][rows, :], (1, r // 128))
        u_ref[b, rows, :] = u
        return jnp.max(u, axis=0, keepdims=True)

    def weights(b, j, m):
        rows = slice(j * kb, (j + 1) * kb)
        w = jnp.exp2((u_ref[b, rows, :] - m) * gain)
        w_ref[b, rows, :] = w.astype(BF16)
        return jnp.sum(w, axis=0, keepdims=True)

    def largest(ms):
        return functools.reduce(jnp.maximum, ms)

    nj = k // kb
    m0 = largest([dots(0, j) for j in range(nj)])
    ms, ss = [], []
    for j in range(nj):
        ms.append(dots(1, j))
        ss.append(weights(0, j, m0))
    m1 = largest(ms)
    st_ref[0:1, :] = m0
    st_ref[1:2, :] = sum(ss)
    for f in range(2 * NZ):
        off = pl.multiple_of(idx_ref[2 + f] * 128, 128)
        pos = 0
        for x_ref in x_refs:
            n = x_ref.shape[0]
            xp_ref[pos : pos + n, f * 128 : (f + 1) * 128] = x_ref[:, pl.ds(off, 128)]
            pos += n
    st_ref[2:3, :] = m1
    st_ref[3:4, :] = sum([weights(1, j, m1) for j in range(nj)])
    st_ref[4:8, :] = jnp.zeros((4, r), F32)


def score(idx, xs, cents, norms, gain, after):
    r, d = sum(x.shape[0] for x in xs), xs[0].shape[1]
    k = norms[0].shape[0]
    return pl.pallas_call(
        functools.partial(_score_kernel, gain, len(xs)),
        out_shape=(
            jax.ShapeDtypeStruct((2, k, r), BF16),
            jax.ShapeDtypeStruct((8, r), F32),
            jax.ShapeDtypeStruct((r, d), BF16),
        ),
        in_specs=[SMEM] + [VMEM] * (len(xs) + 4 + len(after)),
        out_specs=(VMEM, VMEM, VMEM),
        scratch_shapes=[pltpu.VMEM((2, k, r), F32), pltpu.VMEM((d, r), BF16)],
        compiler_params=_params(14),
        cost_estimate=pl.CostEstimate(
            flops=8 * r * k * d, bytes_accessed=2 * r * d, transcendentals=2 * r * k
        ),
        name="score",
    )(idx, *xs, *cents, *norms, *after)


def _sum_kernel(half, group, n_arr, has_add, *refs):
    w_refs, x_refs, sc_refs = refs[:n_arr], refs[n_arr : 2 * n_arr], refs[2 * n_arr]
    pos = 2 * n_arr + 1
    add_ref = refs[pos] if has_add else None
    outs = refs[pos + 1 if has_add else pos : -1]
    cnt_ref = refs[-1]
    k, r = w_refs[0].shape[1:]
    kb = 256
    per = kb // 128
    n_blk = NZ
    cols = slice(group * n_blk * 128, (group + 1) * n_blk * 128)

    def put(f, rows, v):
        if has_add:
            outs[f][rows, :] = v
        else:
            outs[0][f, rows, :] = v

    for j in range(k // kb):
        rows = slice(j * kb, (j + 1) * kb)
        acc, lanes = None, None
        for a in range(n_arr):
            sc = sc_refs[half : half + 1, a * r : (a + 1) * r]
            w = (w_refs[a][half, rows, :].astype(F32) * sc).astype(BF16)
            wf = w.astype(F32)
            for t in range(r // 128):
                part = wf[:, t * 128 : (t + 1) * 128]
                lanes = part if lanes is None else lanes + part
            d = jnp.dot(w, x_refs[a][:, cols], preferred_element_type=F32)
            acc = d if acc is None else acc + d
        col = jnp.sum(lanes.T, axis=0, keepdims=True)
        for t in range(per):
            cnt_ref[j * per + t : j * per + t + 1, :] = col[:, t * 128 : (t + 1) * 128]
        for f in range(n_blk):
            v = acc[:, f * 128 : (f + 1) * 128]
            if has_add:
                v = v + add_ref[f, rows, :].astype(F32)
            put(f, rows, v.astype(BF16))
    c = cnt_ref[...]
    if has_add:
        c = c + _unpack_counts(add_ref[0, k : k + COUNT_ROWS, :])
    packed = _pack_counts(c)
    for f in range(n_blk):
        put(f, slice(k, k + COUNT_ROWS), packed)


def _pack_counts(c):
    hi = c.astype(BF16).astype(F32)
    mid = (c - hi).astype(BF16).astype(F32)
    lo = (c - hi) - mid
    return jnp.concatenate([hi, mid, lo, jnp.zeros_like(lo)], axis=0).astype(BF16)


def _unpack_counts(rows):
    t = rows.astype(F32)
    return (t[0:8] + t[8:16]) + t[16:24]


def weighted_sums(half, group, ws, xs, scales, add=None):
    n_arr = len(ws)
    k, r = ws[0].shape[1:]
    rows = k + COUNT_ROWS
    operands = [*ws, *xs, scales]
    if add is None:
        out_shape = [jax.ShapeDtypeStruct((NZ, rows, 128), BF16)]
    else:
        operands.append(add)
        out_shape = [jax.ShapeDtypeStruct((rows, 128), BF16)] * NZ
    return pl.pallas_call(
        functools.partial(_sum_kernel, half, group, n_arr, add is not None),
        out_shape=out_shape,
        in_specs=[VMEM] * len(operands),
        out_specs=[VMEM] * len(out_shape),
        scratch_shapes=[pltpu.VMEM((8, 128), F32)],
        compiler_params=_params(14),
        cost_estimate=pl.CostEstimate(
            flops=4 * k * n_arr * r * NZ * 128, bytes_accessed=2 * rows * NZ * 128,
            transcendentals=0,
        ),
        name="sums_sib" if add is None else "sums_own",
    )(*operands)


def _total(parts):
    total = None
    for p in parts:
        v = p[...].astype(F32)
        total = v if total is None else total + v
    return total


def _add_kernel(*refs):
    o_ref = refs[-1]
    k = o_ref.shape[0] - COUNT_ROWS
    total = _total(refs[:-1])
    o_ref[:k, :] = total[:k].astype(BF16)
    o_ref[k:, :] = _pack_counts(_unpack_counts(total[k:]))


def add_blocks(parts):
    return pl.pallas_call(
        _add_kernel,
        out_shape=jax.ShapeDtypeStruct(parts[0].shape, BF16),
        in_specs=[VMEM] * len(parts),
        out_specs=VMEM,
        compiler_params=_params(8),
        cost_estimate=pl.CostEstimate(
            flops=0, bytes_accessed=10 * parts[0].size, transcendentals=0
        ),
        name="add_blocks",
    )(*parts)


def _final_kernel(n, idx_ref, *refs):
    parts = (refs[:n], refs[n : n + 1])
    c_ref, o_ref = refs[n + 1 :]
    k = c_ref.shape[0] // 2
    for j in range(2):
        side = idx_ref[0] if j == 0 else 1 - idx_ref[0]
        off = pl.multiple_of(side * k, k)
        total = _total(parts[j])
        c = _unpack_counts(total[k:])
        cnt = jnp.concatenate([c[q : q + 1, :] for q in range(k // 128)], axis=1)
        cols = pl.ds(pl.multiple_of(idx_ref[1] * 128, 128), 128)
        top = total[:k] + PRIOR * c_ref[pl.ds(off, k), cols].astype(F32)
        o_ref[:, pl.ds(off, k)] = top.T / (cnt + PRIOR)


def finish(idx, mine, other, centroids):
    return pl.pallas_call(
        functools.partial(_final_kernel, len(mine)),
        out_shape=jax.ShapeDtypeStruct((128, centroids.shape[0]), F32),
        in_specs=[SMEM] + [VMEM] * (len(mine) + 2),
        out_specs=VMEM,
        compiler_params=_params(12),
        name="finish",
    )(idx, *mine, other, centroids)


def _slots():
    place = {}
    for a in range(4):
        place[0, a] = (0, a * 128)
        place[2, a] = (3, a * 128)
        place[1, a] = (1 if a < 2 else 2, (a % 2) * 128)
        place[3, a] = (1 if a >= 2 else 2, 256 + (a % 2) * 128)
    return [place[b, a] for b in range(4) for a in range(4)]


def _gather_slots(refs, row):
    return jnp.concatenate(
        [refs[n][row : row + 1, off : off + 128] for n, off in _slots()], axis=0
    )


def _merge(pairs, gain):
    m = functools.reduce(jnp.maximum, [p[0] for p in pairs])
    s = sum(p[1] * jnp.exp2((p[0] - m) * gain) for p in pairs)
    return m, s


def _shifted(v, d, axis):
    if d == 0:
        return v
    if axis == 1:
        return jnp.concatenate([v[16 - 4 * d :], v[: 16 - 4 * d]], axis=0)
    parts = []
    for b in range(0, 16, 4):
        parts += [v[b + 4 - d : b + 4], v[b : b + 4 - d]]
    return jnp.concatenate(parts, axis=0)


def _pack_kernel(gain, *refs):
    o_ref = refs[-1]
    pairs = [(_gather_slots(refs, 2 * b), _gather_slots(refs, 2 * b + 1)) for b in range(2)]
    o_ref[0], o_ref[1] = _merge(pairs, gain)


def _merge_kernel(gain, axis, *refs):
    o_ref = refs[-1]
    pairs = [
        (_shifted(refs[d][0], d, axis), _shifted(refs[d][1], d, axis)) for d in range(4)
    ]
    o_ref[0], o_ref[1] = _merge(pairs, gain)


def _scale_kernel(gain, axis, *refs):
    stats, o_ref = refs[4:8], refs[-1]
    pairs = [
        (_shifted(refs[d][0], d, axis), _shifted(refs[d][1], d, axis)) for d in range(4)
    ]
    top, total = _merge(pairs, gain)
    r = stats[0].shape[1]
    for b in range(2):
        q = jnp.exp2((_gather_slots(stats, 2 * b) - top) * gain) / total
        for i, (n, off) in enumerate(_slots()):
            o_ref[b : b + 1, n * r + off : n * r + off + 128] = q[i : i + 1, :]


def _small(kernel, shape, args, name):
    return pl.pallas_call(
        kernel,
        out_shape=jax.ShapeDtypeStruct(shape, F32),
        in_specs=[VMEM] * len(args),
        out_specs=VMEM,
        compiler_params=_params(2),
        name=name,
    )(*args)


def local(points, centroids):
    features = points.shape[1]
    gain = BETA_GAIN * features ** (-0.5) * math.log2(math.e)
    dp = lax.axis_index("dp")
    xh, z = dp // NZ, dp % NZ
    blocks = [(1 - xh) * NZ + (z + d) % NZ for d in SHIFTS]
    blocks += [xh * NZ + (z + d) % NZ for d in SHIFTS]
    idx = jnp.stack([xh, dp] + blocks).astype(jnp.int32)

    shards = [points] + [send_first(points, d) for d in (1, 2, 3)]
    cents = (centroids, send_core(centroids))
    line = jnp.concatenate(shards, axis=0)
    half = line.shape[0] // 2
    line_a, line_b = line[:half], line[half:]
    up_a, down_b = send_second(line_a, 1), send_second(line_b, 3)
    norms = [half_norms(idx, c) for c in cents]
    line_a, line_b, norms[1] = lax.optimization_barrier((line_a, line_b, norms[1]))
    up_b, down_a = send_second(line_b, 1), send_second(line_a, 3)

    ws, stats, xs = [], [], []

    def run(*xin):
        w, st, xp = score(idx, xin, cents, norms, gain, stats[-1:])
        ws.append(w)
        stats.append(st)
        xs.append(xp)

    run(line)
    up_a, down_b, stats[0] = lax.optimization_barrier((up_a, down_b, stats[0]))
    far_a, far_b = send_second(up_a, 1), send_second(down_b, 3)
    run(up_a, down_b)
    run(up_b, down_a)
    run(far_a, far_b)

    shape = (2, 16, 128)
    pack = _small(functools.partial(_pack_kernel, gain), shape, stats, "stats_pack")
    every = [pack] + [send_first(pack, d) for d in (1, 2, 3)]
    pack = _small(functools.partial(_merge_kernel, gain, 0), shape, every, "stats_merge")
    every = [pack] + [send_second(pack, d) for d in (1, 2, 3)]
    scales = _small(
        functools.partial(_scale_kernel, gain, 1),
        (8, sum(st.shape[1] for st in stats)),
        every + stats,
        "stats_scale",
    )

    swapped = [send_core(weighted_sums(1, g, ws, xs, scales)[0]) for g in range(2)]
    got = []
    for g in range(2):
        sums = weighted_sums(0, g, ws, xs, scales, add=swapped[g])
        got.append([sums[3]] + [send_z(sums[n], d) for n, d in enumerate(SHIFTS[:3])])
    other = send_far(add_blocks(got[0]))
    return finish(idx, got[1], other, centroids)


def solution(mesh):
    return jax.shard_map(
        local,
        mesh=mesh,
        in_specs=(P(("dp", "cent"), None), P("cent", None)),
        out_specs=P("dp", "cent"),
        check_vma=False,
    )
```

time: 269 us -> 102 us (0.38)
  waiting for transfers between devices: 102 us -> 21.5 us
  blocking collectives: 77.8 us -> 0 us
  Pallas kernels: 0 us -> 39.2 us
  matrix products: 38.3 us -> 0 us
  starting transfers between devices: 0.04 us -> 37.5 us
  other arithmetic: 27.2 us -> 0.07 us
  between operations: 13.5 us -> 0.32 us
  local copies, waits for them, and re-layouts: 9.11 us -> 3.34 us
    unnamed x3 -> x0, waiting for transfers between devices: 62.7 us -> none
    psum x2 -> x0, blocking collectives: 50.6 us -> none  [the longest x1 29.8 us: local(): row_total = lax.psum(local_sum * jnp.exp(local_max - row_top), 'cent')]
    all_gather x1 -> x0, waiting for transfers between devices: 39.7 us -> none  [local(): gathered = lax.all_gather(points, 'cent', axis=0, tiled=True)]
    pallas_call x0 -> x15, Pallas kernels: none -> 39.2 us  [the longest x4 22.9 us: score(): pl.pallas_call(functools.partial(_score_kernel, gain, len(xs)), out_shape...]
    dot_general x5 -> x0, matrix products: 38.3 us -> none  [the longest x4 27.4 us: logits_of(): lax.dot_general(xblock, centroids, (((1,), (1,)), ((), ())), preferred_el...]
    ppermute x0 -> x25, starting transfers between devices: none -> 37.5 us  [_send(): return lax.ppermute(a, AXES, pairs)]
    pmax x1 -> x0, blocking collectives: 27.2 us -> none  [local(): row_top = lax.pmax(local_max, 'cent')]
    ppermute x0 -> x25, waiting for transfers between devices: none -> 21.5 us  [_send(): return lax.ppermute(a, AXES, pairs)]
  transfers between devices with their start and end apart: 2 -> 25, of which waited for: 2 -> 10; matrix products, arithmetic and copies ran while one was open for 1% -> 1% of each run, Pallas kernels for 0% -> 28%
where the time goes in v2:
time: 102 us
  Pallas kernels  39.2 us (38%)
  starting transfers between devices  37.5 us (37%)
  waiting for transfers between devices  21.5 us (21%)
  local copies, waits for them, and re-layouts  3.34 us (3%)
    ppermute x25, starting transfers between devices, _send(): return lax.ppermute(a, AXES, pairs)  37.5 us
    pallas_call x4, Pallas kernels, score(): pl.pallas_call(functools.partial(_score_kernel, gain, len(xs)), out_shape...  22.9 us
    ppermute x25, waiting for transfers between devices, _send(): return lax.ppermute(a, AXES, pairs)  21.5 us
    pallas_call x4, Pallas kernels, weighted_sums(): pl.pallas_call(functools.partial(_sum_kernel, half, group, n_arr, add is...  10.4 us
    pallas_call x2, Pallas kernels, half_norms(): pl.pallas_call(_norm_kernel, out_shape=jax.ShapeDtypeStruct((k // 2, 128)...  3.85 us
    unnamed x8, local copies, waits for them, and re-layouts  3.22 us
  transfers between devices with their start and end apart: 25, of which 10 were waited for; matrix products, arithmetic and copies ran while one was open for 1% of the time, Pallas kernels for 28%

profile of v2, /device:TPU:1, one launch (start us, length us, event | category | flops | bytes accessed | tf_op | source)
XLA Modules:
  0.0 101.9 jit_solution(2414458360543356240)
XLA Ops:
  0.0 1.4 %collective-permute-start.3 = (bf16[2048,1024]{1,0:T(8,128)(2,1)}, bf16[2048,1024]{1,0:T(8,128)(2,1)}, u32[]{:S(2)}, u32[]{:S(2)}) collective-permute-start(bf16[2048,1024]{1,0:T(8,128)(2,1)} %refs_5_.1), channel_id=1, source_target_pairs={{0,1},{1,0},{2,3},{3,2},{4,5},{5,4},{6,7},{7,6},{8,9},{9,8},{10,11... | collective-permute-start | bytes 12582920 | tf_op jit(solution)/shard_map/ppermute | solution.py:36
  1.4 1.3 %collective-permute-start = (bf16[128,1024]{1,0:T(8,128)(2,1)}, bf16[128,1024]{1,0:T(8,128)(2,1)S(1)}, u32[]{:S(2)}, u32[]{:S(2)}) collective-permute-start(bf16[128,1024]{1,0:T(8,128)(2,1)} %param.2), channel_id=1, source_target_pairs={{0,2},{1,9},{2,4},{3,11},{4,6},{5,13},{6,0},{7,15},{8,10},{9,65},{... | collective-permute-start | bytes 786440 | tf_op jit(solution)/shard_map/ppermute | solution.py:36
  2.7 2.5 %collective-permute-start.1 = (bf16[128,1024]{1,0:T(8,128)(2,1)}, bf16[128,1024]{1,0:T(8,128)(2,1)S(1)}, u32[]{:S(2)}, u32[]{:S(2)}) collective-permute-start(bf16[128,1024]{1,0:T(8,128)(2,1)} %param.2), channel_id=1, source_target_pairs={{0,4},{1,65},{2,6},{3,67},{4,0},{5,69},{6,2},{7,71},{8,12},{9,73},... | collective-permute-start | bytes 786440 | tf_op jit(solution)/shard_map/ppermute | solution.py:36
  5.2 1.2 %collective-permute-start.2 = (bf16[128,1024]{1,0:T(8,128)(2,1)}, bf16[128,1024]{1,0:T(8,128)(2,1)S(1)}, u32[]{:S(2)}, u32[]{:S(2)}) collective-permute-start(bf16[128,1024]{1,0:T(8,128)(2,1)} %param.2), channel_id=1, source_target_pairs={{0,6},{1,73},{2,0},{3,75},{4,2},{5,77},{6,4},{7,79},{8,14},{9,1},{... | collective-permute-start | bytes 786440 | tf_op jit(solution)/shard_map/ppermute | solution.py:36
  6.3 1.0 constant_dynamic-update-slice_fusion.1
  7.4 0.1 stack.43.idx_ref
  7.5 2.2 %copy-done = bf16[2048,1024]{1,0:T(8,128)(2,1)S(1)} copy-done((bf16[2048,1024]{1,0:T(8,128)(2,1)S(1)}, bf16[2048,1024]{1,0:T(8,128)(2,1)}, u32[]{:S(2)}) %copy-start) | copy-done | bytes 4194328
  9.7 1.0 %half_norms.2.refs_3_.refs_4_ = f32[1024,128]{1,0:T(8,128)S(1)} custom-call(s32[10]{0:T(128)S(1)} %stack.43.idx_ref, bf16[2048,1024]{1,0:T(8,128)(2,1)S(1)} %copy-done), custom_call_target="tpu_custom_call" | custom-call | flops 2097152 | bytes 4194304 | tf_op jit(solution)/shard_map/half_norms/pallas_call | solution.py:74
  10.7 1.4 %collective-permute-start.4 = (bf16[256,1024]{1,0:T(8,128)(2,1)S(1)}, bf16[256,1024]{1,0:T(8,128)(2,1)S(1)}, u32[]{:S(2)}, u32[]{:S(2)}) collective-permute-start(bf16[256,1024]{1,0:T(8,128)(2,1)S(1)} %constant_dynamic-update-slice_fusion), channel_id=1, source_target_pairs={{0,8},{1,3},{2,10},{3,5},{4,12},{5,7},{6,14},{7,1},{8,64},{9,11},{... | collective-permute-start | bytes 1572872 | tf_op jit(solution)/shard_map/ppermute | solution.py:36
  12.1 0.1 collective-permute-done.1
  12.3 2.5 %collective-permute-start.5 = (bf16[256,1024]{1,0:T(8,128)(2,1)S(1)}, bf16[256,1024]{1,0:T(8,128)(2,1)S(1)}, u32[]{:S(2)}, u32[]{:S(2)}) collective-permute-start(bf16[256,1024]{1,0:T(8,128)(2,1)S(1)} %constant_dynamic-update-slice_fusion.2), channel_id=1, source_target_pairs={{0,72},{1,7},{2,74},{3,1},{4,76},{5,3},{6,78},{7,5},{8,0},{9,15},{... | collective-permute-start | bytes 1572872 | tf_op jit(solution)/shard_map/ppermute | solution.py:36
  14.9 2.8 %half_norms.3.refs_4_.refs_5_ = f32[1024,128]{1,0:T(8,128)S(1)} custom-call(s32[10]{0:T(128)S(1)} %stack.43.idx_ref, bf16[2048,1024]{1,0:T(8,128)(2,1)} %collective-permute-done.3.c_ref.refs_2_.refs_3_), custom_call_target="tpu_custom_call" | custom-call | flops 2097152 | bytes 4194304 | tf_op jit(solution)/shard_map/half_norms/pallas_call | solution.py:74
  17.8 2.7 %collective-permute-start.7 = (bf16[256,1024]{1,0:T(8,128)(2,1)S(1)}, bf16[256,1024]{1,0:T(8,128)(2,1)S(1)}, u32[]{:S(2)}, u32[]{:S(2)}) collective-permute-start(bf16[256,1024]{1,0:T(8,128)(2,1)S(1)} %constant_dynamic-update-slice_fusion), channel_id=1, source_target_pairs={{0,72},{1,7},{2,74},{3,1},{4,76},{5,3},{6,78},{7,5},{8,0},{9,15},{... | collective-permute-start | bytes 1572872 | tf_op jit(solution)/shard_map/ppermute | solution.py:36
  20.5 5.7 %score.4 = (bf16[2,1024,512]{2,1,0:T(8,128)(2,1)S(1)}, f32[8,512]{1,0:T(8,128)S(1)}, bf16[512,1024]{1,0:T(8,128)(2,1)S(1)}) custom-call(s32[10]{0:T(128)S(1)} %stack.43.idx_ref, bf16[512,1024]{1,0:T(8,128)(2,1)S(1)} %pad_maximum_fusion.refs_0_, bf16[2048,1024]{1,0:T(8,128)(2,1)S(1)} %copy-done.1, ...), custom_call_target="tpu_custom_call" | custom-call | flops 4294967296 | bytes 1048576 | tf_op jit(solution)/shard_map/score/pallas_call | solution.py:142
  26.2 0.1 collective-permute-start.8
  26.3 2.7 %collective-permute-start.9 = (bf16[256,1024]{1,0:T(8,128)(2,1)S(1)}, bf16[256,1024]{1,0:T(8,128)(2,1)S(1)}, u32[]{:S(2)}, u32[]{:S(2)}) collective-permute-start(bf16[256,1024]{1,0:T(8,128)(2,1)S(1)} %collective-permute-done.5.refs_1_), channel_id=1, source_target_pairs={{0,72},{1,7},{2,74},{3,1},{4,76},{5,3},{6,78},{7,5},{8,0},{9,15},{... | collective-permute-start | bytes 1572872 | tf_op jit(solution)/shard_map/ppermute | solution.py:36
  29.0 5.7 %score.5 = (bf16[2,1024,512]{2,1,0:T(8,128)(2,1)S(1)}, f32[8,512]{1,0:T(8,128)S(1)}, bf16[512,1024]{1,0:T(8,128)(2,1)S(1)}) custom-call(s32[10]{0:T(128)S(1)} %stack.43.idx_ref, bf16[256,1024]{1,0:T(8,128)(2,1)S(1)} %collective-permute-done.4.refs_0_, bf16[256,1024]{1,0:T(8,128)(2,1)S(1)} %collective-permute-done.5.refs_1_, ...), custom_call_target="tpu_custom_call" | custom-call | flops 4294967296 | bytes 1048576 | tf_op jit(solution)/shard_map/score/pallas_call | solution.py:142
  34.7 5.7 %score.6 = (bf16[2,1024,512]{2,1,0:T(8,128)(2,1)S(1)}, f32[8,512]{1,0:T(8,128)S(1)}, bf16[512,1024]{1,0:T(8,128)(2,1)S(1)}) custom-call(s32[10]{0:T(128)S(1)} %stack.43.idx_ref, bf16[256,1024]{1,0:T(8,128)(2,1)S(1)} %collective-permute-done.6.refs_0_, bf16[256,1024]{1,0:T(8,128)(2,1)S(1)} %collective-permute-done.7.refs_1_, ...), custom_call_target="tpu_custom_call" | custom-call | flops 4294967296 | bytes 1048576 | tf_op jit(solution)/shard_map/score/pallas_call | solution.py:142
  40.5 5.7 %score.7 = (bf16[2,1024,512]{2,1,0:T(8,128)(2,1)S(1)}, f32[8,512]{1,0:T(8,128)S(1)}, bf16[512,1024]{1,0:T(8,128)(2,1)S(1)}) custom-call(s32[10]{0:T(128)S(1)} %stack.43.idx_ref, bf16[256,1024]{1,0:T(8,128)(2,1)S(1)} %collective-permute-done.8.refs_0_, bf16[256,1024]{1,0:T(8,128)(2,1)S(1)} %collective-permute-done.9.refs_1_, ...), custom_call_target="tpu_custom_call" | custom-call | flops 4294967296 | bytes 1048576 | tf_op jit(solution)/shard_map/score/pallas_call | solution.py:142
  46.2 2.3 %collective-permute-start.12 = (f32[2,16,128]{2,1,0:T(8,128)S(1)}, f32[2,16,128]{2,1,0:T(8,128)S(1)}, u32[]{:S(2)}, u32[]{:S(2)}) collective-permute-start(f32[2,16,128]{2,1,0:T(8,128)S(1)} %stats_pack.1.refs_0_), channel_id=1, source_target_pairs={{0,6},{1,73},{2,0},{3,75},{4,2},{5,77},{6,4},{7,79},{8,14},{9,1},{... | collective-permute-start | bytes 49160 | tf_op jit(solution)/shard_map/ppermute | solution.py:36
  48.5 0.8 collective-permute-start.11
  49.4 0.4 collective-permute-start.10
  49.8 2.8 %collective-permute-done.11.refs_2_ = f32[2,16,128]{2,1,0:T(8,128)S(1)} collective-permute-done((f32[2,16,128]{2,1,0:T(8,128)S(1)}, f32[2,16,128]{2,1,0:T(8,128)S(1)}, u32[]{:S(2)}, u32[]{:S(2)}) %collective-permute-start.11) | collective-permute-done | bytes 16416 | tf_op jit(solution)/shard_map/ppermute | solution.py:36
  52.6 0.6 collective-permute-done.10.refs_1_
  53.3 0.8 collective-permute-start.14
  54.1 0.6 collective-permute-start.13
  54.7 1.2 %collective-permute-done.15.refs_3_ = f32[2,16,128]{2,1,0:T(8,128)S(1)} collective-permute-done((f32[2,16,128]{2,1,0:T(8,128)S(1)}, f32[2,16,128]{2,1,0:T(8,128)S(1)}, u32[]{:S(2)}, u32[]{:S(2)}) %collective-permute-start.15) | collective-permute-done | bytes 16416 | tf_op jit(solution)/shard_map/ppermute | solution.py:36
  55.9 1.5 %collective-permute-done.14.refs_2_ = f32[2,16,128]{2,1,0:T(8,128)S(1)} collective-permute-done((f32[2,16,128]{2,1,0:T(8,128)S(1)}, f32[2,16,128]{2,1,0:T(8,128)S(1)}, u32[]{:S(2)}, u32[]{:S(2)}) %collective-permute-start.14) | collective-permute-done | bytes 16416 | tf_op jit(solution)/shard_map/ppermute | solution.py:36
  57.5 0.8 collective-permute-done.13.refs_1_
  58.3 2.6 %sums_sib.3 = bf16[4,1056,128]{2,1,0:T(8,128)(2,1)S(1)} custom-call(bf16[2,1024,512]{2,1,0:T(8,128)(2,1)S(1)} %get-tuple-element.32.refs_0_, bf16[2,1024,512]{2,1,0:T(8,128)(2,1)S(1)} %get-tuple-element.37.refs_1_, bf16[2,1024,512]{2,1,0:T(8,128)(2,1)S(1)} %get-tuple-element.41.refs_2_, bf16[2,1024,512]{2,1,0:T(8,128)(2,1)S(1)} %get-tuple-element.43.refs_3_, ...), custom_call_target="tpu_custom_call" | custom-call | flops 4294967296 | bytes 1081344 | tf_op jit(solution)/shard_map/sums_sib/pallas_call | solution.py:228
  60.9 5.8 %collective-permute-start.20 = (bf16[4,1056,128]{2,1,0:T(8,128)(2,1)S(1)}, bf16[4,1056,128]{2,1,0:T(8,128)(2,1)S(1)}, u32[]{:S(2)}, u32[]{:S(2)}) collective-permute-start(bf16[4,1056,128]{2,1,0:T(8,128)(2,1)S(1)} %sums_sib.3), channel_id=1, source_target_pairs={{0,1},{1,0},{2,3},{3,2},{4,5},{5,4},{6,7},{7,6},{8,9},{9,8},{10,11... | collective-permute-start | bytes 3244040 | tf_op jit(solution)/shard_map/ppermute | solution.py:36
  66.7 2.6 %sums_sib.2 = bf16[4,1056,128]{2,1,0:T(8,128)(2,1)S(1)} custom-call(bf16[2,1024,512]{2,1,0:T(8,128)(2,1)S(1)} %get-tuple-element.32.refs_0_, bf16[2,1024,512]{2,1,0:T(8,128)(2,1)S(1)} %get-tuple-element.37.refs_1_, bf16[2,1024,512]{2,1,0:T(8,128)(2,1)S(1)} %get-tuple-element.41.refs_2_, bf16[2,1024,512]{2,1,0:T(8,128)(2,1)S(1)} %get-tuple-element.43.refs_3_, ...), custom_call_target="tpu_custom_call" | custom-call | flops 4294967296 | bytes 1081344 | tf_op jit(solution)/shard_map/sums_sib/pallas_call | solution.py:228
  69.3 0.1 collective-permute-start.16
  69.4 2.6 %sums_own.3 = (bf16[1056,128]{1,0:T(8,128)(2,1)S(1)}, bf16[1056,128]{1,0:T(8,128)(2,1)S(1)}, bf16[1056,128]{1,0:T(8,128)(2,1)S(1)}, bf16[1056,128]{1,0:T(8,128)(2,1)S(1)}) custom-call(bf16[2,1024,512]{2,1,0:T(8,128)(2,1)S(1)} %get-tuple-element.32.refs_0_, bf16[2,1024,512]{2,1,0:T(8,128)(2,1)S(1)} %get-tuple-element.37.refs_1_, ...), custom_call_target="tpu_custom_call" | custom-call | flops 4294967296 | bytes 1081344 | tf_op jit(solution)/shard_map/sums_own/pallas_call | solution.py:228
  72.0 3.7 %collective-permute-start.21 = (bf16[1056,128]{1,0:T(8,128)(2,1)S(1)}, bf16[1056,128]{1,0:T(8,128)(2,1)S(1)}, u32[]{:S(2)}, u32[]{:S(2)}) collective-permute-start(bf16[1056,128]{1,0:T(8,128)(2,1)S(1)} %get-tuple-element.54), channel_id=1, source_target_pairs={{0,32},{1,33},{2,34},{3,35},{4,36},{5,37},{6,38},{7,39},{8,40},{9,... | collective-permute-start | bytes 811016 | tf_op jit(solution)/shard_map/ppermute | solution.py:36
  75.7 0.7 collective-permute-start.22
  76.4 1.9 %collective-permute-start.23 = (bf16[1056,128]{1,0:T(8,128)(2,1)S(1)}, bf16[1056,128]{1,0:T(8,128)(2,1)S(1)}, u32[]{:S(2)}, u32[]{:S(2)}) collective-permute-start(bf16[1056,128]{1,0:T(8,128)(2,1)S(1)} %get-tuple-element.56), channel_id=1, source_target_pairs={{0,48},{1,49},{2,50},{3,51},{4,52},{5,53},{6,54},{7,55},{8,56},{9,... | collective-permute-start | bytes 811016 | tf_op jit(solution)/shard_map/ppermute | solution.py:36
  78.4 2.6 %sums_own.2 = (bf16[1056,128]{1,0:T(8,128)(2,1)S(1)}, bf16[1056,128]{1,0:T(8,128)(2,1)S(1)}, bf16[1056,128]{1,0:T(8,128)(2,1)S(1)}, bf16[1056,128]{1,0:T(8,128)(2,1)S(1)}) custom-call(bf16[2,1024,512]{2,1,0:T(8,128)(2,1)S(1)} %get-tuple-element.32.refs_0_, bf16[2,1024,512]{2,1,0:T(8,128)(2,1)S(1)} %get-tuple-element.37.refs_1_, ...), custom_call_target="tpu_custom_call" | custom-call | flops 4294967296 | bytes 1081344 | tf_op jit(solution)/shard_map/sums_own/pallas_call | solution.py:228
  81.0 0.1 collective-permute-start.17
  81.1 0.6 collective-permute-start.18
  81.6 0.5 collective-permute-done.21.refs_1_
  82.1 2.8 %collective-permute-start.19 = (bf16[1056,128]{1,0:T(8,128)(2,1)S(1)}, bf16[1056,128]{1,0:T(8,128)(2,1)S(1)}, u32[]{:S(2)}, u32[]{:S(2)}) collective-permute-start(bf16[1056,128]{1,0:T(8,128)(2,1)S(1)} %get-tuple-element.52), channel_id=1, source_target_pairs={{0,48},{1,49},{2,50},{3,51},{4,52},{5,53},{6,54},{7,55},{8,56},{9,... | collective-permute-start | bytes 811016 | tf_op jit(solution)/shard_map/ppermute | solution.py:36
  85.0 3.9 %collective-permute-done.22.refs_2_ = bf16[1056,128]{1,0:T(8,128)(2,1)S(1)} collective-permute-done((bf16[1056,128]{1,0:T(8,128)(2,1)S(1)}, bf16[1056,128]{1,0:T(8,128)(2,1)S(1)}, u32[]{:S(2)}, u32[]{:S(2)}) %collective-permute-start.22) | collective-permute-done | bytes 270368 | tf_op jit(solution)/shard_map/ppermute | solution.py:36
  88.9 0.1 add_blocks.1
  89.0 1.0 collective-permute-start.24
  90.0 3.8 %collective-permute-done.17.refs_1_ = bf16[1056,128]{1,0:T(8,128)(2,1)S(1)} collective-permute-done((bf16[1056,128]{1,0:T(8,128)(2,1)S(1)}, bf16[1056,128]{1,0:T(8,128)(2,1)S(1)}, u32[]{:S(2)}, u32[]{:S(2)}) %collective-permute-start.17) | collective-permute-done | bytes 270368 | tf_op jit(solution)/shard_map/ppermute | solution.py:36
  93.8 6.2 %collective-permute-done.18.refs_2_ = bf16[1056,128]{1,0:T(8,128)(2,1)S(1)} collective-permute-done((bf16[1056,128]{1,0:T(8,128)(2,1)S(1)}, bf16[1056,128]{1,0:T(8,128)(2,1)S(1)}, u32[]{:S(2)}, u32[]{:S(2)}) %collective-permute-start.18) | collective-permute-done | bytes 270368 | tf_op jit(solution)/shard_map/ppermute | solution.py:36
  100.0 1.9 %finish.1 = f32[128,2048]{1,0:T(8,128)} custom-call(s32[10]{0:T(128)S(1)} %stack.43.idx_ref, bf16[1056,128]{1,0:T(8,128)(2,1)S(1)} %get-tuple-element.49.refs_0_, bf16[1056,128]{1,0:T(8,128)(2,1)S(1)} %collective-permute-done.17.refs_1_, bf16[1056,128]{1,0:T(8,128)(2,1)S(1)} %collective-permute-done.18.refs_2_, ...), custom_call_target="tpu_custom_call" | custom-call | tf_op jit(solution)/shard_map/finish/pallas_call | solution.py:289
  (29 shorter events, 0.4 us)
Async XLA Ops:
  0.0 14.9 %collective-permute-start.3 = (bf16[2048,1024]{1,0:T(8,128)(2,1)}, bf16[2048,1024]{1,0:T(8,128)(2,1)}, u32[]{:S(2)}, u32[]{:S(2)}) collective-permute-start(bf16[2048,1024]{1,0:T(8,128)(2,1)} %refs_5_.1), channel_id=1, source_target_pairs={{0,1},{1,0},{2,3},{3,2},{4,5},{5,4},{6,7},{7,6},{8,9},{9,8},{10,11... | collective-permute-start | bytes 12582920 | tf_op jit(solution)/shard_map/ppermute | solution.py:36
  1.4 9.3 %collective-permute-start = (bf16[128,1024]{1,0:T(8,128)(2,1)}, bf16[128,1024]{1,0:T(8,128)(2,1)S(1)}, u32[]{:S(2)}, u32[]{:S(2)}) collective-permute-start(bf16[128,1024]{1,0:T(8,128)(2,1)} %param.2), channel_id=1, source_target_pairs={{0,2},{1,9},{2,4},{3,11},{4,6},{5,13},{6,0},{7,15},{8,10},{9,65},{... | collective-permute-start | bytes 786440 | tf_op jit(solution)/shard_map/ppermute | solution.py:36
  2.7 9.5 %collective-permute-start.1 = (bf16[128,1024]{1,0:T(8,128)(2,1)}, bf16[128,1024]{1,0:T(8,128)(2,1)S(1)}, u32[]{:S(2)}, u32[]{:S(2)}) collective-permute-start(bf16[128,1024]{1,0:T(8,128)(2,1)} %param.2), channel_id=1, source_target_pairs={{0,4},{1,65},{2,6},{3,67},{4,0},{5,69},{6,2},{7,71},{8,12},{9,73},... | collective-permute-start | bytes 786440 | tf_op jit(solution)/shard_map/ppermute | solution.py:36
  5.2 7.1 %collective-permute-start.2 = (bf16[128,1024]{1,0:T(8,128)(2,1)}, bf16[128,1024]{1,0:T(8,128)(2,1)S(1)}, u32[]{:S(2)}, u32[]{:S(2)}) collective-permute-start(bf16[128,1024]{1,0:T(8,128)(2,1)} %param.2), channel_id=1, source_target_pairs={{0,6},{1,73},{2,0},{3,75},{4,2},{5,77},{6,4},{7,79},{8,14},{9,1},{... | collective-permute-start | bytes 786440 | tf_op jit(solution)/shard_map/ppermute | solution.py:36
  7.5 2.2 %copy-start = (bf16[2048,1024]{1,0:T(8,128)(2,1)S(1)}, bf16[2048,1024]{1,0:T(8,128)(2,1)}, u32[]{:S(2)}) copy-start(bf16[2048,1024]{1,0:T(8,128)(2,1)} %refs_5_.1) | copy-start | bytes 12582916
  9.7 5.1 %copy-start.2 = (bf16[128,1024]{1,0:T(8,128)(2,1)S(1)}, bf16[128,1024]{1,0:T(8,128)(2,1)}, u32[]{:S(2)}) copy-start(bf16[128,1024]{1,0:T(8,128)(2,1)} %param.2) | copy-start | bytes 786436
  10.7 15.5 %collective-permute-start.4 = (bf16[256,1024]{1,0:T(8,128)(2,1)S(1)}, bf16[256,1024]{1,0:T(8,128)(2,1)S(1)}, u32[]{:S(2)}, u32[]{:S(2)}) collective-permute-start(bf16[256,1024]{1,0:T(8,128)(2,1)S(1)} %constant_dynamic-update-slice_fusion), channel_id=1, source_target_pairs={{0,8},{1,3},{2,10},{3,5},{4,12},{5,7},{6,14},{7,1},{8,64},{9,11},{... | collective-permute-start | bytes 1572872 | tf_op jit(solution)/shard_map/ppermute | solution.py:36
  12.3 13.9 %collective-permute-start.5 = (bf16[256,1024]{1,0:T(8,128)(2,1)S(1)}, bf16[256,1024]{1,0:T(8,128)(2,1)S(1)}, u32[]{:S(2)}, u32[]{:S(2)}) collective-permute-start(bf16[256,1024]{1,0:T(8,128)(2,1)S(1)} %constant_dynamic-update-slice_fusion.2), channel_id=1, source_target_pairs={{0,72},{1,7},{2,74},{3,1},{4,76},{5,3},{6,78},{7,5},{8,0},{9,15},{... | collective-permute-start | bytes 1572872 | tf_op jit(solution)/shard_map/ppermute | solution.py:36
  14.9 5.6 %copy-start.1 = (bf16[2048,1024]{1,0:T(8,128)(2,1)S(1)}, bf16[2048,1024]{1,0:T(8,128)(2,1)}, u32[]{:S(2)}) copy-start(bf16[2048,1024]{1,0:T(8,128)(2,1)} %refs_5_.1) | copy-start | bytes 12582916
  17.7 17.0 %collective-permute-start.6 = (bf16[256,1024]{1,0:T(8,128)(2,1)S(1)}, bf16[256,1024]{1,0:T(8,128)(2,1)S(1)}, u32[]{:S(2)}, u32[]{:S(2)}) collective-permute-start(bf16[256,1024]{1,0:T(8,128)(2,1)S(1)} %constant_dynamic-update-slice_fusion.2), channel_id=1, source_target_pairs={{0,8},{1,3},{2,10},{3,5},{4,12},{5,7},{6,14},{7,1},{8,64},{9,11},{... | collective-permute-start | bytes 1572872 | tf_op jit(solution)/shard_map/ppermute | solution.py:36
  17.8 16.9 %collective-permute-start.7 = (bf16[256,1024]{1,0:T(8,128)(2,1)S(1)}, bf16[256,1024]{1,0:T(8,128)(2,1)S(1)}, u32[]{:S(2)}, u32[]{:S(2)}) collective-permute-start(bf16[256,1024]{1,0:T(8,128)(2,1)S(1)} %constant_dynamic-update-slice_fusion), channel_id=1, source_target_pairs={{0,72},{1,7},{2,74},{3,1},{4,76},{5,3},{6,78},{7,5},{8,0},{9,15},{... | collective-permute-start | bytes 1572872 | tf_op jit(solution)/shard_map/ppermute | solution.py:36
  26.2 14.2 %collective-permute-start.8 = (bf16[256,1024]{1,0:T(8,128)(2,1)S(1)}, bf16[256,1024]{1,0:T(8,128)(2,1)S(1)}, u32[]{:S(2)}, u32[]{:S(2)}) collective-permute-start(bf16[256,1024]{1,0:T(8,128)(2,1)S(1)} %collective-permute-done.4.refs_0_), channel_id=1, source_target_pairs={{0,8},{1,3},{2,10},{3,5},{4,12},{5,7},{6,14},{7,1},{8,64},{9,11},{... | collective-permute-start | bytes 1572872 | tf_op jit(solution)/shard_map/ppermute | solution.py:36
  26.3 14.1 %collective-permute-start.9 = (bf16[256,1024]{1,0:T(8,128)(2,1)S(1)}, bf16[256,1024]{1,0:T(8,128)(2,1)S(1)}, u32[]{:S(2)}, u32[]{:S(2)}) collective-permute-start(bf16[256,1024]{1,0:T(8,128)(2,1)S(1)} %collective-permute-done.5.refs_1_), channel_id=1, source_target_pairs={{0,72},{1,7},{2,74},{3,1},{4,76},{5,3},{6,78},{7,5},{8,0},{9,15},{... | collective-permute-start | bytes 1572872 | tf_op jit(solution)/shard_map/ppermute | solution.py:36
  46.2 3.6 %collective-permute-start.12 = (f32[2,16,128]{2,1,0:T(8,128)S(1)}, f32[2,16,128]{2,1,0:T(8,128)S(1)}, u32[]{:S(2)}, u32[]{:S(2)}) collective-permute-start(f32[2,16,128]{2,1,0:T(8,128)S(1)} %stats_pack.1.refs_0_), channel_id=1, source_target_pairs={{0,6},{1,73},{2,0},{3,75},{4,2},{5,77},{6,4},{7,79},{8,14},{9,1},{... | collective-permute-start | bytes 49160 | tf_op jit(solution)/shard_map/ppermute | solution.py:36
  48.5 4.1 %collective-permute-start.11 = (f32[2,16,128]{2,1,0:T(8,128)S(1)}, f32[2,16,128]{2,1,0:T(8,128)S(1)}, u32[]{:S(2)}, u32[]{:S(2)}) collective-permute-start(f32[2,16,128]{2,1,0:T(8,128)S(1)} %stats_pack.1.refs_0_), channel_id=1, source_target_pairs={{0,4},{1,65},{2,6},{3,67},{4,0},{5,69},{6,2},{7,71},{8,12},{9,73},... | collective-permute-start | bytes 49160 | tf_op jit(solution)/shard_map/ppermute | solution.py:36
  49.4 3.8 %collective-permute-start.10 = (f32[2,16,128]{2,1,0:T(8,128)S(1)}, f32[2,16,128]{2,1,0:T(8,128)S(1)}, u32[]{:S(2)}, u32[]{:S(2)}) collective-permute-start(f32[2,16,128]{2,1,0:T(8,128)S(1)} %stats_pack.1.refs_0_), channel_id=1, source_target_pairs={{0,2},{1,9},{2,4},{3,11},{4,6},{5,13},{6,0},{7,15},{8,10},{9,65},{... | collective-permute-start | bytes 49160 | tf_op jit(solution)/shard_map/ppermute | solution.py:36
  53.2 2.7 %collective-permute-start.15 = (f32[2,16,128]{2,1,0:T(8,128)S(1)}, f32[2,16,128]{2,1,0:T(8,128)S(1)}, u32[]{:S(2)}, u32[]{:S(2)}) collective-permute-start(f32[2,16,128]{2,1,0:T(8,128)S(1)} %stats_merge.1.refs_0_), channel_id=1, source_target_pairs={{0,72},{1,7},{2,74},{3,1},{4,76},{5,3},{6,78},{7,5},{8,0},{9,15},{... | collective-permute-start | bytes 49160 | tf_op jit(solution)/shard_map/ppermute | solution.py:36
  53.3 4.2 %collective-permute-start.14 = (f32[2,16,128]{2,1,0:T(8,128)S(1)}, f32[2,16,128]{2,1,0:T(8,128)S(1)}, u32[]{:S(2)}, u32[]{:S(2)}) collective-permute-start(f32[2,16,128]{2,1,0:T(8,128)S(1)} %stats_merge.1.refs_0_), channel_id=1, source_target_pairs={{0,64},{1,5},{2,66},{3,7},{4,68},{5,1},{6,70},{7,3},{8,72},{9,13},... | collective-permute-start | bytes 49160 | tf_op jit(solution)/shard_map/ppermute | solution.py:36
  54.1 4.1 %collective-permute-start.13 = (f32[2,16,128]{2,1,0:T(8,128)S(1)}, f32[2,16,128]{2,1,0:T(8,128)S(1)}, u32[]{:S(2)}, u32[]{:S(2)}) collective-permute-start(f32[2,16,128]{2,1,0:T(8,128)S(1)} %stats_merge.1.refs_0_), channel_id=1, source_target_pairs={{0,8},{1,3},{2,10},{3,5},{4,12},{5,7},{6,14},{7,1},{8,64},{9,11},{... | collective-permute-start | bytes 49160 | tf_op jit(solution)/shard_map/ppermute | solution.py:36
  60.9 8.5 %collective-permute-start.20 = (bf16[4,1056,128]{2,1,0:T(8,128)(2,1)S(1)}, bf16[4,1056,128]{2,1,0:T(8,128)(2,1)S(1)}, u32[]{:S(2)}, u32[]{:S(2)}) collective-permute-start(bf16[4,1056,128]{2,1,0:T(8,128)(2,1)S(1)} %sums_sib.3), channel_id=1, source_target_pairs={{0,1},{1,0},{2,3},{3,2},{4,5},{5,4},{6,7},{7,6},{8,9},{9,8},{10,11... | collective-permute-start | bytes 3244040 | tf_op jit(solution)/shard_map/ppermute | solution.py:36
  69.3 9.1 %collective-permute-start.16 = (bf16[4,1056,128]{2,1,0:T(8,128)(2,1)S(1)}, bf16[4,1056,128]{2,1,0:T(8,128)(2,1)S(1)}, u32[]{:S(2)}, u32[]{:S(2)}) collective-permute-start(bf16[4,1056,128]{2,1,0:T(8,128)(2,1)S(1)} %sums_sib.2), channel_id=1, source_target_pairs={{0,1},{1,0},{2,3},{3,2},{4,5},{5,4},{6,7},{7,6},{8,9},{9,8},{10,11... | collective-permute-start | bytes 3244040 | tf_op jit(solution)/shard_map/ppermute | solution.py:36
  72.0 10.1 %collective-permute-start.21 = (bf16[1056,128]{1,0:T(8,128)(2,1)S(1)}, bf16[1056,128]{1,0:T(8,128)(2,1)S(1)}, u32[]{:S(2)}, u32[]{:S(2)}) collective-permute-start(bf16[1056,128]{1,0:T(8,128)(2,1)S(1)} %get-tuple-element.54), channel_id=1, source_target_pairs={{0,32},{1,33},{2,34},{3,35},{4,36},{5,37},{6,38},{7,39},{8,40},{9,... | collective-permute-start | bytes 811016 | tf_op jit(solution)/shard_map/ppermute | solution.py:36
  75.7 13.2 %collective-permute-start.22 = (bf16[1056,128]{1,0:T(8,128)(2,1)S(1)}, bf16[1056,128]{1,0:T(8,128)(2,1)S(1)}, u32[]{:S(2)}, u32[]{:S(2)}) collective-permute-start(bf16[1056,128]{1,0:T(8,128)(2,1)S(1)} %get-tuple-element.55), channel_id=1, source_target_pairs={{0,16},{1,17},{2,18},{3,19},{4,20},{5,21},{6,22},{7,23},{8,24},{9,... | collective-permute-start | bytes 811016 | tf_op jit(solution)/shard_map/ppermute | solution.py:36
  76.4 12.5 %collective-permute-start.23 = (bf16[1056,128]{1,0:T(8,128)(2,1)S(1)}, bf16[1056,128]{1,0:T(8,128)(2,1)S(1)}, u32[]{:S(2)}, u32[]{:S(2)}) collective-permute-start(bf16[1056,128]{1,0:T(8,128)(2,1)S(1)} %get-tuple-element.56), channel_id=1, source_target_pairs={{0,48},{1,49},{2,50},{3,51},{4,52},{5,53},{6,54},{7,55},{8,56},{9,... | collective-permute-start | bytes 811016 | tf_op jit(solution)/shard_map/ppermute | solution.py:36
  81.0 12.8 %collective-permute-start.17 = (bf16[1056,128]{1,0:T(8,128)(2,1)S(1)}, bf16[1056,128]{1,0:T(8,128)(2,1)S(1)}, u32[]{:S(2)}, u32[]{:S(2)}) collective-permute-start(bf16[1056,128]{1,0:T(8,128)(2,1)S(1)} %get-tuple-element.50), channel_id=1, source_target_pairs={{0,32},{1,33},{2,34},{3,35},{4,36},{5,37},{6,38},{7,39},{8,40},{9,... | collective-permute-start | bytes 811016 | tf_op jit(solution)/shard_map/ppermute | solution.py:36
  81.1 18.9 %collective-permute-start.18 = (bf16[1056,128]{1,0:T(8,128)(2,1)S(1)}, bf16[1056,128]{1,0:T(8,128)(2,1)S(1)}, u32[]{:S(2)}, u32[]{:S(2)}) collective-permute-start(bf16[1056,128]{1,0:T(8,128)(2,1)S(1)} %get-tuple-element.51), channel_id=1, source_target_pairs={{0,16},{1,17},{2,18},{3,19},{4,20},{5,21},{6,22},{7,23},{8,24},{9,... | collective-permute-start | bytes 811016 | tf_op jit(solution)/shard_map/ppermute | solution.py:36
  82.1 17.9 %collective-permute-start.19 = (bf16[1056,128]{1,0:T(8,128)(2,1)S(1)}, bf16[1056,128]{1,0:T(8,128)(2,1)S(1)}, u32[]{:S(2)}, u32[]{:S(2)}) collective-permute-start(bf16[1056,128]{1,0:T(8,128)(2,1)S(1)} %get-tuple-element.52), channel_id=1, source_target_pairs={{0,48},{1,49},{2,50},{3,51},{4,52},{5,53},{6,54},{7,55},{8,56},{9,... | collective-permute-start | bytes 811016 | tf_op jit(solution)/shard_map/ppermute | solution.py:36
  89.0 11.0 %collective-permute-start.24 = (bf16[1056,128]{1,0:T(8,128)(2,1)S(1)}, bf16[1056,128]{1,0:T(8,128)(2,1)S(1)}, u32[]{:S(2)}, u32[]{:S(2)}) collective-permute-start(bf16[1056,128]{1,0:T(8,128)(2,1)S(1)} %add_blocks.1), channel_id=1, source_target_pairs={{0,64},{1,65},{2,66},{3,67},{4,68},{5,69},{6,70},{7,71},{8,72},{9,... | collective-permute-start | bytes 811016 | tf_op jit(solution)/shard_map/ppermute | solution.py:36

commit v3 on v2

--- a/solution.py
+++ b/solution.py
@@ -60,38 +60,77 @@
     return pltpu.CompilerParams(vmem_limit_bytes=mib << 20)
 
 
-def _norm_kernel(idx_ref, c_ref, o_ref):
-    k = o_ref.shape[0]
-    step = 128
-    for j in range(k // step):
-        v = c_ref[pl.ds(pl.multiple_of(idx_ref[0] * k + j * step, step), step), :].astype(F32)
+def _load_kernel(dp_ref, c_ref, half_ref, o_ref, sems):
+    k = half_ref.shape[0]
+    n = sems.shape[0]
+    step = k // n
+    base = (dp_ref[0] // NZ) * k
+    copies = []
+    for j in range(n):
+        src = c_ref.at[pl.ds(pl.multiple_of(base + j * step, step), step), :]
+        dst = half_ref.at[pl.ds(j * step, step), :]
+        copies.append(pltpu.make_async_copy(src, dst, sems.at[j]))
+        copies[-1].start()
+    for j in range(n):
+        copies[j].wait()
+        rows = slice(j * step, (j + 1) * step)
+        v = half_ref[rows, :].astype(F32)
         s = 0.5 * jnp.sum(v * v, axis=1, keepdims=True)
-        o_ref[j * step : (j + 1) * step, :] = jnp.broadcast_to(s, (step, 128))
-
-
-def half_norms(idx, cents):
-    k, d = cents.shape
-    return pl.pallas_call(
-        _norm_kernel,
-        out_shape=jax.ShapeDtypeStruct((k // 2, 128), F32),
-        in_specs=[SMEM, VMEM],
+        o_ref[rows, :] = jnp.broadcast_to(s, (step, 128))
+
+
+def load_half(dp, cents):
+    k, d = cents.shape[0] // 2, cents.shape[1]
+    return pl.pallas_call(
+        _load_kernel,
+        out_shape=(
+            jax.ShapeDtypeStruct((k, d), BF16),
+            jax.ShapeDtypeStruct((k, 128), F32),
+        ),
+        in_specs=[SMEM, pl.BlockSpec(memory_space=pltpu.HBM)],
+        out_specs=(VMEM, VMEM),
+        scratch_shapes=[pltpu.SemaphoreType.DMA((8,))],
+        compiler_params=_params(4),
+        cost_estimate=pl.CostEstimate(
+            flops=2 * k * d, bytes_accessed=k * d * 2, transcendentals=0
+        ),
+        name="load_half",
+    )(dp, cents)
+
+
+def _join_kernel(*refs):
+    pos = 0
+    for r in refs[:2]:
+        n = r.shape[0]
+        refs[-1][pos : pos + n, :] = r[...]
+        pos += n
+
+
+def join(a, b, *after):
+    parts = (a, b, *after)
+    rows, d = a.shape[0] + b.shape[0], a.shape[1]
+    return pl.pallas_call(
+        _join_kernel,
+        out_shape=jax.ShapeDtypeStruct((rows, d), parts[0].dtype),
+        in_specs=[VMEM] * len(parts),
         out_specs=VMEM,
-        compiler_params=_params(8),
-        cost_estimate=pl.CostEstimate(
-            flops=k * d, bytes_accessed=k * d * 2, transcendentals=0
-        ),
-        name="half_norms",
-    )(idx, cents)
-
-
-def _score_kernel(gain, n_x, idx_ref, *refs):
+        compiler_params=_params(2),
+        name="join",
+    )(*parts)
+
+
+def _block(dp, n):
+    xh = (dp // NZ + 1 - n // NZ) % 2
+    return xh * NZ + (dp + SHIFTS[n % NZ]) % NZ
+
+
+def _score_kernel(gain, n_x, dp_ref, *refs):
     x_refs = refs[:n_x]
     c_refs, h_refs = refs[n_x : n_x + 2], refs[n_x + 2 : n_x + 4]
     w_ref, st_ref, xp_ref, u_ref, xt_ref = refs[-5:]
     k = h_refs[0].shape[0]
     r = w_ref.shape[2]
     kb = 256
-    base = idx_ref[0] * k
     pos = 0
     for x_ref in x_refs:
         n = x_ref.shape[0]
@@ -100,8 +139,7 @@
 
     def dots(b, j):
         rows = slice(j * kb, (j + 1) * kb)
-        c = c_refs[b][pl.ds(pl.multiple_of(base + j * kb, kb), kb), :]
-        u = jnp.dot(c, xt_ref[...], preferred_element_type=F32)
+        u = jnp.dot(c_refs[b][rows, :], xt_ref[...], preferred_element_type=F32)
         u = u - jnp.tile(h_refs[b][rows, :], (1, r // 128))
         u_ref[b, rows, :] = u
         return jnp.max(u, axis=0, keepdims=True)
@@ -125,7 +163,7 @@
     st_ref[0:1, :] = m0
     st_ref[1:2, :] = sum(ss)
     for f in range(2 * NZ):
-        off = pl.multiple_of(idx_ref[2 + f] * 128, 128)
+        off = pl.multiple_of(_block(dp_ref[0], f) * 128, 128)
         pos = 0
         for x_ref in x_refs:
             n = x_ref.shape[0]
@@ -136,7 +174,7 @@
     st_ref[4:8, :] = jnp.zeros((4, r), F32)
 
 
-def score(idx, xs, cents, norms, gain, after):
+def score(dp, xs, cents, norms, gain, after):
     r, d = sum(x.shape[0] for x in xs), xs[0].shape[1]
     k = norms[0].shape[0]
     return pl.pallas_call(
@@ -154,7 +192,7 @@
             flops=8 * r * k * d, bytes_accessed=2 * r * d, transcendentals=2 * r * k
         ),
         name="score",
-    )(idx, *xs, *cents, *norms, *after)
+    )(dp, *xs, *cents, *norms, *after)
 
 
 def _sum_kernel(half, group, n_arr, has_add, *refs):
@@ -270,22 +308,22 @@
     )(*parts)
 
 
-def _final_kernel(n, idx_ref, *refs):
+def _final_kernel(n, dp_ref, *refs):
     parts = (refs[:n], refs[n : n + 1])
     c_ref, o_ref = refs[n + 1 :]
     k = c_ref.shape[0] // 2
     for j in range(2):
-        side = idx_ref[0] if j == 0 else 1 - idx_ref[0]
+        side = dp_ref[0] // NZ if j == 0 else 1 - dp_ref[0] // NZ
         off = pl.multiple_of(side * k, k)
         total = _total(parts[j])
         c = _unpack_counts(total[k:])
         cnt = jnp.concatenate([c[q : q + 1, :] for q in range(k // 128)], axis=1)
-        cols = pl.ds(pl.multiple_of(idx_ref[1] * 128, 128), 128)
+        cols = pl.ds(pl.multiple_of(dp_ref[0] * 128, 128), 128)
         top = total[:k] + PRIOR * c_ref[pl.ds(off, k), cols].astype(F32)
         o_ref[:, pl.ds(off, k)] = top.T / (cnt + PRIOR)
 
 
-def finish(idx, mine, other, centroids):
+def finish(dp, mine, other, centroids):
     return pl.pallas_call(
         functools.partial(_final_kernel, len(mine)),
         out_shape=jax.ShapeDtypeStruct((128, centroids.shape[0]), F32),
@@ -293,7 +331,7 @@
         out_specs=VMEM,
         compiler_params=_params(12),
         name="finish",
-    )(idx, *mine, other, centroids)
+    )(dp, *mine, other, centroids)
 
 
 def _slots():
@@ -370,31 +408,29 @@
 def local(points, centroids):
     features = points.shape[1]
     gain = BETA_GAIN * features ** (-0.5) * math.log2(math.e)
-    dp = lax.axis_index("dp")
-    xh, z = dp // NZ, dp % NZ
-    blocks = [(1 - xh) * NZ + (z + d) % NZ for d in SHIFTS]
-    blocks += [xh * NZ + (z + d) % NZ for d in SHIFTS]
-    idx = jnp.stack([xh, dp] + blocks).astype(jnp.int32)
+    dp = lax.axis_index("dp").astype(jnp.int32).reshape(1)
 
     shards = [points] + [send_first(points, d) for d in (1, 2, 3)]
-    cents = (centroids, send_core(centroids))
-    line = jnp.concatenate(shards, axis=0)
-    half = line.shape[0] // 2
-    line_a, line_b = line[:half], line[half:]
+    whole = (centroids, send_core(centroids))
+    own, own_norm = load_half(dp, whole[0])
+    line_a, line_b = join(shards[0], shards[1], own_norm), join(shards[2], shards[3], own_norm)
+    half = line_a.shape[0]
     up_a, down_b = send_second(line_a, 1), send_second(line_b, 3)
-    norms = [half_norms(idx, c) for c in cents]
-    line_a, line_b, norms[1] = lax.optimization_barrier((line_a, line_b, norms[1]))
-    up_b, down_a = send_second(line_b, 1), send_second(line_a, 3)
+    sib, sib_norm = load_half(dp, whole[1])
+    cents = (own, sib)
+    late_a, late_b, sib_norm = lax.optimization_barrier((line_a, line_b, sib_norm))
+    norms = (own_norm, sib_norm)
+    up_b, down_a = send_second(late_b, 1), send_second(late_a, 3)
 
     ws, stats, xs = [], [], []
 
     def run(*xin):
-        w, st, xp = score(idx, xin, cents, norms, gain, stats[-1:])
+        w, st, xp = score(dp, xin, cents, norms, gain, stats[-1:])
         ws.append(w)
         stats.append(st)
         xs.append(xp)
 
-    run(line)
+    run(line_a, line_b)
     up_a, down_b, stats[0] = lax.optimization_barrier((up_a, down_b, stats[0]))
     far_a, far_b = send_second(up_a, 1), send_second(down_b, 3)
     run(up_a, down_b)
@@ -419,7 +455,7 @@
         sums = weighted_sums(0, g, ws, xs, scales, add=swapped[g])
         got.append([sums[3]] + [send_z(sums[n], d) for n, d in enumerate(SHIFTS[:3])])
     other = send_far(add_blocks(got[0]))
-    return finish(idx, got[1], other, centroids)
+    return finish(dp, got[1], other, centroids)
 
 
 def solution(mesh):

time: 102 us -> 94.1 us (0.923)
  Pallas kernels: 39.2 us -> 29.7 us
  starting transfers between devices: 37.5 us -> 39.3 us
  local copies, waits for them, and re-layouts: 3.34 us -> 2.19 us
    pallas_call x4, Pallas kernels: 22.9 us -> 14.3 us  [score(): pl.pallas_call(functools.partial(_score_kernel, gain, len(xs)), out_shape...]
    ppermute x25, starting transfers between devices: 37.5 us -> 39.3 us  [_send(): return lax.ppermute(a, AXES, pairs)]
    unnamed x8 -> x6, local copies, waits for them, and re-layouts: 3.22 us -> 2.19 us
    pallas_call x2 -> x4, Pallas kernels: 3.85 us -> 3.41 us  [the longest x2 3.34 us: load_half(): pl.pallas_call(_load_kernel, out_shape=(jax.ShapeDtypeStruct((k, d), BF16...]
  transfers between devices with their start and end apart: 25 -> 25, of which waited for: 10 -> 9; matrix products, arithmetic and copies ran while one was open for 1% -> 0% of each run, Pallas kernels for 28% -> 23%
where the time goes in v3:
time: 94.1 us; the launch traced here: 93.9 us
  starting transfers between devices  39.3 us (42%)
  Pallas kernels  29.7 us (32%)
  waiting for transfers between devices  22.5 us (24%)
  local copies, waits for them, and re-layouts  2.19 us (2%)
    ppermute x25, starting transfers between devices, _send(): return lax.ppermute(a, AXES, pairs)  39.3 us
    ppermute x25, waiting for transfers between devices, _send(): return lax.ppermute(a, AXES, pairs)  22.5 us
    pallas_call x4, Pallas kernels, score(): pl.pallas_call(functools.partial(_score_kernel, gain, len(xs)), out_shape...  14.3 us
    pallas_call x4, Pallas kernels, weighted_sums(): pl.pallas_call(functools.partial(_sum_kernel, half, group, n_arr, add is...  10.4 us
    pallas_call x2, Pallas kernels, load_half(): pl.pallas_call(_load_kernel, out_shape=(jax.ShapeDtypeStruct((k, d), BF16...  3.34 us
    unnamed x6, local copies, waits for them, and re-layouts  2.19 us
  transfers between devices with their start and end apart: 25, of which 9 were waited for; matrix products, arithmetic and copies ran while one was open for 0% of the time, Pallas kernels for 23%

profile of v3, /device:TPU:1, one launch (start us, length us, event | category | flops | bytes accessed | tf_op | source)
XLA Modules:
  0.0 93.9 jit_solution(13954433468001385576)
XLA Ops:
  0.0 1.4 %collective-permute-start.3 = (bf16[2048,1024]{1,0:T(8,128)(2,1)}, bf16[2048,1024]{1,0:T(8,128)(2,1)}, u32[]{:S(2)}, u32[]{:S(2)}) collective-permute-start(bf16[2048,1024]{1,0:T(8,128)(2,1)} %refs_5_.1), channel_id=1, source_target_pairs={{0,1},{1,0},{2,3},{3,2},{4,5},{5,4},{6,7},{7,6},{8,9},{9,8},{10,11... | collective-permute-start | bytes 12582920 | tf_op jit(solution)/shard_map/ppermute | solution.py:36
  1.4 1.3 %collective-permute-start = (bf16[128,1024]{1,0:T(8,128)(2,1)}, bf16[128,1024]{1,0:T(8,128)(2,1)S(1)}, u32[]{:S(2)}, u32[]{:S(2)}) collective-permute-start(bf16[128,1024]{1,0:T(8,128)(2,1)} %refs_0_.1), channel_id=1, source_target_pairs={{0,2},{1,9},{2,4},{3,11},{4,6},{5,13},{6,0},{7,15},{8,10},{9,65},{... | collective-permute-start | bytes 786440 | tf_op jit(solution)/shard_map/ppermute | solution.py:36
  2.7 1.4 %collective-permute-start.2 = (bf16[128,1024]{1,0:T(8,128)(2,1)}, bf16[128,1024]{1,0:T(8,128)(2,1)S(1)}, u32[]{:S(2)}, u32[]{:S(2)}) collective-permute-start(bf16[128,1024]{1,0:T(8,128)(2,1)} %refs_0_.1), channel_id=1, source_target_pairs={{0,6},{1,73},{2,0},{3,75},{4,2},{5,77},{6,4},{7,79},{8,14},{9,1},{... | collective-permute-start | bytes 786440 | tf_op jit(solution)/shard_map/ppermute | solution.py:36
  4.1 1.6 %collective-permute-start.1 = (bf16[128,1024]{1,0:T(8,128)(2,1)}, bf16[128,1024]{1,0:T(8,128)(2,1)S(1)}, u32[]{:S(2)}, u32[]{:S(2)}) collective-permute-start(bf16[128,1024]{1,0:T(8,128)(2,1)} %refs_0_.1), channel_id=1, source_target_pairs={{0,4},{1,65},{2,6},{3,67},{4,0},{5,69},{6,2},{7,71},{8,12},{9,73},... | collective-permute-start | bytes 786440 | tf_op jit(solution)/shard_map/ppermute | solution.py:36
  5.7 2.2 %copy-done = bf16[2048,1024]{1,0:T(8,128)(2,1)S(1)} copy-done((bf16[2048,1024]{1,0:T(8,128)(2,1)S(1)}, bf16[2048,1024]{1,0:T(8,128)(2,1)}, u32[]{:S(2)}) %copy-start) | copy-done | bytes 4194328
  7.9 1.3 %load_half.2 = (bf16[1024,1024]{1,0:T(8,128)(2,1)S(1)}, f32[1024,128]{1,0:T(8,128)S(1)}) custom-call(s32[1]{0:T(128)} %bitcast.dp_ref, bf16[2048,1024]{1,0:T(8,128)(2,1)S(1)} %copy-done), custom_call_target="tpu_custom_call" | custom-call | flops 2097152 | bytes 2097152 | tf_op jit(solution)/shard_map/load_half/pallas_call | solution.py:84
  9.3 1.4 %collective-permute-start.4 = (bf16[256,1024]{1,0:T(8,128)(2,1)S(1)}, bf16[256,1024]{1,0:T(8,128)(2,1)S(1)}, u32[]{:S(2)}, u32[]{:S(2)}) collective-permute-start(bf16[256,1024]{1,0:T(8,128)(2,1)S(1)} %join.2.refs_0_), channel_id=1, source_target_pairs={{0,8},{1,3},{2,10},{3,5},{4,12},{5,7},{6,14},{7,1},{8,64},{9,11},{... | collective-permute-start | bytes 1572872 | tf_op jit(solution)/shard_map/ppermute | solution.py:36
  10.6 0.0 collective-permute-done.2.refs_1_
  10.6 1.6 %collective-permute-done.1.refs_0_ = bf16[128,1024]{1,0:T(8,128)(2,1)S(1)} collective-permute-done((bf16[128,1024]{1,0:T(8,128)(2,1)}, bf16[128,1024]{1,0:T(8,128)(2,1)S(1)}, u32[]{:S(2)}, u32[]{:S(2)}) %collective-permute-start.1) | collective-permute-done | bytes 262176 | tf_op jit(solution)/shard_map/ppermute | solution.py:36
  12.3 2.5 %collective-permute-start.5 = (bf16[256,1024]{1,0:T(8,128)(2,1)S(1)}, bf16[256,1024]{1,0:T(8,128)(2,1)S(1)}, u32[]{:S(2)}, u32[]{:S(2)}) collective-permute-start(bf16[256,1024]{1,0:T(8,128)(2,1)S(1)} %join.3.refs_1_), channel_id=1, source_target_pairs={{0,72},{1,7},{2,74},{3,1},{4,76},{5,3},{6,78},{7,5},{8,0},{9,15},{... | collective-permute-start | bytes 1572872 | tf_op jit(solution)/shard_map/ppermute | solution.py:36
  14.8 2.1 %load_half.3 = (bf16[1024,1024]{1,0:T(8,128)(2,1)S(1)}, f32[1024,128]{1,0:T(8,128)S(1)}) custom-call(s32[1]{0:T(128)} %bitcast.dp_ref, bf16[2048,1024]{1,0:T(8,128)(2,1)} %collective-permute-done.3.c_ref), custom_call_target="tpu_custom_call" | custom-call | flops 2097152 | bytes 2097152 | tf_op jit(solution)/shard_map/load_half/pallas_call | solution.py:84
  16.9 0.1 collective-permute-start.6
  16.9 2.7 %collective-permute-start.7 = (bf16[256,1024]{1,0:T(8,128)(2,1)S(1)}, bf16[256,1024]{1,0:T(8,128)(2,1)S(1)}, u32[]{:S(2)}, u32[]{:S(2)}) collective-permute-start(bf16[256,1024]{1,0:T(8,128)(2,1)S(1)} %join.2.refs_0_), channel_id=1, source_target_pairs={{0,72},{1,7},{2,74},{3,1},{4,76},{5,3},{6,78},{7,5},{8,0},{9,15},{... | collective-permute-start | bytes 1572872 | tf_op jit(solution)/shard_map/ppermute | solution.py:36
  19.6 3.6 %score.4 = (bf16[2,1024,512]{2,1,0:T(8,128)(2,1)S(1)}, f32[8,512]{1,0:T(8,128)S(1)}, bf16[512,1024]{1,0:T(8,128)(2,1)S(1)}) custom-call(s32[1]{0:T(128)} %bitcast.dp_ref, bf16[256,1024]{1,0:T(8,128)(2,1)S(1)} %join.2.refs_0_, bf16[256,1024]{1,0:T(8,128)(2,1)S(1)} %join.3.refs_1_, bf16[1024,1024]{1,0:T(8,128)(2,1)S(1)} %get-tuple-element.36.refs_2_, ...), custom_call_target="tpu_custom_call" | custom-call | flops 4294967296 | bytes 1048576 | tf_op jit(solution)/shard_map/score/pallas_call | solution.py:180
  23.2 0.0 collective-permute-done.5.refs_1_
  23.2 0.1 collective-permute-start.8
  23.3 2.7 %collective-permute-start.9 = (bf16[256,1024]{1,0:T(8,128)(2,1)S(1)}, bf16[256,1024]{1,0:T(8,128)(2,1)S(1)}, u32[]{:S(2)}, u32[]{:S(2)}) collective-permute-start(bf16[256,1024]{1,0:T(8,128)(2,1)S(1)} %collective-permute-done.5.refs_1_), channel_id=1, source_target_pairs={{0,72},{1,7},{2,74},{3,1},{4,76},{5,3},{6,78},{7,5},{8,0},{9,15},{... | collective-permute-start | bytes 1572872 | tf_op jit(solution)/shard_map/ppermute | solution.py:36
  25.9 3.6 %score.5 = (bf16[2,1024,512]{2,1,0:T(8,128)(2,1)S(1)}, f32[8,512]{1,0:T(8,128)S(1)}, bf16[512,1024]{1,0:T(8,128)(2,1)S(1)}) custom-call(s32[1]{0:T(128)} %bitcast.dp_ref, bf16[256,1024]{1,0:T(8,128)(2,1)S(1)} %collective-permute-done.4.refs_0_, bf16[256,1024]{1,0:T(8,128)(2,1)S(1)} %collective-permute-done.5.refs_1_, ...), custom_call_target="tpu_custom_call" | custom-call | flops 4294967296 | bytes 1048576 | tf_op jit(solution)/shard_map/score/pallas_call | solution.py:180
  29.5 0.0 collective-permute-done.6.refs_0_
  29.5 3.6 %score.6 = (bf16[2,1024,512]{2,1,0:T(8,128)(2,1)S(1)}, f32[8,512]{1,0:T(8,128)S(1)}, bf16[512,1024]{1,0:T(8,128)(2,1)S(1)}) custom-call(s32[1]{0:T(128)} %bitcast.dp_ref, bf16[256,1024]{1,0:T(8,128)(2,1)S(1)} %collective-permute-done.6.refs_0_, bf16[256,1024]{1,0:T(8,128)(2,1)S(1)} %collective-permute-done.7.refs_1_, ...), custom_call_target="tpu_custom_call" | custom-call | flops 4294967296 | bytes 1048576 | tf_op jit(solution)/shard_map/score/pallas_call | solution.py:180
  33.1 3.6 %score.7 = (bf16[2,1024,512]{2,1,0:T(8,128)(2,1)S(1)}, f32[8,512]{1,0:T(8,128)S(1)}, bf16[512,1024]{1,0:T(8,128)(2,1)S(1)}) custom-call(s32[1]{0:T(128)} %bitcast.dp_ref, bf16[256,1024]{1,0:T(8,128)(2,1)S(1)} %collective-permute-done.8.refs_0_, bf16[256,1024]{1,0:T(8,128)(2,1)S(1)} %collective-permute-done.9.refs_1_, ...), custom_call_target="tpu_custom_call" | custom-call | flops 4294967296 | bytes 1048576 | tf_op jit(solution)/shard_map/score/pallas_call | solution.py:180
  36.7 2.1 %collective-permute-start.12 = (f32[2,16,128]{2,1,0:T(8,128)S(1)}, f32[2,16,128]{2,1,0:T(8,128)S(1)}, u32[]{:S(2)}, u32[]{:S(2)}) collective-permute-start(f32[2,16,128]{2,1,0:T(8,128)S(1)} %stats_pack.1.refs_0_), channel_id=1, source_target_pairs={{0,6},{1,73},{2,0},{3,75},{4,2},{5,77},{6,4},{7,79},{8,14},{9,1},{... | collective-permute-start | bytes 49160 | tf_op jit(solution)/shard_map/ppermute | solution.py:36
  38.8 0.9 %collective-permute-start.11 = (f32[2,16,128]{2,1,0:T(8,128)S(1)}, f32[2,16,128]{2,1,0:T(8,128)S(1)}, u32[]{:S(2)}, u32[]{:S(2)}) collective-permute-start(f32[2,16,128]{2,1,0:T(8,128)S(1)} %stats_pack.1.refs_0_), channel_id=1, source_target_pairs={{0,4},{1,65},{2,6},{3,67},{4,0},{5,69},{6,2},{7,71},{8,12},{9,73},... | collective-permute-start | bytes 49160 | tf_op jit(solution)/shard_map/ppermute | solution.py:36
  39.8 3.1 %collective-permute-done.11.refs_2_ = f32[2,16,128]{2,1,0:T(8,128)S(1)} collective-permute-done((f32[2,16,128]{2,1,0:T(8,128)S(1)}, f32[2,16,128]{2,1,0:T(8,128)S(1)}, u32[]{:S(2)}, u32[]{:S(2)}) %collective-permute-start.11) | collective-permute-done | bytes 16416 | tf_op jit(solution)/shard_map/ppermute | solution.py:36
  42.9 0.6 collective-permute-done.10.refs_1_
  43.6 2.2 %collective-permute-start.15 = (f32[2,16,128]{2,1,0:T(8,128)S(1)}, f32[2,16,128]{2,1,0:T(8,128)S(1)}, u32[]{:S(2)}, u32[]{:S(2)}) collective-permute-start(f32[2,16,128]{2,1,0:T(8,128)S(1)} %stats_merge.1.refs_0_), channel_id=1, source_target_pairs={{0,72},{1,7},{2,74},{3,1},{4,76},{5,3},{6,78},{7,5},{8,0},{9,15},{... | collective-permute-start | bytes 49160 | tf_op jit(solution)/shard_map/ppermute | solution.py:36
  45.8 0.7 collective-permute-start.13
  46.4 0.2 collective-permute-done.15.refs_3_
  46.6 3.2 %collective-permute-done.14.refs_2_ = f32[2,16,128]{2,1,0:T(8,128)S(1)} collective-permute-done((f32[2,16,128]{2,1,0:T(8,128)S(1)}, f32[2,16,128]{2,1,0:T(8,128)S(1)}, u32[]{:S(2)}, u32[]{:S(2)}) %collective-permute-start.14) | collective-permute-done | bytes 16416 | tf_op jit(solution)/shard_map/ppermute | solution.py:36
  49.9 2.6 %sums_sib.3 = bf16[4,1056,128]{2,1,0:T(8,128)(2,1)S(1)} custom-call(bf16[2,1024,512]{2,1,0:T(8,128)(2,1)S(1)} %get-tuple-element.40.refs_0_, bf16[2,1024,512]{2,1,0:T(8,128)(2,1)S(1)} %get-tuple-element.45.refs_1_, bf16[2,1024,512]{2,1,0:T(8,128)(2,1)S(1)} %get-tuple-element.49.refs_2_, bf16[2,1024,512]{2,1,0:T(8,128)(2,1)S(1)} %get-tuple-element.51.refs_3_, ...), custom_call_target="tpu_custom_call" | custom-call | flops 4294967296 | bytes 1081344 | tf_op jit(solution)/shard_map/sums_sib/pallas_call | solution.py:266
  52.5 6.7 %collective-permute-start.20 = (bf16[4,1056,128]{2,1,0:T(8,128)(2,1)S(1)}, bf16[4,1056,128]{2,1,0:T(8,128)(2,1)S(1)}, u32[]{:S(2)}, u32[]{:S(2)}) collective-permute-start(bf16[4,1056,128]{2,1,0:T(8,128)(2,1)S(1)} %sums_sib.3), channel_id=1, source_target_pairs={{0,1},{1,0},{2,3},{3,2},{4,5},{5,4},{6,7},{7,6},{8,9},{9,8},{10,11... | collective-permute-start | bytes 3244040 | tf_op jit(solution)/shard_map/ppermute | solution.py:36
  59.2 2.6 %sums_sib.2 = bf16[4,1056,128]{2,1,0:T(8,128)(2,1)S(1)} custom-call(bf16[2,1024,512]{2,1,0:T(8,128)(2,1)S(1)} %get-tuple-element.40.refs_0_, bf16[2,1024,512]{2,1,0:T(8,128)(2,1)S(1)} %get-tuple-element.45.refs_1_, bf16[2,1024,512]{2,1,0:T(8,128)(2,1)S(1)} %get-tuple-element.49.refs_2_, bf16[2,1024,512]{2,1,0:T(8,128)(2,1)S(1)} %get-tuple-element.51.refs_3_, ...), custom_call_target="tpu_custom_call" | custom-call | flops 4294967296 | bytes 1081344 | tf_op jit(solution)/shard_map/sums_sib/pallas_call | solution.py:266
  61.8 0.1 collective-permute-start.16
  61.9 2.6 %sums_own.3 = (bf16[1056,128]{1,0:T(8,128)(2,1)S(1)}, bf16[1056,128]{1,0:T(8,128)(2,1)S(1)}, bf16[1056,128]{1,0:T(8,128)(2,1)S(1)}, bf16[1056,128]{1,0:T(8,128)(2,1)S(1)}) custom-call(bf16[2,1024,512]{2,1,0:T(8,128)(2,1)S(1)} %get-tuple-element.40.refs_0_, bf16[2,1024,512]{2,1,0:T(8,128)(2,1)S(1)} %get-tuple-element.45.refs_1_, ...), custom_call_target="tpu_custom_call" | custom-call | flops 4294967296 | bytes 1081344 | tf_op jit(solution)/shard_map/sums_own/pallas_call | solution.py:266
  64.5 3.7 %collective-permute-start.21 = (bf16[1056,128]{1,0:T(8,128)(2,1)S(1)}, bf16[1056,128]{1,0:T(8,128)(2,1)S(1)}, u32[]{:S(2)}, u32[]{:S(2)}) collective-permute-start(bf16[1056,128]{1,0:T(8,128)(2,1)S(1)} %get-tuple-element.62), channel_id=1, source_target_pairs={{0,32},{1,33},{2,34},{3,35},{4,36},{5,37},{6,38},{7,39},{8,40},{9,... | collective-permute-start | bytes 811016 | tf_op jit(solution)/shard_map/ppermute | solution.py:36
  68.2 0.7 collective-permute-start.22
  68.9 1.9 %collective-permute-start.23 = (bf16[1056,128]{1,0:T(8,128)(2,1)S(1)}, bf16[1056,128]{1,0:T(8,128)(2,1)S(1)}, u32[]{:S(2)}, u32[]{:S(2)}) collective-permute-start(bf16[1056,128]{1,0:T(8,128)(2,1)S(1)} %get-tuple-element.64), channel_id=1, source_target_pairs={{0,48},{1,49},{2,50},{3,51},{4,52},{5,53},{6,54},{7,55},{8,56},{9,... | collective-permute-start | bytes 811016 | tf_op jit(solution)/shard_map/ppermute | solution.py:36
  70.9 2.6 %sums_own.2 = (bf16[1056,128]{1,0:T(8,128)(2,1)S(1)}, bf16[1056,128]{1,0:T(8,128)(2,1)S(1)}, bf16[1056,128]{1,0:T(8,128)(2,1)S(1)}, bf16[1056,128]{1,0:T(8,128)(2,1)S(1)}) custom-call(bf16[2,1024,512]{2,1,0:T(8,128)(2,1)S(1)} %get-tuple-element.40.refs_0_, bf16[2,1024,512]{2,1,0:T(8,128)(2,1)S(1)} %get-tuple-element.45.refs_1_, ...), custom_call_target="tpu_custom_call" | custom-call | flops 4294967296 | bytes 1081344 | tf_op jit(solution)/shard_map/sums_own/pallas_call | solution.py:266
  73.5 0.1 collective-permute-start.17
  73.6 0.6 collective-permute-start.18
  74.2 0.5 collective-permute-done.21.refs_1_
  74.7 2.8 %collective-permute-start.19 = (bf16[1056,128]{1,0:T(8,128)(2,1)S(1)}, bf16[1056,128]{1,0:T(8,128)(2,1)S(1)}, u32[]{:S(2)}, u32[]{:S(2)}) collective-permute-start(bf16[1056,128]{1,0:T(8,128)(2,1)S(1)} %get-tuple-element.60), channel_id=1, source_target_pairs={{0,48},{1,49},{2,50},{3,51},{4,52},{5,53},{6,54},{7,55},{8,56},{9,... | collective-permute-start | bytes 811016 | tf_op jit(solution)/shard_map/ppermute | solution.py:36
  77.4 3.9 %collective-permute-done.22.refs_2_ = bf16[1056,128]{1,0:T(8,128)(2,1)S(1)} collective-permute-done((bf16[1056,128]{1,0:T(8,128)(2,1)S(1)}, bf16[1056,128]{1,0:T(8,128)(2,1)S(1)}, u32[]{:S(2)}, u32[]{:S(2)}) %collective-permute-start.22) | collective-permute-done | bytes 270368 | tf_op jit(solution)/shard_map/ppermute | solution.py:36
  81.4 0.1 add_blocks.1
  81.5 1.8 %collective-permute-start.24 = (bf16[1056,128]{1,0:T(8,128)(2,1)S(1)}, bf16[1056,128]{1,0:T(8,128)(2,1)S(1)}, u32[]{:S(2)}, u32[]{:S(2)}) collective-permute-start(bf16[1056,128]{1,0:T(8,128)(2,1)S(1)} %add_blocks.1), channel_id=1, source_target_pairs={{0,64},{1,65},{2,66},{3,67},{4,68},{5,69},{6,70},{7,71},{8,72},{9,... | collective-permute-start | bytes 811016 | tf_op jit(solution)/shard_map/ppermute | solution.py:36
  83.4 2.9 %collective-permute-done.17.refs_1_ = bf16[1056,128]{1,0:T(8,128)(2,1)S(1)} collective-permute-done((bf16[1056,128]{1,0:T(8,128)(2,1)S(1)}, bf16[1056,128]{1,0:T(8,128)(2,1)S(1)}, u32[]{:S(2)}, u32[]{:S(2)}) %collective-permute-start.17) | collective-permute-done | bytes 270368 | tf_op jit(solution)/shard_map/ppermute | solution.py:36
  86.3 6.2 %collective-permute-done.18.refs_2_ = bf16[1056,128]{1,0:T(8,128)(2,1)S(1)} collective-permute-done((bf16[1056,128]{1,0:T(8,128)(2,1)S(1)}, bf16[1056,128]{1,0:T(8,128)(2,1)S(1)}, u32[]{:S(2)}, u32[]{:S(2)}) %collective-permute-start.18) | collective-permute-done | bytes 270368 | tf_op jit(solution)/shard_map/ppermute | solution.py:36
  92.5 1.4 %finish.1 = f32[128,2048]{1,0:T(8,128)} custom-call(s32[1]{0:T(128)} %bitcast.dp_ref, bf16[1056,128]{1,0:T(8,128)(2,1)S(1)} %get-tuple-element.57.refs_0_, bf16[1056,128]{1,0:T(8,128)(2,1)S(1)} %collective-permute-done.17.refs_1_, bf16[1056,128]{1,0:T(8,128)(2,1)S(1)} %collective-permute-done.18.refs_2_, ...), custom_call_target="tpu_custom_call" | custom-call | tf_op jit(solution)/shard_map/finish/pallas_call | solution.py:327
  (25 shorter events, 0.2 us)
Async XLA Ops:
  0.0 14.8 %collective-permute-start.3 = (bf16[2048,1024]{1,0:T(8,128)(2,1)}, bf16[2048,1024]{1,0:T(8,128)(2,1)}, u32[]{:S(2)}, u32[]{:S(2)}) collective-permute-start(bf16[2048,1024]{1,0:T(8,128)(2,1)} %refs_5_.1), channel_id=1, source_target_pairs={{0,1},{1,0},{2,3},{3,2},{4,5},{5,4},{6,7},{7,6},{8,9},{9,8},{10,11... | collective-permute-start | bytes 12582920 | tf_op jit(solution)/shard_map/ppermute | solution.py:36
  1.4 7.8 %collective-permute-start = (bf16[128,1024]{1,0:T(8,128)(2,1)}, bf16[128,1024]{1,0:T(8,128)(2,1)S(1)}, u32[]{:S(2)}, u32[]{:S(2)}) collective-permute-start(bf16[128,1024]{1,0:T(8,128)(2,1)} %refs_0_.1), channel_id=1, source_target_pairs={{0,2},{1,9},{2,4},{3,11},{4,6},{5,13},{6,0},{7,15},{8,10},{9,65},{... | collective-permute-start | bytes 786440 | tf_op jit(solution)/shard_map/ppermute | solution.py:36
  2.7 7.9 %collective-permute-start.2 = (bf16[128,1024]{1,0:T(8,128)(2,1)}, bf16[128,1024]{1,0:T(8,128)(2,1)S(1)}, u32[]{:S(2)}, u32[]{:S(2)}) collective-permute-start(bf16[128,1024]{1,0:T(8,128)(2,1)} %refs_0_.1), channel_id=1, source_target_pairs={{0,6},{1,73},{2,0},{3,75},{4,2},{5,77},{6,4},{7,79},{8,14},{9,1},{... | collective-permute-start | bytes 786440 | tf_op jit(solution)/shard_map/ppermute | solution.py:36
  4.1 8.1 %collective-permute-start.1 = (bf16[128,1024]{1,0:T(8,128)(2,1)}, bf16[128,1024]{1,0:T(8,128)(2,1)S(1)}, u32[]{:S(2)}, u32[]{:S(2)}) collective-permute-start(bf16[128,1024]{1,0:T(8,128)(2,1)} %refs_0_.1), channel_id=1, source_target_pairs={{0,4},{1,65},{2,6},{3,67},{4,0},{5,69},{6,2},{7,71},{8,12},{9,73},... | collective-permute-start | bytes 786440 | tf_op jit(solution)/shard_map/ppermute | solution.py:36
  5.7 2.2 %copy-start = (bf16[2048,1024]{1,0:T(8,128)(2,1)S(1)}, bf16[2048,1024]{1,0:T(8,128)(2,1)}, u32[]{:S(2)}) copy-start(bf16[2048,1024]{1,0:T(8,128)(2,1)} %refs_5_.1) | copy-start | bytes 12582916
  7.9 1.3 %copy-start.2 = (bf16[128,1024]{1,0:T(8,128)(2,1)S(1)}, bf16[128,1024]{1,0:T(8,128)(2,1)}, u32[]{:S(2)}) copy-start(bf16[128,1024]{1,0:T(8,128)(2,1)} %refs_0_.1) | copy-start | bytes 786436
  9.3 13.9 %collective-permute-start.4 = (bf16[256,1024]{1,0:T(8,128)(2,1)S(1)}, bf16[256,1024]{1,0:T(8,128)(2,1)S(1)}, u32[]{:S(2)}, u32[]{:S(2)}) collective-permute-start(bf16[256,1024]{1,0:T(8,128)(2,1)S(1)} %join.2.refs_0_), channel_id=1, source_target_pairs={{0,8},{1,3},{2,10},{3,5},{4,12},{5,7},{6,14},{7,1},{8,64},{9,11},{... | collective-permute-start | bytes 1572872 | tf_op jit(solution)/shard_map/ppermute | solution.py:36
  12.3 10.9 %collective-permute-start.5 = (bf16[256,1024]{1,0:T(8,128)(2,1)S(1)}, bf16[256,1024]{1,0:T(8,128)(2,1)S(1)}, u32[]{:S(2)}, u32[]{:S(2)}) collective-permute-start(bf16[256,1024]{1,0:T(8,128)(2,1)S(1)} %join.3.refs_1_), channel_id=1, source_target_pairs={{0,72},{1,7},{2,74},{3,1},{4,76},{5,3},{6,78},{7,5},{8,0},{9,15},{... | collective-permute-start | bytes 1572872 | tf_op jit(solution)/shard_map/ppermute | solution.py:36
  16.9 12.7 %collective-permute-start.6 = (bf16[256,1024]{1,0:T(8,128)(2,1)S(1)}, bf16[256,1024]{1,0:T(8,128)(2,1)S(1)}, u32[]{:S(2)}, u32[]{:S(2)}) collective-permute-start(bf16[256,1024]{1,0:T(8,128)(2,1)S(1)} %join.3.refs_1_), channel_id=1, source_target_pairs={{0,8},{1,3},{2,10},{3,5},{4,12},{5,7},{6,14},{7,1},{8,64},{9,11},{... | collective-permute-start | bytes 1572872 | tf_op jit(solution)/shard_map/ppermute | solution.py:36
  16.9 12.6 %collective-permute-start.7 = (bf16[256,1024]{1,0:T(8,128)(2,1)S(1)}, bf16[256,1024]{1,0:T(8,128)(2,1)S(1)}, u32[]{:S(2)}, u32[]{:S(2)}) collective-permute-start(bf16[256,1024]{1,0:T(8,128)(2,1)S(1)} %join.2.refs_0_), channel_id=1, source_target_pairs={{0,72},{1,7},{2,74},{3,1},{4,76},{5,3},{6,78},{7,5},{8,0},{9,15},{... | collective-permute-start | bytes 1572872 | tf_op jit(solution)/shard_map/ppermute | solution.py:36
  23.2 9.9 %collective-permute-start.8 = (bf16[256,1024]{1,0:T(8,128)(2,1)S(1)}, bf16[256,1024]{1,0:T(8,128)(2,1)S(1)}, u32[]{:S(2)}, u32[]{:S(2)}) collective-permute-start(bf16[256,1024]{1,0:T(8,128)(2,1)S(1)} %collective-permute-done.4.refs_0_), channel_id=1, source_target_pairs={{0,8},{1,3},{2,10},{3,5},{4,12},{5,7},{6,14},{7,1},{8,64},{9,11},{... | collective-permute-start | bytes 1572872 | tf_op jit(solution)/shard_map/ppermute | solution.py:36
  23.3 9.8 %collective-permute-start.9 = (bf16[256,1024]{1,0:T(8,128)(2,1)S(1)}, bf16[256,1024]{1,0:T(8,128)(2,1)S(1)}, u32[]{:S(2)}, u32[]{:S(2)}) collective-permute-start(bf16[256,1024]{1,0:T(8,128)(2,1)S(1)} %collective-permute-done.5.refs_1_), channel_id=1, source_target_pairs={{0,72},{1,7},{2,74},{3,1},{4,76},{5,3},{6,78},{7,5},{8,0},{9,15},{... | collective-permute-start | bytes 1572872 | tf_op jit(solution)/shard_map/ppermute | solution.py:36
  36.7 3.0 %collective-permute-start.12 = (f32[2,16,128]{2,1,0:T(8,128)S(1)}, f32[2,16,128]{2,1,0:T(8,128)S(1)}, u32[]{:S(2)}, u32[]{:S(2)}) collective-permute-start(f32[2,16,128]{2,1,0:T(8,128)S(1)} %stats_pack.1.refs_0_), channel_id=1, source_target_pairs={{0,6},{1,73},{2,0},{3,75},{4,2},{5,77},{6,4},{7,79},{8,14},{9,1},{... | collective-permute-start | bytes 49160 | tf_op jit(solution)/shard_map/ppermute | solution.py:36
  38.8 4.1 %collective-permute-start.11 = (f32[2,16,128]{2,1,0:T(8,128)S(1)}, f32[2,16,128]{2,1,0:T(8,128)S(1)}, u32[]{:S(2)}, u32[]{:S(2)}) collective-permute-start(f32[2,16,128]{2,1,0:T(8,128)S(1)} %stats_pack.1.refs_0_), channel_id=1, source_target_pairs={{0,4},{1,65},{2,6},{3,67},{4,0},{5,69},{6,2},{7,71},{8,12},{9,73},... | collective-permute-start | bytes 49160 | tf_op jit(solution)/shard_map/ppermute | solution.py:36
  39.8 3.8 %collective-permute-start.10 = (f32[2,16,128]{2,1,0:T(8,128)S(1)}, f32[2,16,128]{2,1,0:T(8,128)S(1)}, u32[]{:S(2)}, u32[]{:S(2)}) collective-permute-start(f32[2,16,128]{2,1,0:T(8,128)S(1)} %stats_pack.1.refs_0_), channel_id=1, source_target_pairs={{0,2},{1,9},{2,4},{3,11},{4,6},{5,13},{6,0},{7,15},{8,10},{9,65},{... | collective-permute-start | bytes 49160 | tf_op jit(solution)/shard_map/ppermute | solution.py:36
  43.6 3.1 %collective-permute-start.15 = (f32[2,16,128]{2,1,0:T(8,128)S(1)}, f32[2,16,128]{2,1,0:T(8,128)S(1)}, u32[]{:S(2)}, u32[]{:S(2)}) collective-permute-start(f32[2,16,128]{2,1,0:T(8,128)S(1)} %stats_merge.1.refs_0_), channel_id=1, source_target_pairs={{0,72},{1,7},{2,74},{3,1},{4,76},{5,3},{6,78},{7,5},{8,0},{9,15},{... | collective-permute-start | bytes 49160 | tf_op jit(solution)/shard_map/ppermute | solution.py:36
  45.8 4.1 %collective-permute-start.14 = (f32[2,16,128]{2,1,0:T(8,128)S(1)}, f32[2,16,128]{2,1,0:T(8,128)S(1)}, u32[]{:S(2)}, u32[]{:S(2)}) collective-permute-start(f32[2,16,128]{2,1,0:T(8,128)S(1)} %stats_merge.1.refs_0_), channel_id=1, source_target_pairs={{0,64},{1,5},{2,66},{3,7},{4,68},{5,1},{6,70},{7,3},{8,72},{9,13},... | collective-permute-start | bytes 49160 | tf_op jit(solution)/shard_map/ppermute | solution.py:36
  45.8 4.1 %collective-permute-start.13 = (f32[2,16,128]{2,1,0:T(8,128)S(1)}, f32[2,16,128]{2,1,0:T(8,128)S(1)}, u32[]{:S(2)}, u32[]{:S(2)}) collective-permute-start(f32[2,16,128]{2,1,0:T(8,128)S(1)} %stats_merge.1.refs_0_), channel_id=1, source_target_pairs={{0,8},{1,3},{2,10},{3,5},{4,12},{5,7},{6,14},{7,1},{8,64},{9,11},{... | collective-permute-start | bytes 49160 | tf_op jit(solution)/shard_map/ppermute | solution.py:36
  52.5 9.4 %collective-permute-start.20 = (bf16[4,1056,128]{2,1,0:T(8,128)(2,1)S(1)}, bf16[4,1056,128]{2,1,0:T(8,128)(2,1)S(1)}, u32[]{:S(2)}, u32[]{:S(2)}) collective-permute-start(bf16[4,1056,128]{2,1,0:T(8,128)(2,1)S(1)} %sums_sib.3), channel_id=1, source_target_pairs={{0,1},{1,0},{2,3},{3,2},{4,5},{5,4},{6,7},{7,6},{8,9},{9,8},{10,11... | collective-permute-start | bytes 3244040 | tf_op jit(solution)/shard_map/ppermute | solution.py:36
  61.8 9.1 %collective-permute-start.16 = (bf16[4,1056,128]{2,1,0:T(8,128)(2,1)S(1)}, bf16[4,1056,128]{2,1,0:T(8,128)(2,1)S(1)}, u32[]{:S(2)}, u32[]{:S(2)}) collective-permute-start(bf16[4,1056,128]{2,1,0:T(8,128)(2,1)S(1)} %sums_sib.2), channel_id=1, source_target_pairs={{0,1},{1,0},{2,3},{3,2},{4,5},{5,4},{6,7},{7,6},{8,9},{9,8},{10,11... | collective-permute-start | bytes 3244040 | tf_op jit(solution)/shard_map/ppermute | solution.py:36
  64.5 10.1 %collective-permute-start.21 = (bf16[1056,128]{1,0:T(8,128)(2,1)S(1)}, bf16[1056,128]{1,0:T(8,128)(2,1)S(1)}, u32[]{:S(2)}, u32[]{:S(2)}) collective-permute-start(bf16[1056,128]{1,0:T(8,128)(2,1)S(1)} %get-tuple-element.62), channel_id=1, source_target_pairs={{0,32},{1,33},{2,34},{3,35},{4,36},{5,37},{6,38},{7,39},{8,40},{9,... | collective-permute-start | bytes 811016 | tf_op jit(solution)/shard_map/ppermute | solution.py:36
  68.2 13.2 %collective-permute-start.22 = (bf16[1056,128]{1,0:T(8,128)(2,1)S(1)}, bf16[1056,128]{1,0:T(8,128)(2,1)S(1)}, u32[]{:S(2)}, u32[]{:S(2)}) collective-permute-start(bf16[1056,128]{1,0:T(8,128)(2,1)S(1)} %get-tuple-element.63), channel_id=1, source_target_pairs={{0,16},{1,17},{2,18},{3,19},{4,20},{5,21},{6,22},{7,23},{8,24},{9,... | collective-permute-start | bytes 811016 | tf_op jit(solution)/shard_map/ppermute | solution.py:36
  68.9 12.5 %collective-permute-start.23 = (bf16[1056,128]{1,0:T(8,128)(2,1)S(1)}, bf16[1056,128]{1,0:T(8,128)(2,1)S(1)}, u32[]{:S(2)}, u32[]{:S(2)}) collective-permute-start(bf16[1056,128]{1,0:T(8,128)(2,1)S(1)} %get-tuple-element.64), channel_id=1, source_target_pairs={{0,48},{1,49},{2,50},{3,51},{4,52},{5,53},{6,54},{7,55},{8,56},{9,... | collective-permute-start | bytes 811016 | tf_op jit(solution)/shard_map/ppermute | solution.py:36
  70.9 21.7 %copy-start.1 = (bf16[2048,1024]{1,0:T(8,128)(2,1)S(1)}, bf16[2048,1024]{1,0:T(8,128)(2,1)}, u32[]{:S(2)}) copy-start(bf16[2048,1024]{1,0:T(8,128)(2,1)} %refs_5_.1) | copy-start | bytes 12582916
  73.5 12.8 %collective-permute-start.17 = (bf16[1056,128]{1,0:T(8,128)(2,1)S(1)}, bf16[1056,128]{1,0:T(8,128)(2,1)S(1)}, u32[]{:S(2)}, u32[]{:S(2)}) collective-permute-start(bf16[1056,128]{1,0:T(8,128)(2,1)S(1)} %get-tuple-element.58), channel_id=1, source_target_pairs={{0,32},{1,33},{2,34},{3,35},{4,36},{5,37},{6,38},{7,39},{8,40},{9,... | collective-permute-start | bytes 811016 | tf_op jit(solution)/shard_map/ppermute | solution.py:36
  73.6 18.9 %collective-permute-start.18 = (bf16[1056,128]{1,0:T(8,128)(2,1)S(1)}, bf16[1056,128]{1,0:T(8,128)(2,1)S(1)}, u32[]{:S(2)}, u32[]{:S(2)}) collective-permute-start(bf16[1056,128]{1,0:T(8,128)(2,1)S(1)} %get-tuple-element.59), channel_id=1, source_target_pairs={{0,16},{1,17},{2,18},{3,19},{4,20},{5,21},{6,22},{7,23},{8,24},{9,... | collective-permute-start | bytes 811016 | tf_op jit(solution)/shard_map/ppermute | solution.py:36
  74.7 17.9 %collective-permute-start.19 = (bf16[1056,128]{1,0:T(8,128)(2,1)S(1)}, bf16[1056,128]{1,0:T(8,128)(2,1)S(1)}, u32[]{:S(2)}, u32[]{:S(2)}) collective-permute-start(bf16[1056,128]{1,0:T(8,128)(2,1)S(1)} %get-tuple-element.60), channel_id=1, source_target_pairs={{0,48},{1,49},{2,50},{3,51},{4,52},{5,53},{6,54},{7,55},{8,56},{9,... | collective-permute-start | bytes 811016 | tf_op jit(solution)/shard_map/ppermute | solution.py:36
  81.5 11.0 %collective-permute-start.24 = (bf16[1056,128]{1,0:T(8,128)(2,1)S(1)}, bf16[1056,128]{1,0:T(8,128)(2,1)S(1)}, u32[]{:S(2)}, u32[]{:S(2)}) collective-permute-start(bf16[1056,128]{1,0:T(8,128)(2,1)S(1)} %add_blocks.1), channel_id=1, source_target_pairs={{0,64},{1,65},{2,66},{3,67},{4,68},{5,69},{6,70},{7,71},{8,72},{9,... | collective-permute-start | bytes 811016 | tf_op jit(solution)/shard_map/ppermute | solution.py:36

commit v4 on v3

--- a/solution.py
+++ b/solution.py
@@ -16,6 +16,8 @@
 NX, NY, NZ = 4, 4, 4
 AXES = ("dp", "cent")
 COUNT_ROWS = 32
+LIGHT = pl.CostEstimate(flops=1024, bytes_accessed=1024, transcendentals=0)
+COSTS = (pl.CostEstimate(flops=40 << 30, bytes_accessed=1024, transcendentals=0), LIGHT)
 SHIFTS = (2, 1, 3, 0)
 VMEM = pl.BlockSpec(memory_space=pltpu.VMEM)
 SMEM = pl.BlockSpec(memory_space=pltpu.SMEM)
@@ -79,7 +81,7 @@
         o_ref[rows, :] = jnp.broadcast_to(s, (step, 128))
 
 
-def load_half(dp, cents):
+def load_half(dp, cents, mib):
     k, d = cents.shape[0] // 2, cents.shape[1]
     return pl.pallas_call(
         _load_kernel,
@@ -90,10 +92,8 @@
         in_specs=[SMEM, pl.BlockSpec(memory_space=pltpu.HBM)],
         out_specs=(VMEM, VMEM),
         scratch_shapes=[pltpu.SemaphoreType.DMA((8,))],
-        compiler_params=_params(4),
-        cost_estimate=pl.CostEstimate(
-            flops=2 * k * d, bytes_accessed=k * d * 2, transcendentals=0
-        ),
+        compiler_params=_params(mib),
+        cost_estimate=LIGHT,
         name="load_half",
     )(dp, cents)
 
@@ -188,36 +188,24 @@
         out_specs=(VMEM, VMEM, VMEM),
         scratch_shapes=[pltpu.VMEM((2, k, r), F32), pltpu.VMEM((d, r), BF16)],
         compiler_params=_params(14),
-        cost_estimate=pl.CostEstimate(
-            flops=8 * r * k * d, bytes_accessed=2 * r * d, transcendentals=2 * r * k
-        ),
+        cost_estimate=LIGHT,
         name="score",
     )(dp, *xs, *cents, *norms, *after)
 
 
-def _sum_kernel(half, group, n_arr, has_add, *refs):
-    w_refs, x_refs, sc_refs = refs[:n_arr], refs[n_arr : 2 * n_arr], refs[2 * n_arr]
-    pos = 2 * n_arr + 1
-    add_ref = refs[pos] if has_add else None
-    outs = refs[pos + 1 if has_add else pos : -1]
-    cnt_ref = refs[-1]
+def _sum_kernel(half, group, n_arr, *refs):
+    w_refs, x_refs, sc_ref = refs[:n_arr], refs[n_arr : 2 * n_arr], refs[2 * n_arr]
+    packed = half == 1
+    out_ref, cnt_ref = refs[-2:]
     k, r = w_refs[0].shape[1:]
     kb = 256
     per = kb // 128
-    n_blk = NZ
-    cols = slice(group * n_blk * 128, (group + 1) * n_blk * 128)
-
-    def put(f, rows, v):
-        if has_add:
-            outs[f][rows, :] = v
-        else:
-            outs[0][f, rows, :] = v
-
+    cols = slice(group * NZ * 128, (group + 1) * NZ * 128)
     for j in range(k // kb):
         rows = slice(j * kb, (j + 1) * kb)
         acc, lanes = None, None
         for a in range(n_arr):
-            sc = sc_refs[half : half + 1, a * r : (a + 1) * r]
+            sc = sc_ref[half : half + 1, a * r : (a + 1) * r]
             w = (w_refs[a][half, rows, :].astype(F32) * sc).astype(BF16)
             wf = w.astype(F32)
             for t in range(r // 128):
@@ -228,17 +216,11 @@
         col = jnp.sum(lanes.T, axis=0, keepdims=True)
         for t in range(per):
             cnt_ref[j * per + t : j * per + t + 1, :] = col[:, t * 128 : (t + 1) * 128]
-        for f in range(n_blk):
-            v = acc[:, f * 128 : (f + 1) * 128]
-            if has_add:
-                v = v + add_ref[f, rows, :].astype(F32)
-            put(f, rows, v.astype(BF16))
-    c = cnt_ref[...]
-    if has_add:
-        c = c + _unpack_counts(add_ref[0, k : k + COUNT_ROWS, :])
-    packed = _pack_counts(c)
-    for f in range(n_blk):
-        put(f, slice(k, k + COUNT_ROWS), packed)
+        for f in range(NZ):
+            out_ref[f, rows, :] = acc[:, f * 128 : (f + 1) * 128].astype(out_ref.dtype)
+    if packed:
+        for f in range(NZ):
+            out_ref[f, k:, :] = _pack_counts(cnt_ref[...])
 
 
 def _pack_counts(c):
@@ -253,85 +235,104 @@
     return (t[0:8] + t[8:16]) + t[16:24]
 
 
-def weighted_sums(half, group, ws, xs, scales, add=None):
+COUNTS = jax.ShapeDtypeStruct((8, 128), F32)
+
+
+def weighted_sums(half, group, ws, xs, scales, after=()):
     n_arr = len(ws)
     k, r = ws[0].shape[1:]
-    rows = k + COUNT_ROWS
-    operands = [*ws, *xs, scales]
-    if add is None:
-        out_shape = [jax.ShapeDtypeStruct((NZ, rows, 128), BF16)]
+    operands = [*ws, *xs, scales, *after]
+    if half == 1:
+        out_shape = jax.ShapeDtypeStruct((NZ, k + COUNT_ROWS, 128), BF16)
+        out_specs, scratch = VMEM, [pltpu.VMEM((8, 128), F32)]
     else:
-        operands.append(add)
-        out_shape = [jax.ShapeDtypeStruct((rows, 128), BF16)] * NZ
-    return pl.pallas_call(
-        functools.partial(_sum_kernel, half, group, n_arr, add is not None),
+        out_shape = (jax.ShapeDtypeStruct((NZ, k, 128), F32), COUNTS)
+        out_specs, scratch = (VMEM, VMEM), []
+    return pl.pallas_call(
+        functools.partial(_sum_kernel, half, group, n_arr),
         out_shape=out_shape,
         in_specs=[VMEM] * len(operands),
-        out_specs=[VMEM] * len(out_shape),
-        scratch_shapes=[pltpu.VMEM((8, 128), F32)],
+        out_specs=out_specs,
+        scratch_shapes=scratch,
         compiler_params=_params(14),
-        cost_estimate=pl.CostEstimate(
-            flops=4 * k * n_arr * r * NZ * 128, bytes_accessed=2 * rows * NZ * 128,
-            transcendentals=0,
-        ),
-        name="sums_sib" if add is None else "sums_own",
+        cost_estimate=COSTS[half],
+        name="sums_sib" if half else "sums_own",
     )(*operands)
 
 
-def _total(parts):
-    total = None
-    for p in parts:
-        v = p[...].astype(F32)
-        total = v if total is None else total + v
-    return total
-
-
-def _add_kernel(*refs):
+def _call(kernel, out_shape, args, name, mib=8):
+    many = isinstance(out_shape, tuple)
+    return pl.pallas_call(
+        kernel,
+        out_shape=out_shape,
+        in_specs=[VMEM] * len(args),
+        out_specs=(VMEM,) * len(out_shape) if many else VMEM,
+        compiler_params=_params(mib),
+        cost_estimate=LIGHT,
+        name=name,
+    )(*args)
+
+
+def _mix_kernel(acc_ref, cnt_ref, add_ref, *refs):
+    keep_ref, sum_ref = refs[-2:]
+    outs = refs[-2 - (NZ - 1) : -2]
+    k = acc_ref.shape[1]
+    c = cnt_ref[...] + _unpack_counts(add_ref[0, k:, :])
+    sum_ref[...] = c
+    packed = _pack_counts(c)
+    for f in range(NZ - 1):
+        outs[f][:k, :] = (acc_ref[f] + add_ref[f, :k, :].astype(F32)).astype(BF16)
+        outs[f][k:, :] = packed
+    keep_ref[...] = acc_ref[NZ - 1] + add_ref[NZ - 1, :k, :].astype(F32)
+
+
+def mix(acc, cnt, add):
+    k = acc.shape[1]
+    out = (jax.ShapeDtypeStruct((k + COUNT_ROWS, 128), BF16),) * (NZ - 1)
+    out += (jax.ShapeDtypeStruct((k, 128), F32), COUNTS)
+    return _call(_mix_kernel, out, [acc, cnt, add], "mix")
+
+
+def _totals(keep_ref, cnt_ref, refs):
+    k = keep_ref.shape[0]
+    total, c = keep_ref[...], cnt_ref[...]
+    for r in refs:
+        total = total + r[:k, :].astype(F32)
+        c = c + _unpack_counts(r[k:, :])
+    return total, c
+
+
+def _far_kernel(keep_ref, cnt_ref, *refs):
     o_ref = refs[-1]
-    k = o_ref.shape[0] - COUNT_ROWS
-    total = _total(refs[:-1])
-    o_ref[:k, :] = total[:k].astype(BF16)
-    o_ref[k:, :] = _pack_counts(_unpack_counts(total[k:]))
-
-
-def add_blocks(parts):
-    return pl.pallas_call(
-        _add_kernel,
-        out_shape=jax.ShapeDtypeStruct(parts[0].shape, BF16),
-        in_specs=[VMEM] * len(parts),
-        out_specs=VMEM,
-        compiler_params=_params(8),
-        cost_estimate=pl.CostEstimate(
-            flops=0, bytes_accessed=10 * parts[0].size, transcendentals=0
-        ),
-        name="add_blocks",
-    )(*parts)
-
-
-def _final_kernel(n, dp_ref, *refs):
-    parts = (refs[:n], refs[n : n + 1])
-    c_ref, o_ref = refs[n + 1 :]
+    k = keep_ref.shape[0]
+    total, c = _totals(keep_ref, cnt_ref, refs[: NZ - 1])
+    o_ref[:k, :] = total.astype(BF16)
+    o_ref[k:, :] = _pack_counts(c)
+
+
+def _final_kernel(dp_ref, keep_ref, cnt_ref, *refs):
+    other_ref, c_ref, o_ref = refs[-3:]
     k = c_ref.shape[0] // 2
-    for j in range(2):
-        side = dp_ref[0] // NZ if j == 0 else 1 - dp_ref[0] // NZ
+    xh = dp_ref[0] // NZ
+    cols = pl.ds(pl.multiple_of(dp_ref[0] * 128, 128), 128)
+    mine = _totals(keep_ref, cnt_ref, refs[:-3])
+    other = other_ref[:k, :].astype(F32), _unpack_counts(other_ref[k:, :])
+    for side, (total, c) in ((xh, mine), (1 - xh, other)):
         off = pl.multiple_of(side * k, k)
-        total = _total(parts[j])
-        c = _unpack_counts(total[k:])
         cnt = jnp.concatenate([c[q : q + 1, :] for q in range(k // 128)], axis=1)
-        cols = pl.ds(pl.multiple_of(dp_ref[0] * 128, 128), 128)
-        top = total[:k] + PRIOR * c_ref[pl.ds(off, k), cols].astype(F32)
+        top = total + PRIOR * c_ref[pl.ds(off, k), cols].astype(F32)
         o_ref[:, pl.ds(off, k)] = top.T / (cnt + PRIOR)
 
 
-def finish(dp, mine, other, centroids):
-    return pl.pallas_call(
-        functools.partial(_final_kernel, len(mine)),
+def finish(dp, parts, other, centroids):
+    return pl.pallas_call(
+        _final_kernel,
         out_shape=jax.ShapeDtypeStruct((128, centroids.shape[0]), F32),
-        in_specs=[SMEM] + [VMEM] * (len(mine) + 2),
+        in_specs=[SMEM] + [VMEM] * (len(parts) + 2),
         out_specs=VMEM,
         compiler_params=_params(12),
         name="finish",
-    )(dp, *mine, other, centroids)
+    )(dp, *parts, other, centroids)
 
 
 def _slots():
@@ -394,17 +395,6 @@
             o_ref[b : b + 1, n * r + off : n * r + off + 128] = q[i : i + 1, :]
 
 
-def _small(kernel, shape, args, name):
-    return pl.pallas_call(
-        kernel,
-        out_shape=jax.ShapeDtypeStruct(shape, F32),
-        in_specs=[VMEM] * len(args),
-        out_specs=VMEM,
-        compiler_params=_params(2),
-        name=name,
-    )(*args)
-
-
 def local(points, centroids):
     features = points.shape[1]
     gain = BETA_GAIN * features ** (-0.5) * math.log2(math.e)
@@ -412,11 +402,11 @@
 
     shards = [points] + [send_first(points, d) for d in (1, 2, 3)]
     whole = (centroids, send_core(centroids))
-    own, own_norm = load_half(dp, whole[0])
+    own, own_norm = load_half(dp, whole[0], 4)
     line_a, line_b = join(shards[0], shards[1], own_norm), join(shards[2], shards[3], own_norm)
     half = line_a.shape[0]
     up_a, down_b = send_second(line_a, 1), send_second(line_b, 3)
-    sib, sib_norm = load_half(dp, whole[1])
+    sib, sib_norm = load_half(dp, whole[1], 4)
     cents = (own, sib)
     late_a, late_b, sib_norm = lax.optimization_barrier((line_a, line_b, sib_norm))
     norms = (own_norm, sib_norm)
@@ -437,24 +427,28 @@
     run(up_b, down_a)
     run(far_a, far_b)
 
-    shape = (2, 16, 128)
-    pack = _small(functools.partial(_pack_kernel, gain), shape, stats, "stats_pack")
+    shape = jax.ShapeDtypeStruct((2, 16, 128), F32)
+    pack = _call(functools.partial(_pack_kernel, gain), shape, stats, "stats_pack", 2)
     every = [pack] + [send_first(pack, d) for d in (1, 2, 3)]
-    pack = _small(functools.partial(_merge_kernel, gain, 0), shape, every, "stats_merge")
+    pack = _call(functools.partial(_merge_kernel, gain, 0), shape, every, "stats_merge", 2)
     every = [pack] + [send_second(pack, d) for d in (1, 2, 3)]
-    scales = _small(
+    scales = _call(
         functools.partial(_scale_kernel, gain, 1),
-        (8, sum(st.shape[1] for st in stats)),
+        jax.ShapeDtypeStruct((8, sum(st.shape[1] for st in stats)), F32),
         every + stats,
         "stats_scale",
+        2,
     )
 
-    swapped = [send_core(weighted_sums(1, g, ws, xs, scales)[0]) for g in range(2)]
-    got = []
+    got, order = [], []
     for g in range(2):
-        sums = weighted_sums(0, g, ws, xs, scales, add=swapped[g])
-        got.append([sums[3]] + [send_z(sums[n], d) for n, d in enumerate(SHIFTS[:3])])
-    other = send_far(add_blocks(got[0]))
+        part = send_core(weighted_sums(1, g, ws, xs, scales, order))
+        acc, cnt = weighted_sums(0, g, ws, xs, scales, order)
+        *blocks, keep, cnt = mix(acc, cnt, part)
+        order = [cnt]
+        got.append([keep, cnt] + [send_z(v, d) for v, d in zip(blocks, SHIFTS)])
+    rows = jax.ShapeDtypeStruct(blocks[0].shape, BF16)
+    other = send_far(_call(_far_kernel, rows, got[0] + order, "far_sum"))
     return finish(dp, got[1], other, centroids)
 
 

time: 94.1 us -> 92 us (0.978)
  waiting for transfers between devices: 22.5 us -> 19.6 us
    ppermute x25, waiting for transfers between devices: 22.5 us -> 19.6 us  [_send(): return lax.ppermute(a, AXES, pairs)]
    pallas_call x9 -> x11, Pallas kernels: 12 us -> 12.5 us  [the longest x4 10.5 us: weighted_sums(): pl.pallas_call(functools.partial(_sum_kernel, half, group, n_arr), out_sh...]
  transfers between devices with their start and end apart: 25 -> 25, of which waited for: 9 -> 10; matrix products, arithmetic and copies ran while one was open for 0% -> 0% of each run, Pallas kernels for 23% -> 24%
where the time goes in v4:
time: 92 us; the launch traced here: 91.9 us
  starting transfers between devices  39.6 us (43%)
  Pallas kernels  30.2 us (33%)
  waiting for transfers between devices  19.6 us (21%)
  local copies, waits for them, and re-layouts  2.2 us (2%)
    ppermute x25, starting transfers between devices, _send(): return lax.ppermute(a, AXES, pairs)  39.6 us
    ppermute x25, waiting for transfers between devices, _send(): return lax.ppermute(a, AXES, pairs)  19.6 us
    pallas_call x4, Pallas kernels, score(): pl.pallas_call(functools.partial(_score_kernel, gain, len(xs)), out_shape...  14.3 us
    pallas_call x4, Pallas kernels, weighted_sums(): pl.pallas_call(functools.partial(_sum_kernel, half, group, n_arr), out_sh...  10.5 us
    pallas_call x2, Pallas kernels, load_half(): pl.pallas_call(_load_kernel, out_shape=(jax.ShapeDtypeStruct((k, d), BF16...  3.34 us
    unnamed x6, local copies, waits for them, and re-layouts  2.2 us
  transfers between devices with their start and end apart: 25, of which 10 were waited for; matrix products, arithmetic and copies ran while one was open for 0% of the time, Pallas kernels for 24%

profile of v4, /device:TPU:1, one launch (start us, length us, event | category | flops | bytes accessed | tf_op | source)
XLA Modules:
  0.0 91.9 jit_solution(1894887621756732682)
XLA Ops:
  0.0 1.4 %collective-permute-start.3 = (bf16[2048,1024]{1,0:T(8,128)(2,1)}, bf16[2048,1024]{1,0:T(8,128)(2,1)}, u32[]{:S(2)}, u32[]{:S(2)}) collective-permute-start(bf16[2048,1024]{1,0:T(8,128)(2,1)} %refs_4_.1), channel_id=1, source_target_pairs={{0,1},{1,0},{2,3},{3,2},{4,5},{5,4},{6,7},{7,6},{8,9},{9,8},{10,11... | collective-permute-start | bytes 12582920 | tf_op jit(solution)/shard_map/ppermute | solution.py:38
  1.4 1.3 %collective-permute-start = (bf16[128,1024]{1,0:T(8,128)(2,1)}, bf16[128,1024]{1,0:T(8,128)(2,1)S(1)}, u32[]{:S(2)}, u32[]{:S(2)}) collective-permute-start(bf16[128,1024]{1,0:T(8,128)(2,1)} %refs_0_.1), channel_id=1, source_target_pairs={{0,2},{1,9},{2,4},{3,11},{4,6},{5,13},{6,0},{7,15},{8,10},{9,65},{... | collective-permute-start | bytes 786440 | tf_op jit(solution)/shard_map/ppermute | solution.py:38
  2.7 1.4 %collective-permute-start.2 = (bf16[128,1024]{1,0:T(8,128)(2,1)}, bf16[128,1024]{1,0:T(8,128)(2,1)S(1)}, u32[]{:S(2)}, u32[]{:S(2)}) collective-permute-start(bf16[128,1024]{1,0:T(8,128)(2,1)} %refs_0_.1), channel_id=1, source_target_pairs={{0,6},{1,73},{2,0},{3,75},{4,2},{5,77},{6,4},{7,79},{8,14},{9,1},{... | collective-permute-start | bytes 786440 | tf_op jit(solution)/shard_map/ppermute | solution.py:38
  4.1 1.6 %collective-permute-start.1 = (bf16[128,1024]{1,0:T(8,128)(2,1)}, bf16[128,1024]{1,0:T(8,128)(2,1)S(1)}, u32[]{:S(2)}, u32[]{:S(2)}) collective-permute-start(bf16[128,1024]{1,0:T(8,128)(2,1)} %refs_0_.1), channel_id=1, source_target_pairs={{0,4},{1,65},{2,6},{3,67},{4,0},{5,69},{6,2},{7,71},{8,12},{9,73},... | collective-permute-start | bytes 786440 | tf_op jit(solution)/shard_map/ppermute | solution.py:38
  5.7 2.2 %copy-done = bf16[2048,1024]{1,0:T(8,128)(2,1)S(1)} copy-done((bf16[2048,1024]{1,0:T(8,128)(2,1)S(1)}, bf16[2048,1024]{1,0:T(8,128)(2,1)}, u32[]{:S(2)}) %copy-start) | copy-done | bytes 4194328
  7.9 1.3 %load_half.2 = (bf16[1024,1024]{1,0:T(8,128)(2,1)S(1)}, f32[1024,128]{1,0:T(8,128)S(1)}) custom-call(s32[1]{0:T(128)} %bitcast.dp_ref, bf16[2048,1024]{1,0:T(8,128)(2,1)S(1)} %copy-done), custom_call_target="tpu_custom_call" | custom-call | flops 1024 | bytes 1024 | tf_op jit(solution)/shard_map/load_half/pallas_call | solution.py:86
  9.3 1.4 %collective-permute-start.4 = (bf16[256,1024]{1,0:T(8,128)(2,1)S(1)}, bf16[256,1024]{1,0:T(8,128)(2,1)S(1)}, u32[]{:S(2)}, u32[]{:S(2)}) collective-permute-start(bf16[256,1024]{1,0:T(8,128)(2,1)S(1)} %join.2.refs_0_), channel_id=1, source_target_pairs={{0,8},{1,3},{2,10},{3,5},{4,12},{5,7},{6,14},{7,1},{8,64},{9,11},{... | collective-permute-start | bytes 1572872 | tf_op jit(solution)/shard_map/ppermute | solution.py:38
  10.6 1.6 %collective-permute-done.1.refs_0_ = bf16[128,1024]{1,0:T(8,128)(2,1)S(1)} collective-permute-done((bf16[128,1024]{1,0:T(8,128)(2,1)}, bf16[128,1024]{1,0:T(8,128)(2,1)S(1)}, u32[]{:S(2)}, u32[]{:S(2)}) %collective-permute-start.1) | collective-permute-done | bytes 262176 | tf_op jit(solution)/shard_map/ppermute | solution.py:38
  12.3 2.5 %collective-permute-start.5 = (bf16[256,1024]{1,0:T(8,128)(2,1)S(1)}, bf16[256,1024]{1,0:T(8,128)(2,1)S(1)}, u32[]{:S(2)}, u32[]{:S(2)}) collective-permute-start(bf16[256,1024]{1,0:T(8,128)(2,1)S(1)} %join.3.refs_1_), channel_id=1, source_target_pairs={{0,72},{1,7},{2,74},{3,1},{4,76},{5,3},{6,78},{7,5},{8,0},{9,15},{... | collective-permute-start | bytes 1572872 | tf_op jit(solution)/shard_map/ppermute | solution.py:38
  14.8 2.1 %load_half.3 = (bf16[1024,1024]{1,0:T(8,128)(2,1)S(1)}, f32[1024,128]{1,0:T(8,128)S(1)}) custom-call(s32[1]{0:T(128)} %bitcast.dp_ref, bf16[2048,1024]{1,0:T(8,128)(2,1)} %collective-permute-done.3.c_ref), custom_call_target="tpu_custom_call" | custom-call | flops 1024 | bytes 1024 | tf_op jit(solution)/shard_map/load_half/pallas_call | solution.py:86
  16.9 0.1 collective-permute-start.6
  16.9 2.7 %collective-permute-start.7 = (bf16[256,1024]{1,0:T(8,128)(2,1)S(1)}, bf16[256,1024]{1,0:T(8,128)(2,1)S(1)}, u32[]{:S(2)}, u32[]{:S(2)}) collective-permute-start(bf16[256,1024]{1,0:T(8,128)(2,1)S(1)} %join.2.refs_0_), channel_id=1, source_target_pairs={{0,72},{1,7},{2,74},{3,1},{4,76},{5,3},{6,78},{7,5},{8,0},{9,15},{... | collective-permute-start | bytes 1572872 | tf_op jit(solution)/shard_map/ppermute | solution.py:38
  19.6 3.6 %score.4 = (bf16[2,1024,512]{2,1,0:T(8,128)(2,1)S(1)}, f32[8,512]{1,0:T(8,128)S(1)}, bf16[512,1024]{1,0:T(8,128)(2,1)S(1)}) custom-call(s32[1]{0:T(128)} %bitcast.dp_ref, bf16[256,1024]{1,0:T(8,128)(2,1)S(1)} %join.2.refs_0_, bf16[256,1024]{1,0:T(8,128)(2,1)S(1)} %join.3.refs_1_, bf16[1024,1024]{1,0:T(8,128)(2,1)S(1)} %get-tuple-element.42.refs_2_, ...), custom_call_target="tpu_custom_call" | custom-call | flops 1024 | bytes 1024 | tf_op jit(solution)/shard_map/score/pallas_call | solution.py:180
  23.2 0.1 collective-permute-start.8
  23.3 2.7 %collective-permute-start.9 = (bf16[256,1024]{1,0:T(8,128)(2,1)S(1)}, bf16[256,1024]{1,0:T(8,128)(2,1)S(1)}, u32[]{:S(2)}, u32[]{:S(2)}) collective-permute-start(bf16[256,1024]{1,0:T(8,128)(2,1)S(1)} %collective-permute-done.5.refs_1_), channel_id=1, source_target_pairs={{0,72},{1,7},{2,74},{3,1},{4,76},{5,3},{6,78},{7,5},{8,0},{9,15},{... | collective-permute-start | bytes 1572872 | tf_op jit(solution)/shard_map/ppermute | solution.py:38
  26.0 3.6 %score.5 = (bf16[2,1024,512]{2,1,0:T(8,128)(2,1)S(1)}, f32[8,512]{1,0:T(8,128)S(1)}, bf16[512,1024]{1,0:T(8,128)(2,1)S(1)}) custom-call(s32[1]{0:T(128)} %bitcast.dp_ref, bf16[256,1024]{1,0:T(8,128)(2,1)S(1)} %collective-permute-done.4.refs_0_, bf16[256,1024]{1,0:T(8,128)(2,1)S(1)} %collective-permute-done.5.refs_1_, ...), custom_call_target="tpu_custom_call" | custom-call | flops 1024 | bytes 1024 | tf_op jit(solution)/shard_map/score/pallas_call | solution.py:180
  29.5 3.6 %score.6 = (bf16[2,1024,512]{2,1,0:T(8,128)(2,1)S(1)}, f32[8,512]{1,0:T(8,128)S(1)}, bf16[512,1024]{1,0:T(8,128)(2,1)S(1)}) custom-call(s32[1]{0:T(128)} %bitcast.dp_ref, bf16[256,1024]{1,0:T(8,128)(2,1)S(1)} %collective-permute-done.6.refs_0_, bf16[256,1024]{1,0:T(8,128)(2,1)S(1)} %collective-permute-done.7.refs_1_, ...), custom_call_target="tpu_custom_call" | custom-call | flops 1024 | bytes 1024 | tf_op jit(solution)/shard_map/score/pallas_call | solution.py:180
  33.1 3.6 %score.7 = (bf16[2,1024,512]{2,1,0:T(8,128)(2,1)S(1)}, f32[8,512]{1,0:T(8,128)S(1)}, bf16[512,1024]{1,0:T(8,128)(2,1)S(1)}) custom-call(s32[1]{0:T(128)} %bitcast.dp_ref, bf16[256,1024]{1,0:T(8,128)(2,1)S(1)} %collective-permute-done.8.refs_0_, bf16[256,1024]{1,0:T(8,128)(2,1)S(1)} %collective-permute-done.9.refs_1_, ...), custom_call_target="tpu_custom_call" | custom-call | flops 1024 | bytes 1024 | tf_op jit(solution)/shard_map/score/pallas_call | solution.py:180
  36.8 2.1 %collective-permute-start.12 = (f32[2,16,128]{2,1,0:T(8,128)S(1)}, f32[2,16,128]{2,1,0:T(8,128)S(1)}, u32[]{:S(2)}, u32[]{:S(2)}) collective-permute-start(f32[2,16,128]{2,1,0:T(8,128)S(1)} %stats_pack.1.refs_0_), channel_id=1, source_target_pairs={{0,6},{1,73},{2,0},{3,75},{4,2},{5,77},{6,4},{7,79},{8,14},{9,1},{... | collective-permute-start | bytes 49160 | tf_op jit(solution)/shard_map/ppermute | solution.py:38
  38.8 0.9 %collective-permute-start.11 = (f32[2,16,128]{2,1,0:T(8,128)S(1)}, f32[2,16,128]{2,1,0:T(8,128)S(1)}, u32[]{:S(2)}, u32[]{:S(2)}) collective-permute-start(f32[2,16,128]{2,1,0:T(8,128)S(1)} %stats_pack.1.refs_0_), channel_id=1, source_target_pairs={{0,4},{1,65},{2,6},{3,67},{4,0},{5,69},{6,2},{7,71},{8,12},{9,73},... | collective-permute-start | bytes 49160 | tf_op jit(solution)/shard_map/ppermute | solution.py:38
  39.8 3.2 %collective-permute-done.11.refs_2_ = f32[2,16,128]{2,1,0:T(8,128)S(1)} collective-permute-done((f32[2,16,128]{2,1,0:T(8,128)S(1)}, f32[2,16,128]{2,1,0:T(8,128)S(1)}, u32[]{:S(2)}, u32[]{:S(2)}) %collective-permute-start.11) | collective-permute-done | bytes 16416 | tf_op jit(solution)/shard_map/ppermute | solution.py:38
  42.9 0.6 collective-permute-done.10.refs_1_
  43.6 2.2 %collective-permute-start.15 = (f32[2,16,128]{2,1,0:T(8,128)S(1)}, f32[2,16,128]{2,1,0:T(8,128)S(1)}, u32[]{:S(2)}, u32[]{:S(2)}) collective-permute-start(f32[2,16,128]{2,1,0:T(8,128)S(1)} %stats_merge.1.refs_0_), channel_id=1, source_target_pairs={{0,72},{1,7},{2,74},{3,1},{4,76},{5,3},{6,78},{7,5},{8,0},{9,15},{... | collective-permute-start | bytes 49160 | tf_op jit(solution)/shard_map/ppermute | solution.py:38
  45.8 0.7 collective-permute-start.13
  46.4 0.2 collective-permute-done.15.refs_3_
  46.6 3.2 %collective-permute-done.14.refs_2_ = f32[2,16,128]{2,1,0:T(8,128)S(1)} collective-permute-done((f32[2,16,128]{2,1,0:T(8,128)S(1)}, f32[2,16,128]{2,1,0:T(8,128)S(1)}, u32[]{:S(2)}, u32[]{:S(2)}) %collective-permute-start.14) | collective-permute-done | bytes 16416 | tf_op jit(solution)/shard_map/ppermute | solution.py:38
  49.9 2.7 %sums_sib.2 = bf16[4,1056,128]{2,1,0:T(8,128)(2,1)S(1)} custom-call(bf16[2,1024,512]{2,1,0:T(8,128)(2,1)S(1)} %get-tuple-element.46.refs_0_, bf16[2,1024,512]{2,1,0:T(8,128)(2,1)S(1)} %get-tuple-element.51.refs_1_, bf16[2,1024,512]{2,1,0:T(8,128)(2,1)S(1)} %get-tuple-element.55.refs_2_, bf16[2,1024,512]{2,1,0:T(8,128)(2,1)S(1)} %get-tuple-element.57.refs_3_, ...), custom_call_target="tpu_custom_call" | custom-call | flops 1024 | bytes 1024 | tf_op jit(solution)/shard_map/sums_sib/pallas_call | solution.py:251
  52.6 6.7 %collective-permute-start.16 = (bf16[4,1056,128]{2,1,0:T(8,128)(2,1)S(1)}, bf16[4,1056,128]{2,1,0:T(8,128)(2,1)S(1)}, u32[]{:S(2)}, u32[]{:S(2)}) collective-permute-start(bf16[4,1056,128]{2,1,0:T(8,128)(2,1)S(1)} %sums_sib.2), channel_id=1, source_target_pairs={{0,1},{1,0},{2,3},{3,2},{4,5},{5,4},{6,7},{7,6},{8,9},{9,8},{10,11... | collective-permute-start | bytes 3244040 | tf_op jit(solution)/shard_map/ppermute | solution.py:38
  59.3 2.6 %sums_own.2 = (f32[4,1024,128]{2,1,0:T(8,128)S(1)}, f32[8,128]{1,0:T(8,128)S(1)}) custom-call(bf16[2,1024,512]{2,1,0:T(8,128)(2,1)S(1)} %get-tuple-element.46.refs_0_, bf16[2,1024,512]{2,1,0:T(8,128)(2,1)S(1)} %get-tuple-element.51.refs_1_, bf16[2,1024,512]{2,1,0:T(8,128)(2,1)S(1)} %get-tuple-element.55.refs_2_, ...), custom_call_target="tpu_custom_call" | custom-call | flops 42949672960 | bytes 1024 | tf_op jit(solution)/shard_map/sums_own/pallas_call | solution.py:251
  61.9 0.2 mix.2
  62.1 3.7 %collective-permute-start.21 = (bf16[1056,128]{1,0:T(8,128)(2,1)S(1)}, bf16[1056,128]{1,0:T(8,128)(2,1)S(1)}, u32[]{:S(2)}, u32[]{:S(2)}) collective-permute-start(bf16[1056,128]{1,0:T(8,128)(2,1)S(1)} %get-tuple-element.74), channel_id=1, source_target_pairs={{0,32},{1,33},{2,34},{3,35},{4,36},{5,37},{6,38},{7,39},{8,40},{9,... | collective-permute-start | bytes 811016 | tf_op jit(solution)/shard_map/ppermute | solution.py:38
  65.7 0.7 collective-permute-start.22
  66.5 1.9 %collective-permute-start.23 = (bf16[1056,128]{1,0:T(8,128)(2,1)S(1)}, bf16[1056,128]{1,0:T(8,128)(2,1)S(1)}, u32[]{:S(2)}, u32[]{:S(2)}) collective-permute-start(bf16[1056,128]{1,0:T(8,128)(2,1)S(1)} %get-tuple-element.76), channel_id=1, source_target_pairs={{0,48},{1,49},{2,50},{3,51},{4,52},{5,53},{6,54},{7,55},{8,56},{9,... | collective-permute-start | bytes 811016 | tf_op jit(solution)/shard_map/ppermute | solution.py:38
  68.4 2.7 %sums_sib.3 = bf16[4,1056,128]{2,1,0:T(8,128)(2,1)S(1)} custom-call(bf16[2,1024,512]{2,1,0:T(8,128)(2,1)S(1)} %get-tuple-element.46.refs_0_, bf16[2,1024,512]{2,1,0:T(8,128)(2,1)S(1)} %get-tuple-element.51.refs_1_, bf16[2,1024,512]{2,1,0:T(8,128)(2,1)S(1)} %get-tuple-element.55.refs_2_, bf16[2,1024,512]{2,1,0:T(8,128)(2,1)S(1)} %get-tuple-element.57.refs_3_, ...), custom_call_target="tpu_custom_call" | custom-call | flops 1024 | bytes 1024 | tf_op jit(solution)/shard_map/sums_sib/pallas_call | solution.py:251
  71.1 1.0 %collective-permute-start.17 = (bf16[4,1056,128]{2,1,0:T(8,128)(2,1)S(1)}, bf16[4,1056,128]{2,1,0:T(8,128)(2,1)S(1)}, u32[]{:S(2)}, u32[]{:S(2)}) collective-permute-start(bf16[4,1056,128]{2,1,0:T(8,128)(2,1)S(1)} %sums_sib.3), channel_id=1, source_target_pairs={{0,1},{1,0},{2,3},{3,2},{4,5},{5,4},{6,7},{7,6},{8,9},{9,8},{10,11... | collective-permute-start | bytes 3244040 | tf_op jit(solution)/shard_map/ppermute | solution.py:38
  72.1 2.6 %sums_own.3 = (f32[4,1024,128]{2,1,0:T(8,128)S(1)}, f32[8,128]{1,0:T(8,128)S(1)}) custom-call(bf16[2,1024,512]{2,1,0:T(8,128)(2,1)S(1)} %get-tuple-element.46.refs_0_, bf16[2,1024,512]{2,1,0:T(8,128)(2,1)S(1)} %get-tuple-element.51.refs_1_, bf16[2,1024,512]{2,1,0:T(8,128)(2,1)S(1)} %get-tuple-element.55.refs_2_, ...), custom_call_target="tpu_custom_call" | custom-call | flops 42949672960 | bytes 1024 | tf_op jit(solution)/shard_map/sums_own/pallas_call | solution.py:251
  74.7 0.2 mix.3
  75.0 0.1 collective-permute-start.18
  75.0 0.3 collective-permute-start.19
  75.4 2.5 %collective-permute-start.20 = (bf16[1056,128]{1,0:T(8,128)(2,1)S(1)}, bf16[1056,128]{1,0:T(8,128)(2,1)S(1)}, u32[]{:S(2)}, u32[]{:S(2)}) collective-permute-start(bf16[1056,128]{1,0:T(8,128)(2,1)S(1)} %get-tuple-element.72), channel_id=1, source_target_pairs={{0,48},{1,49},{2,50},{3,51},{4,52},{5,53},{6,54},{7,55},{8,56},{9,... | collective-permute-start | bytes 811016 | tf_op jit(solution)/shard_map/ppermute | solution.py:38
  77.8 0.7 collective-permute-done.22.refs_1_
  78.5 0.4 collective-permute-done.23.refs_2_
  78.9 0.1 far_sum.1
  79.0 1.8 %collective-permute-start.24 = (bf16[1056,128]{1,0:T(8,128)(2,1)S(1)}, bf16[1056,128]{1,0:T(8,128)(2,1)S(1)}, u32[]{:S(2)}, u32[]{:S(2)}) collective-permute-start(bf16[1056,128]{1,0:T(8,128)(2,1)S(1)} %far_sum.1), channel_id=1, source_target_pairs={{0,64},{1,65},{2,66},{3,67},{4,68},{5,69},{6,70},{7,71},{8,72},{9,... | collective-permute-start | bytes 811016 | tf_op jit(solution)/shard_map/ppermute | solution.py:38
  80.8 3.8 %collective-permute-done.18.refs_0_ = bf16[1056,128]{1,0:T(8,128)(2,1)S(1)} collective-permute-done((bf16[1056,128]{1,0:T(8,128)(2,1)S(1)}, bf16[1056,128]{1,0:T(8,128)(2,1)S(1)}, u32[]{:S(2)}, u32[]{:S(2)}) %collective-permute-start.18) | collective-permute-done | bytes 270368 | tf_op jit(solution)/shard_map/ppermute | solution.py:38
  84.6 5.7 %collective-permute-done.19.refs_1_ = bf16[1056,128]{1,0:T(8,128)(2,1)S(1)} collective-permute-done((bf16[1056,128]{1,0:T(8,128)(2,1)S(1)}, bf16[1056,128]{1,0:T(8,128)(2,1)S(1)}, u32[]{:S(2)}, u32[]{:S(2)}) %collective-permute-start.19) | collective-permute-done | bytes 270368 | tf_op jit(solution)/shard_map/ppermute | solution.py:38
  90.3 0.2 collective-permute-done.20.refs_2_
  90.5 1.4 %finish.1 = f32[128,2048]{1,0:T(8,128)} custom-call(s32[1]{0:T(128)} %bitcast.dp_ref, f32[1024,128]{1,0:T(8,128)S(1)} %get-tuple-element.68.keep_ref, f32[8,128]{1,0:T(8,128)S(1)} %get-tuple-element.69.refs_3_.cnt_ref, bf16[1056,128]{1,0:T(8,128)(2,1)S(1)} %collective-permute-done.18.refs_0_, bf16[1056,128]{1,0:T(8,128)(2,1)S(1)} %collective-permute-done.19.refs_1_, ...), custom_call_target="tpu_custom_call" | custom-call | tf_op jit(solution)/shard_map/finish/pallas_call | solution.py:328
  (27 shorter events, 0.2 us)
Async XLA Ops:
  0.0 14.8 %collective-permute-start.3 = (bf16[2048,1024]{1,0:T(8,128)(2,1)}, bf16[2048,1024]{1,0:T(8,128)(2,1)}, u32[]{:S(2)}, u32[]{:S(2)}) collective-permute-start(bf16[2048,1024]{1,0:T(8,128)(2,1)} %refs_4_.1), channel_id=1, source_target_pairs={{0,1},{1,0},{2,3},{3,2},{4,5},{5,4},{6,7},{7,6},{8,9},{9,8},{10,11... | collective-permute-start | bytes 12582920 | tf_op jit(solution)/shard_map/ppermute | solution.py:38
  1.4 7.8 %collective-permute-start = (bf16[128,1024]{1,0:T(8,128)(2,1)}, bf16[128,1024]{1,0:T(8,128)(2,1)S(1)}, u32[]{:S(2)}, u32[]{:S(2)}) collective-permute-start(bf16[128,1024]{1,0:T(8,128)(2,1)} %refs_0_.1), channel_id=1, source_target_pairs={{0,2},{1,9},{2,4},{3,11},{4,6},{5,13},{6,0},{7,15},{8,10},{9,65},{... | collective-permute-start | bytes 786440 | tf_op jit(solution)/shard_map/ppermute | solution.py:38
  2.7 7.9 %collective-permute-start.2 = (bf16[128,1024]{1,0:T(8,128)(2,1)}, bf16[128,1024]{1,0:T(8,128)(2,1)S(1)}, u32[]{:S(2)}, u32[]{:S(2)}) collective-permute-start(bf16[128,1024]{1,0:T(8,128)(2,1)} %refs_0_.1), channel_id=1, source_target_pairs={{0,6},{1,73},{2,0},{3,75},{4,2},{5,77},{6,4},{7,79},{8,14},{9,1},{... | collective-permute-start | bytes 786440 | tf_op jit(solution)/shard_map/ppermute | solution.py:38
  4.1 8.1 %collective-permute-start.1 = (bf16[128,1024]{1,0:T(8,128)(2,1)}, bf16[128,1024]{1,0:T(8,128)(2,1)S(1)}, u32[]{:S(2)}, u32[]{:S(2)}) collective-permute-start(bf16[128,1024]{1,0:T(8,128)(2,1)} %refs_0_.1), channel_id=1, source_target_pairs={{0,4},{1,65},{2,6},{3,67},{4,0},{5,69},{6,2},{7,71},{8,12},{9,73},... | collective-permute-start | bytes 786440 | tf_op jit(solution)/shard_map/ppermute | solution.py:38
  5.7 2.2 %copy-start = (bf16[2048,1024]{1,0:T(8,128)(2,1)S(1)}, bf16[2048,1024]{1,0:T(8,128)(2,1)}, u32[]{:S(2)}) copy-start(bf16[2048,1024]{1,0:T(8,128)(2,1)} %refs_4_.1) | copy-start | bytes 12582916
  7.9 1.3 %copy-start.2 = (bf16[128,1024]{1,0:T(8,128)(2,1)S(1)}, bf16[128,1024]{1,0:T(8,128)(2,1)}, u32[]{:S(2)}) copy-start(bf16[128,1024]{1,0:T(8,128)(2,1)} %refs_0_.1) | copy-start | bytes 786436
  9.3 13.9 %collective-permute-start.4 = (bf16[256,1024]{1,0:T(8,128)(2,1)S(1)}, bf16[256,1024]{1,0:T(8,128)(2,1)S(1)}, u32[]{:S(2)}, u32[]{:S(2)}) collective-permute-start(bf16[256,1024]{1,0:T(8,128)(2,1)S(1)} %join.2.refs_0_), channel_id=1, source_target_pairs={{0,8},{1,3},{2,10},{3,5},{4,12},{5,7},{6,14},{7,1},{8,64},{9,11},{... | collective-permute-start | bytes 1572872 | tf_op jit(solution)/shard_map/ppermute | solution.py:38
  12.3 10.9 %collective-permute-start.5 = (bf16[256,1024]{1,0:T(8,128)(2,1)S(1)}, bf16[256,1024]{1,0:T(8,128)(2,1)S(1)}, u32[]{:S(2)}, u32[]{:S(2)}) collective-permute-start(bf16[256,1024]{1,0:T(8,128)(2,1)S(1)} %join.3.refs_1_), channel_id=1, source_target_pairs={{0,72},{1,7},{2,74},{3,1},{4,76},{5,3},{6,78},{7,5},{8,0},{9,15},{... | collective-permute-start | bytes 1572872 | tf_op jit(solution)/shard_map/ppermute | solution.py:38
  16.9 12.7 %collective-permute-start.6 = (bf16[256,1024]{1,0:T(8,128)(2,1)S(1)}, bf16[256,1024]{1,0:T(8,128)(2,1)S(1)}, u32[]{:S(2)}, u32[]{:S(2)}) collective-permute-start(bf16[256,1024]{1,0:T(8,128)(2,1)S(1)} %join.3.refs_1_), channel_id=1, source_target_pairs={{0,8},{1,3},{2,10},{3,5},{4,12},{5,7},{6,14},{7,1},{8,64},{9,11},{... | collective-permute-start | bytes 1572872 | tf_op jit(solution)/shard_map/ppermute | solution.py:38
  16.9 12.6 %collective-permute-start.7 = (bf16[256,1024]{1,0:T(8,128)(2,1)S(1)}, bf16[256,1024]{1,0:T(8,128)(2,1)S(1)}, u32[]{:S(2)}, u32[]{:S(2)}) collective-permute-start(bf16[256,1024]{1,0:T(8,128)(2,1)S(1)} %join.2.refs_0_), channel_id=1, source_target_pairs={{0,72},{1,7},{2,74},{3,1},{4,76},{5,3},{6,78},{7,5},{8,0},{9,15},{... | collective-permute-start | bytes 1572872 | tf_op jit(solution)/shard_map/ppermute | solution.py:38
  23.2 9.9 %collective-permute-start.8 = (bf16[256,1024]{1,0:T(8,128)(2,1)S(1)}, bf16[256,1024]{1,0:T(8,128)(2,1)S(1)}, u32[]{:S(2)}, u32[]{:S(2)}) collective-permute-start(bf16[256,1024]{1,0:T(8,128)(2,1)S(1)} %collective-permute-done.4.refs_0_), channel_id=1, source_target_pairs={{0,8},{1,3},{2,10},{3,5},{4,12},{5,7},{6,14},{7,1},{8,64},{9,11},{... | collective-permute-start | bytes 1572872 | tf_op jit(solution)/shard_map/ppermute | solution.py:38
  23.3 9.9 %collective-permute-start.9 = (bf16[256,1024]{1,0:T(8,128)(2,1)S(1)}, bf16[256,1024]{1,0:T(8,128)(2,1)S(1)}, u32[]{:S(2)}, u32[]{:S(2)}) collective-permute-start(bf16[256,1024]{1,0:T(8,128)(2,1)S(1)} %collective-permute-done.5.refs_1_), channel_id=1, source_target_pairs={{0,72},{1,7},{2,74},{3,1},{4,76},{5,3},{6,78},{7,5},{8,0},{9,15},{... | collective-permute-start | bytes 1572872 | tf_op jit(solution)/shard_map/ppermute | solution.py:38
  36.8 3.0 %collective-permute-start.12 = (f32[2,16,128]{2,1,0:T(8,128)S(1)}, f32[2,16,128]{2,1,0:T(8,128)S(1)}, u32[]{:S(2)}, u32[]{:S(2)}) collective-permute-start(f32[2,16,128]{2,1,0:T(8,128)S(1)} %stats_pack.1.refs_0_), channel_id=1, source_target_pairs={{0,6},{1,73},{2,0},{3,75},{4,2},{5,77},{6,4},{7,79},{8,14},{9,1},{... | collective-permute-start | bytes 49160 | tf_op jit(solution)/shard_map/ppermute | solution.py:38
  38.8 4.1 %collective-permute-start.11 = (f32[2,16,128]{2,1,0:T(8,128)S(1)}, f32[2,16,128]{2,1,0:T(8,128)S(1)}, u32[]{:S(2)}, u32[]{:S(2)}) collective-permute-start(f32[2,16,128]{2,1,0:T(8,128)S(1)} %stats_pack.1.refs_0_), channel_id=1, source_target_pairs={{0,4},{1,65},{2,6},{3,67},{4,0},{5,69},{6,2},{7,71},{8,12},{9,73},... | collective-permute-start | bytes 49160 | tf_op jit(solution)/shard_map/ppermute | solution.py:38
  39.8 3.8 %collective-permute-start.10 = (f32[2,16,128]{2,1,0:T(8,128)S(1)}, f32[2,16,128]{2,1,0:T(8,128)S(1)}, u32[]{:S(2)}, u32[]{:S(2)}) collective-permute-start(f32[2,16,128]{2,1,0:T(8,128)S(1)} %stats_pack.1.refs_0_), channel_id=1, source_target_pairs={{0,2},{1,9},{2,4},{3,11},{4,6},{5,13},{6,0},{7,15},{8,10},{9,65},{... | collective-permute-start | bytes 49160 | tf_op jit(solution)/shard_map/ppermute | solution.py:38
  43.6 3.1 %collective-permute-start.15 = (f32[2,16,128]{2,1,0:T(8,128)S(1)}, f32[2,16,128]{2,1,0:T(8,128)S(1)}, u32[]{:S(2)}, u32[]{:S(2)}) collective-permute-start(f32[2,16,128]{2,1,0:T(8,128)S(1)} %stats_merge.1.refs_0_), channel_id=1, source_target_pairs={{0,72},{1,7},{2,74},{3,1},{4,76},{5,3},{6,78},{7,5},{8,0},{9,15},{... | collective-permute-start | bytes 49160 | tf_op jit(solution)/shard_map/ppermute | solution.py:38
  45.8 4.1 %collective-permute-start.14 = (f32[2,16,128]{2,1,0:T(8,128)S(1)}, f32[2,16,128]{2,1,0:T(8,128)S(1)}, u32[]{:S(2)}, u32[]{:S(2)}) collective-permute-start(f32[2,16,128]{2,1,0:T(8,128)S(1)} %stats_merge.1.refs_0_), channel_id=1, source_target_pairs={{0,64},{1,5},{2,66},{3,7},{4,68},{5,1},{6,70},{7,3},{8,72},{9,13},... | collective-permute-start | bytes 49160 | tf_op jit(solution)/shard_map/ppermute | solution.py:38
  45.8 4.1 %collective-permute-start.13 = (f32[2,16,128]{2,1,0:T(8,128)S(1)}, f32[2,16,128]{2,1,0:T(8,128)S(1)}, u32[]{:S(2)}, u32[]{:S(2)}) collective-permute-start(f32[2,16,128]{2,1,0:T(8,128)S(1)} %stats_merge.1.refs_0_), channel_id=1, source_target_pairs={{0,8},{1,3},{2,10},{3,5},{4,12},{5,7},{6,14},{7,1},{8,64},{9,11},{... | collective-permute-start | bytes 49160 | tf_op jit(solution)/shard_map/ppermute | solution.py:38
  52.6 9.3 %collective-permute-start.16 = (bf16[4,1056,128]{2,1,0:T(8,128)(2,1)S(1)}, bf16[4,1056,128]{2,1,0:T(8,128)(2,1)S(1)}, u32[]{:S(2)}, u32[]{:S(2)}) collective-permute-start(bf16[4,1056,128]{2,1,0:T(8,128)(2,1)S(1)} %sums_sib.2), channel_id=1, source_target_pairs={{0,1},{1,0},{2,3},{3,2},{4,5},{5,4},{6,7},{7,6},{8,9},{9,8},{10,11... | collective-permute-start | bytes 3244040 | tf_op jit(solution)/shard_map/ppermute | solution.py:38
  62.1 13.3 %collective-permute-start.21 = (bf16[1056,128]{1,0:T(8,128)(2,1)S(1)}, bf16[1056,128]{1,0:T(8,128)(2,1)S(1)}, u32[]{:S(2)}, u32[]{:S(2)}) collective-permute-start(bf16[1056,128]{1,0:T(8,128)(2,1)S(1)} %get-tuple-element.74), channel_id=1, source_target_pairs={{0,32},{1,33},{2,34},{3,35},{4,36},{5,37},{6,38},{7,39},{8,40},{9,... | collective-permute-start | bytes 811016 | tf_op jit(solution)/shard_map/ppermute | solution.py:38
  65.7 12.7 %collective-permute-start.22 = (bf16[1056,128]{1,0:T(8,128)(2,1)S(1)}, bf16[1056,128]{1,0:T(8,128)(2,1)S(1)}, u32[]{:S(2)}, u32[]{:S(2)}) collective-permute-start(bf16[1056,128]{1,0:T(8,128)(2,1)S(1)} %get-tuple-element.75), channel_id=1, source_target_pairs={{0,16},{1,17},{2,18},{3,19},{4,20},{5,21},{6,22},{7,23},{8,24},{9,... | collective-permute-start | bytes 811016 | tf_op jit(solution)/shard_map/ppermute | solution.py:38
  66.5 12.4 %collective-permute-start.23 = (bf16[1056,128]{1,0:T(8,128)(2,1)S(1)}, bf16[1056,128]{1,0:T(8,128)(2,1)S(1)}, u32[]{:S(2)}, u32[]{:S(2)}) collective-permute-start(bf16[1056,128]{1,0:T(8,128)(2,1)S(1)} %get-tuple-element.76), channel_id=1, source_target_pairs={{0,48},{1,49},{2,50},{3,51},{4,52},{5,53},{6,54},{7,55},{8,56},{9,... | collective-permute-start | bytes 811016 | tf_op jit(solution)/shard_map/ppermute | solution.py:38
  71.1 3.6 %collective-permute-start.17 = (bf16[4,1056,128]{2,1,0:T(8,128)(2,1)S(1)}, bf16[4,1056,128]{2,1,0:T(8,128)(2,1)S(1)}, u32[]{:S(2)}, u32[]{:S(2)}) collective-permute-start(bf16[4,1056,128]{2,1,0:T(8,128)(2,1)S(1)} %sums_sib.3), channel_id=1, source_target_pairs={{0,1},{1,0},{2,3},{3,2},{4,5},{5,4},{6,7},{7,6},{8,9},{9,8},{10,11... | collective-permute-start | bytes 3244040 | tf_op jit(solution)/shard_map/ppermute | solution.py:38
  74.7 15.8 %copy-start.1 = (bf16[2048,1024]{1,0:T(8,128)(2,1)S(1)}, bf16[2048,1024]{1,0:T(8,128)(2,1)}, u32[]{:S(2)}) copy-start(bf16[2048,1024]{1,0:T(8,128)(2,1)} %refs_4_.1) | copy-start | bytes 12582916
  75.0 9.7 %collective-permute-start.18 = (bf16[1056,128]{1,0:T(8,128)(2,1)S(1)}, bf16[1056,128]{1,0:T(8,128)(2,1)S(1)}, u32[]{:S(2)}, u32[]{:S(2)}) collective-permute-start(bf16[1056,128]{1,0:T(8,128)(2,1)S(1)} %get-tuple-element.70), channel_id=1, source_target_pairs={{0,32},{1,33},{2,34},{3,35},{4,36},{5,37},{6,38},{7,39},{8,40},{9,... | collective-permute-start | bytes 811016 | tf_op jit(solution)/shard_map/ppermute | solution.py:38
  75.0 15.3 %collective-permute-start.19 = (bf16[1056,128]{1,0:T(8,128)(2,1)S(1)}, bf16[1056,128]{1,0:T(8,128)(2,1)S(1)}, u32[]{:S(2)}, u32[]{:S(2)}) collective-permute-start(bf16[1056,128]{1,0:T(8,128)(2,1)S(1)} %get-tuple-element.71), channel_id=1, source_target_pairs={{0,16},{1,17},{2,18},{3,19},{4,20},{5,21},{6,22},{7,23},{8,24},{9,... | collective-permute-start | bytes 811016 | tf_op jit(solution)/shard_map/ppermute | solution.py:38
  75.4 15.2 %collective-permute-start.20 = (bf16[1056,128]{1,0:T(8,128)(2,1)S(1)}, bf16[1056,128]{1,0:T(8,128)(2,1)S(1)}, u32[]{:S(2)}, u32[]{:S(2)}) collective-permute-start(bf16[1056,128]{1,0:T(8,128)(2,1)S(1)} %get-tuple-element.72), channel_id=1, source_target_pairs={{0,48},{1,49},{2,50},{3,51},{4,52},{5,53},{6,54},{7,55},{8,56},{9,... | collective-permute-start | bytes 811016 | tf_op jit(solution)/shard_map/ppermute | solution.py:38
  79.0 11.5 %collective-permute-start.24 = (bf16[1056,128]{1,0:T(8,128)(2,1)S(1)}, bf16[1056,128]{1,0:T(8,128)(2,1)S(1)}, u32[]{:S(2)}, u32[]{:S(2)}) collective-permute-start(bf16[1056,128]{1,0:T(8,128)(2,1)S(1)} %far_sum.1), channel_id=1, source_target_pairs={{0,64},{1,65},{2,66},{3,67},{4,68},{5,69},{6,70},{7,71},{8,72},{9,... | collective-permute-start | bytes 811016 | tf_op jit(solution)/shard_map/ppermute | solution.py:38

commit v5 on v4

--- a/solution.py
+++ b/solution.py
@@ -62,11 +62,11 @@
     return pltpu.CompilerParams(vmem_limit_bytes=mib << 20)
 
 
-def _load_kernel(dp_ref, c_ref, half_ref, o_ref, sems):
+def _load_kernel(id_ref, c_ref, half_ref, o_ref, sems):
     k = half_ref.shape[0]
     n = sems.shape[0]
     step = k // n
-    base = (dp_ref[0] // NZ) * k
+    base = (_dp(id_ref) // NZ) * k
     copies = []
     for j in range(n):
         src = c_ref.at[pl.ds(pl.multiple_of(base + j * step, step), step), :]
@@ -81,7 +81,7 @@
         o_ref[rows, :] = jnp.broadcast_to(s, (step, 128))
 
 
-def load_half(dp, cents, mib):
+def load_half(ident, cents, mib):
     k, d = cents.shape[0] // 2, cents.shape[1]
     return pl.pallas_call(
         _load_kernel,
@@ -95,7 +95,7 @@
         compiler_params=_params(mib),
         cost_estimate=LIGHT,
         name="load_half",
-    )(dp, cents)
+    )(ident, cents)
 
 
 def _join_kernel(*refs):
@@ -119,27 +119,33 @@
     )(*parts)
 
 
+def _dp(id_ref):
+    return id_ref[0] // 16
+
+
 def _block(dp, n):
     xh = (dp // NZ + 1 - n // NZ) % 2
     return xh * NZ + (dp + SHIFTS[n % NZ]) % NZ
 
 
-def _score_kernel(gain, n_x, dp_ref, *refs):
+def _score_kernel(gain, n_x, id_ref, *refs):
     x_refs = refs[:n_x]
     c_refs, h_refs = refs[n_x : n_x + 2], refs[n_x + 2 : n_x + 4]
-    w_ref, st_ref, xp_ref, u_ref, xt_ref = refs[-5:]
+    w_ref, st_ref, xp_ref, u_ref, x_all_ref = refs[-5:]
     k = h_refs[0].shape[0]
     r = w_ref.shape[2]
     kb = 256
     pos = 0
     for x_ref in x_refs:
         n = x_ref.shape[0]
-        xt_ref[:, pos : pos + n] = x_ref[...].T
+        x_all_ref[pos : pos + n, :] = x_ref[...]
         pos += n
 
     def dots(b, j):
         rows = slice(j * kb, (j + 1) * kb)
-        u = jnp.dot(c_refs[b][rows, :], xt_ref[...], preferred_element_type=F32)
+        u = lax.dot_general(
+            c_refs[b][rows, :], x_all_ref[...], (((1,), (1,)), ((), ())), preferred_element_type=F32
+        )
         u = u - jnp.tile(h_refs[b][rows, :], (1, r // 128))
         u_ref[b, rows, :] = u
         return jnp.max(u, axis=0, keepdims=True)
@@ -163,7 +169,7 @@
     st_ref[0:1, :] = m0
     st_ref[1:2, :] = sum(ss)
     for f in range(2 * NZ):
-        off = pl.multiple_of(_block(dp_ref[0], f) * 128, 128)
+        off = pl.multiple_of(_block(_dp(id_ref), f) * 128, 128)
         pos = 0
         for x_ref in x_refs:
             n = x_ref.shape[0]
@@ -174,7 +180,7 @@
     st_ref[4:8, :] = jnp.zeros((4, r), F32)
 
 
-def score(dp, xs, cents, norms, gain, after):
+def score(ident, xs, cents, norms, gain, after):
     r, d = sum(x.shape[0] for x in xs), xs[0].shape[1]
     k = norms[0].shape[0]
     return pl.pallas_call(
@@ -186,11 +192,11 @@
         ),
         in_specs=[SMEM] + [VMEM] * (len(xs) + 4 + len(after)),
         out_specs=(VMEM, VMEM, VMEM),
-        scratch_shapes=[pltpu.VMEM((2, k, r), F32), pltpu.VMEM((d, r), BF16)],
+        scratch_shapes=[pltpu.VMEM((2, k, r), F32), pltpu.VMEM((r, d), BF16)],
         compiler_params=_params(14),
         cost_estimate=LIGHT,
         name="score",
-    )(dp, *xs, *cents, *norms, *after)
+    )(ident, *xs, *cents, *norms, *after)
 
 
 def _sum_kernel(half, group, n_arr, *refs):
@@ -310,11 +316,11 @@
     o_ref[k:, :] = _pack_counts(c)
 
 
-def _final_kernel(dp_ref, keep_ref, cnt_ref, *refs):
+def _final_kernel(id_ref, keep_ref, cnt_ref, *refs):
     other_ref, c_ref, o_ref = refs[-3:]
     k = c_ref.shape[0] // 2
-    xh = dp_ref[0] // NZ
-    cols = pl.ds(pl.multiple_of(dp_ref[0] * 128, 128), 128)
+    xh = _dp(id_ref) // NZ
+    cols = pl.ds(pl.multiple_of(_dp(id_ref) * 128, 128), 128)
     mine = _totals(keep_ref, cnt_ref, refs[:-3])
     other = other_ref[:k, :].astype(F32), _unpack_counts(other_ref[k:, :])
     for side, (total, c) in ((xh, mine), (1 - xh, other)):
@@ -324,7 +330,7 @@
         o_ref[:, pl.ds(off, k)] = top.T / (cnt + PRIOR)
 
 
-def finish(dp, parts, other, centroids):
+def finish(ident, parts, other, centroids):
     return pl.pallas_call(
         _final_kernel,
         out_shape=jax.ShapeDtypeStruct((128, centroids.shape[0]), F32),
@@ -332,7 +338,7 @@
         out_specs=VMEM,
         compiler_params=_params(12),
         name="finish",
-    )(dp, *parts, other, centroids)
+    )(ident, *parts, other, centroids)
 
 
 def _slots():
@@ -357,37 +363,34 @@
     return m, s
 
 
-def _shifted(v, d, axis):
-    if d == 0:
-        return v
-    if axis == 1:
-        return jnp.concatenate([v[16 - 4 * d :], v[: 16 - 4 * d]], axis=0)
-    parts = []
-    for b in range(0, 16, 4):
-        parts += [v[b + 4 - d : b + 4], v[b : b + 4 - d]]
-    return jnp.concatenate(parts, axis=0)
-
-
-def _pack_kernel(gain, *refs):
-    o_ref = refs[-1]
-    pairs = [(_gather_slots(refs, 2 * b), _gather_slots(refs, 2 * b + 1)) for b in range(2)]
-    o_ref[0], o_ref[1] = _merge(pairs, gain)
-
-
-def _merge_kernel(gain, axis, *refs):
-    o_ref = refs[-1]
-    pairs = [
-        (_shifted(refs[d][0], d, axis), _shifted(refs[d][1], d, axis)) for d in range(4)
+def _absolute(id_ref):
+    dp, cent = _dp(id_ref), id_ref[0] % 16
+    x, y, core = (dp // NZ) * 2 + cent // 8, (cent // 2) % NY, cent % 2
+    first = jnp.where(core == 0, y, x)
+    second = jnp.where(core == 0, x, y)
+    return [((second - b) % 4) * 4 + (first - a) % 4 for b in range(4) for a in range(4)]
+
+
+def _pack_kernel(gain, id_ref, *refs):
+    stats, o_ref, t_ref = refs[:4], refs[-2], refs[-1]
+    pairs = [(_gather_slots(stats, 2 * b), _gather_slots(stats, 2 * b + 1)) for b in range(2)]
+    m, s = _merge(pairs, gain)
+    for i, n in enumerate(_absolute(id_ref)):
+        t_ref[0, pl.ds(n, 1), :] = m[i : i + 1, :]
+        t_ref[1, pl.ds(n, 1), :] = s[i : i + 1, :]
+    v = t_ref[...]
+    for j in range(o_ref.shape[0]):
+        o_ref[j] = v
+
+
+def _scale_kernel(gain, id_ref, all_ref, *refs):
+    stats, o_ref, t_ref = refs[:4], refs[-2], refs[-1]
+    top, total = _merge([(all_ref[j, 0], all_ref[j, 1]) for j in range(all_ref.shape[0])], gain)
+    t_ref[0], t_ref[1] = top, total
+    order = _absolute(id_ref)
+    top, total = [
+        jnp.concatenate([t_ref[q, pl.ds(n, 1), :] for n in order], axis=0) for q in range(2)
     ]
-    o_ref[0], o_ref[1] = _merge(pairs, gain)
-
-
-def _scale_kernel(gain, axis, *refs):
-    stats, o_ref = refs[4:8], refs[-1]
-    pairs = [
-        (_shifted(refs[d][0], d, axis), _shifted(refs[d][1], d, axis)) for d in range(4)
-    ]
-    top, total = _merge(pairs, gain)
     r = stats[0].shape[1]
     for b in range(2):
         q = jnp.exp2((_gather_slots(stats, 2 * b) - top) * gain) / total
@@ -395,49 +398,67 @@
             o_ref[b : b + 1, n * r + off : n * r + off + 128] = q[i : i + 1, :]
 
 
+def _statistics(kernel, shape, ident, args, name):
+    return pl.pallas_call(
+        kernel,
+        out_shape=jax.ShapeDtypeStruct(shape, F32),
+        in_specs=[SMEM] + [VMEM] * len(args),
+        out_specs=VMEM,
+        scratch_shapes=[pltpu.VMEM((2, 16, 128), F32)],
+        compiler_params=_params(2),
+        cost_estimate=LIGHT,
+        name=name,
+    )(ident, *args)
+
+
+def _plane_groups():
+    return [
+        [(xh * 4 + z) * 16 + (xl * 4 + y) * 2 + core
+         for xh in range(2) for xl in range(2) for y in range(NY)]
+        for z in range(NZ) for core in range(2)
+    ]
+
+
 def local(points, centroids):
     features = points.shape[1]
     gain = BETA_GAIN * features ** (-0.5) * math.log2(math.e)
-    dp = lax.axis_index("dp").astype(jnp.int32).reshape(1)
+    ident = lax.axis_index(AXES).astype(jnp.int32).reshape(1)
 
     shards = [points] + [send_first(points, d) for d in (1, 2, 3)]
-    whole = (centroids, send_core(centroids))
-    own, own_norm = load_half(dp, whole[0], 4)
+    shard, ident = lax.optimization_barrier((centroids, ident))
+    whole = (centroids, send_core(shard))
+    own, own_norm = load_half(ident, whole[0], 4)
     line_a, line_b = join(shards[0], shards[1], own_norm), join(shards[2], shards[3], own_norm)
     half = line_a.shape[0]
     up_a, down_b = send_second(line_a, 1), send_second(line_b, 3)
-    sib, sib_norm = load_half(dp, whole[1], 4)
+    sib, sib_norm = load_half(ident, whole[1], 4)
     cents = (own, sib)
-    late_a, late_b, sib_norm = lax.optimization_barrier((line_a, line_b, sib_norm))
+    up_a, sib_norm = lax.optimization_barrier((up_a, sib_norm))
+    far_a = send_second(up_a, 1)
     norms = (own_norm, sib_norm)
-    up_b, down_a = send_second(late_b, 1), send_second(late_a, 3)
+    up_b, down_a = send_second(line_b, 1), send_second(line_a, 3)
 
     ws, stats, xs = [], [], []
 
     def run(*xin):
-        w, st, xp = score(dp, xin, cents, norms, gain, stats[-1:])
+        w, st, xp = score(ident, xin, cents, norms, gain, stats[-1:])
         ws.append(w)
         stats.append(st)
         xs.append(xp)
 
     run(line_a, line_b)
-    up_a, down_b, stats[0] = lax.optimization_barrier((up_a, down_b, stats[0]))
-    far_a, far_b = send_second(up_a, 1), send_second(down_b, 3)
+    down_b, stats[0] = lax.optimization_barrier((down_b, stats[0]))
+    far_b = send_second(down_b, 3)
     run(up_a, down_b)
     run(up_b, down_a)
     run(far_a, far_b)
 
-    shape = jax.ShapeDtypeStruct((2, 16, 128), F32)
-    pack = _call(functools.partial(_pack_kernel, gain), shape, stats, "stats_pack", 2)
-    every = [pack] + [send_first(pack, d) for d in (1, 2, 3)]
-    pack = _call(functools.partial(_merge_kernel, gain, 0), shape, every, "stats_merge", 2)
-    every = [pack] + [send_second(pack, d) for d in (1, 2, 3)]
-    scales = _call(
-        functools.partial(_scale_kernel, gain, 1),
-        jax.ShapeDtypeStruct((8, sum(st.shape[1] for st in stats)), F32),
-        every + stats,
-        "stats_scale",
-        2,
+    shape = (NX * NY, 2, 16, 128)
+    packs = _statistics(functools.partial(_pack_kernel, gain), shape, ident, stats, "stats_pack")
+    packs = lax.all_to_all(packs, AXES, 0, 0, tiled=True, axis_index_groups=_plane_groups())
+    shape = (8, sum(st.shape[1] for st in stats))
+    scales = _statistics(
+        functools.partial(_scale_kernel, gain), shape, ident, [packs] + stats, "stats_scale"
     )
 
     got, order = [], []
@@ -449,7 +470,7 @@
         got.append([keep, cnt] + [send_z(v, d) for v, d in zip(blocks, SHIFTS)])
     rows = jax.ShapeDtypeStruct(blocks[0].shape, BF16)
     other = send_far(_call(_far_kernel, rows, got[0] + order, "far_sum"))
-    return finish(dp, got[1], other, centroids)
+    return finish(ident, got[1], other, centroids)
 
 
 def solution(mesh):

time: 92 us -> 88.5 us (0.962)
  blocking collectives: 0 us -> 13.6 us
  starting transfers between devices: 39.6 us -> 29.1 us
  waiting for transfers between devices: 19.6 us -> 14.4 us
  Pallas kernels: 30.2 us -> 28.8 us
    all_to_all x0 -> x1, blocking collectives: none -> 13.6 us  [local(): lax.all_to_all(packs, AXES, 0, 0, tiled=True, axis_index_groups=_plane_gr...]
    ppermute x25 -> x19, starting transfers between devices: 39.6 us -> 29.1 us  [_send(): return lax.ppermute(a, AXES, pairs)]
    ppermute x25 -> x19, waiting for transfers between devices: 19.6 us -> 14.4 us  [_send(): return lax.ppermute(a, AXES, pairs)]
  transfers between devices with their start and end apart: 25 -> 19, of which waited for: 10 -> 7; matrix products, arithmetic and copies ran while one was open for 0% -> 0% of each run, Pallas kernels for 24% -> 24%
where the time goes in v5:
time: 88.5 us; the launch traced here: 88.3 us
  starting transfers between devices  29.1 us (33%)
  Pallas kernels  28.8 us (33%)
  waiting for transfers between devices  14.4 us (16%)
  blocking collectives  13.6 us (15%)
  local copies, waits for them, and re-layouts  2.2 us (2%)
    ppermute x19, starting transfers between devices, _send(): return lax.ppermute(a, AXES, pairs)  29.1 us
    ppermute x19, waiting for transfers between devices, _send(): return lax.ppermute(a, AXES, pairs)  14.4 us
    pallas_call x4, Pallas kernels, score(): pl.pallas_call(functools.partial(_score_kernel, gain, len(xs)), out_shape...  13.7 us
    all_to_all x1, blocking collectives, local(): lax.all_to_all(packs, AXES, 0, 0, tiled=True, axis_index_groups=_plane_gr...  13.6 us
    pallas_call x4, Pallas kernels, weighted_sums(): pl.pallas_call(functools.partial(_sum_kernel, half, group, n_arr), out_sh...  10.4 us
    pallas_call x2, Pallas kernels, load_half(): pl.pallas_call(_load_kernel, out_shape=(jax.ShapeDtypeStruct((k, d), BF16...  2.55 us
    unnamed x6, local copies, waits for them, and re-layouts  2.2 us
  transfers between devices with their start and end apart: 19, of which 7 were waited for; matrix products, arithmetic and copies ran while one was open for 0% of the time, Pallas kernels for 24%

profile of v5, /device:TPU:1, one launch (start us, length us, event | category | flops | bytes accessed | tf_op | source)
XLA Modules:
  0.0 88.3 jit_solution(12518499071540798096)
XLA Ops:
  0.0 1.4 %collective-permute-start.3 = (bf16[2048,1024]{1,0:T(8,128)(2,1)}, bf16[2048,1024]{1,0:T(8,128)(2,1)S(1)}, u32[]{:S(2)}, u32[]{:S(2)}) collective-permute-start(bf16[2048,1024]{1,0:T(8,128)(2,1)} %refs_4_.1), channel_id=1, source_target_pairs={{0,1},{1,0},{2,3},{3,2},{4,5},{5,4},{6,7},{7,6},{8,9},{9,8},{10,11... | collective-permute-start | bytes 12582920 | tf_op jit(solution)/shard_map/ppermute | solution.py:38
  1.4 1.3 %collective-permute-start = (bf16[128,1024]{1,0:T(8,128)(2,1)}, bf16[128,1024]{1,0:T(8,128)(2,1)S(1)}, u32[]{:S(2)}, u32[]{:S(2)}) collective-permute-start(bf16[128,1024]{1,0:T(8,128)(2,1)} %refs_0_.1), channel_id=1, source_target_pairs={{0,2},{1,9},{2,4},{3,11},{4,6},{5,13},{6,0},{7,15},{8,10},{9,65},{... | collective-permute-start | bytes 786440 | tf_op jit(solution)/shard_map/ppermute | solution.py:38
  2.7 1.4 %collective-permute-start.2 = (bf16[128,1024]{1,0:T(8,128)(2,1)}, bf16[128,1024]{1,0:T(8,128)(2,1)S(1)}, u32[]{:S(2)}, u32[]{:S(2)}) collective-permute-start(bf16[128,1024]{1,0:T(8,128)(2,1)} %refs_0_.1), channel_id=1, source_target_pairs={{0,6},{1,73},{2,0},{3,75},{4,2},{5,77},{6,4},{7,79},{8,14},{9,1},{... | collective-permute-start | bytes 786440 | tf_op jit(solution)/shard_map/ppermute | solution.py:38
  4.1 1.6 %collective-permute-start.1 = (bf16[128,1024]{1,0:T(8,128)(2,1)}, bf16[128,1024]{1,0:T(8,128)(2,1)S(1)}, u32[]{:S(2)}, u32[]{:S(2)}) collective-permute-start(bf16[128,1024]{1,0:T(8,128)(2,1)} %refs_0_.1), channel_id=1, source_target_pairs={{0,4},{1,65},{2,6},{3,67},{4,0},{5,69},{6,2},{7,71},{8,12},{9,73},... | collective-permute-start | bytes 786440 | tf_op jit(solution)/shard_map/ppermute | solution.py:38
  5.7 2.2 %copy-done = bf16[2048,1024]{1,0:T(8,128)(2,1)S(1)} copy-done((bf16[2048,1024]{1,0:T(8,128)(2,1)S(1)}, bf16[2048,1024]{1,0:T(8,128)(2,1)}, u32[]{:S(2)}) %copy-start) | copy-done | bytes 4194328
  7.9 1.3 %load_half.2 = (bf16[1024,1024]{1,0:T(8,128)(2,1)S(1)}, f32[1024,128]{1,0:T(8,128)S(1)}) custom-call(s32[1]{0:T(128)} %bitcast.id_ref, bf16[2048,1024]{1,0:T(8,128)(2,1)S(1)} %copy-done), custom_call_target="tpu_custom_call" | custom-call | flops 1024 | bytes 1024 | tf_op jit(solution)/shard_map/load_half/pallas_call | solution.py:86
  9.3 1.4 %collective-permute-start.4 = (bf16[256,1024]{1,0:T(8,128)(2,1)S(1)}, bf16[256,1024]{1,0:T(8,128)(2,1)S(1)}, u32[]{:S(2)}, u32[]{:S(2)}) collective-permute-start(bf16[256,1024]{1,0:T(8,128)(2,1)S(1)} %join.2.refs_0_), channel_id=1, source_target_pairs={{0,8},{1,3},{2,10},{3,5},{4,12},{5,7},{6,14},{7,1},{8,64},{9,11},{... | collective-permute-start | bytes 1572872 | tf_op jit(solution)/shard_map/ppermute | solution.py:38
  10.6 0.0 collective-permute-done.2.refs_1_
  10.6 1.6 %collective-permute-done.1.refs_0_ = bf16[128,1024]{1,0:T(8,128)(2,1)S(1)} collective-permute-done((bf16[128,1024]{1,0:T(8,128)(2,1)}, bf16[128,1024]{1,0:T(8,128)(2,1)S(1)}, u32[]{:S(2)}, u32[]{:S(2)}) %collective-permute-start.1) | collective-permute-done | bytes 262176 | tf_op jit(solution)/shard_map/ppermute | solution.py:38
  12.3 2.5 %collective-permute-start.5 = (bf16[256,1024]{1,0:T(8,128)(2,1)S(1)}, bf16[256,1024]{1,0:T(8,128)(2,1)S(1)}, u32[]{:S(2)}, u32[]{:S(2)}) collective-permute-start(bf16[256,1024]{1,0:T(8,128)(2,1)S(1)} %join.3.refs_1_), channel_id=1, source_target_pairs={{0,72},{1,7},{2,74},{3,1},{4,76},{5,3},{6,78},{7,5},{8,0},{9,15},{... | collective-permute-start | bytes 1572872 | tf_op jit(solution)/shard_map/ppermute | solution.py:38
  14.8 0.5 collective-permute-start.7
  15.2 1.0 %collective-permute-start.6 = (bf16[256,1024]{1,0:T(8,128)(2,1)S(1)}, bf16[256,1024]{1,0:T(8,128)(2,1)S(1)}, u32[]{:S(2)}, u32[]{:S(2)}) collective-permute-start(bf16[256,1024]{1,0:T(8,128)(2,1)S(1)} %join.3.refs_1_), channel_id=1, source_target_pairs={{0,8},{1,3},{2,10},{3,5},{4,12},{5,7},{6,14},{7,1},{8,64},{9,11},{... | collective-permute-start | bytes 1572872 | tf_op jit(solution)/shard_map/ppermute | solution.py:38
  16.3 1.3 %load_half.3 = (bf16[1024,1024]{1,0:T(8,128)(2,1)S(1)}, f32[1024,128]{1,0:T(8,128)S(1)}) custom-call(s32[1]{0:T(128)} %bitcast.id_ref, bf16[2048,1024]{1,0:T(8,128)(2,1)S(1)} %collective-permute-done.3.c_ref), custom_call_target="tpu_custom_call" | custom-call | flops 1024 | bytes 1024 | tf_op jit(solution)/shard_map/load_half/pallas_call | solution.py:86
  17.5 1.4 %collective-permute-done.4.refs_0_ = bf16[256,1024]{1,0:T(8,128)(2,1)S(1)} collective-permute-done((bf16[256,1024]{1,0:T(8,128)(2,1)S(1)}, bf16[256,1024]{1,0:T(8,128)(2,1)S(1)}, u32[]{:S(2)}, u32[]{:S(2)}) %collective-permute-start.4) | collective-permute-done | bytes 524320 | tf_op jit(solution)/shard_map/ppermute | solution.py:38
  18.9 0.0 collective-permute-start.8
  18.9 3.4 %score.4 = (bf16[2,1024,512]{2,1,0:T(8,128)(2,1)S(1)}, f32[8,512]{1,0:T(8,128)S(1)}, bf16[512,1024]{1,0:T(8,128)(2,1)S(1)}) custom-call(s32[1]{0:T(128)} %bitcast.id_ref, bf16[256,1024]{1,0:T(8,128)(2,1)S(1)} %join.2.refs_0_, bf16[256,1024]{1,0:T(8,128)(2,1)S(1)} %join.3.refs_1_, bf16[1024,1024]{1,0:T(8,128)(2,1)S(1)} %get-tuple-element.43.refs_2_, ...), custom_call_target="tpu_custom_call" | custom-call | flops 1024 | bytes 1024 | tf_op jit(solution)/shard_map/score/pallas_call | solution.py:186
  22.4 2.9 %collective-permute-start.9 = (bf16[256,1024]{1,0:T(8,128)(2,1)S(1)}, bf16[256,1024]{1,0:T(8,128)(2,1)S(1)}, u32[]{:S(2)}, u32[]{:S(2)}) collective-permute-start(bf16[256,1024]{1,0:T(8,128)(2,1)S(1)} %collective-permute-done.5.refs_1_), channel_id=1, source_target_pairs={{0,72},{1,7},{2,74},{3,1},{4,76},{5,3},{6,78},{7,5},{8,0},{9,15},{... | collective-permute-start | bytes 1572872 | tf_op jit(solution)/shard_map/ppermute | solution.py:38
  25.3 3.4 %score.5 = (bf16[2,1024,512]{2,1,0:T(8,128)(2,1)S(1)}, f32[8,512]{1,0:T(8,128)S(1)}, bf16[512,1024]{1,0:T(8,128)(2,1)S(1)}) custom-call(s32[1]{0:T(128)} %bitcast.id_ref, bf16[256,1024]{1,0:T(8,128)(2,1)S(1)} %collective-permute-done.4.refs_0_, bf16[256,1024]{1,0:T(8,128)(2,1)S(1)} %collective-permute-done.5.refs_1_, ...), custom_call_target="tpu_custom_call" | custom-call | flops 1024 | bytes 1024 | tf_op jit(solution)/shard_map/score/pallas_call | solution.py:186
  28.7 0.0 collective-permute-done.7.refs_1_
  28.8 3.4 %score.6 = (bf16[2,1024,512]{2,1,0:T(8,128)(2,1)S(1)}, f32[8,512]{1,0:T(8,128)S(1)}, bf16[512,1024]{1,0:T(8,128)(2,1)S(1)}) custom-call(s32[1]{0:T(128)} %bitcast.id_ref, bf16[256,1024]{1,0:T(8,128)(2,1)S(1)} %collective-permute-done.6.refs_0_, bf16[256,1024]{1,0:T(8,128)(2,1)S(1)} %collective-permute-done.7.refs_1_, ...), custom_call_target="tpu_custom_call" | custom-call | flops 1024 | bytes 1024 | tf_op jit(solution)/shard_map/score/pallas_call | solution.py:186
  32.2 0.0 collective-permute-done.8.refs_0_
  32.2 3.4 %score.7 = (bf16[2,1024,512]{2,1,0:T(8,128)(2,1)S(1)}, f32[8,512]{1,0:T(8,128)S(1)}, bf16[512,1024]{1,0:T(8,128)(2,1)S(1)}) custom-call(s32[1]{0:T(128)} %bitcast.id_ref, bf16[256,1024]{1,0:T(8,128)(2,1)S(1)} %collective-permute-done.8.refs_0_, bf16[256,1024]{1,0:T(8,128)(2,1)S(1)} %collective-permute-done.9.refs_1_, ...), custom_call_target="tpu_custom_call" | custom-call | flops 1024 | bytes 1024 | tf_op jit(solution)/shard_map/score/pallas_call | solution.py:186
  35.7 0.1 stats_pack.1
  35.7 13.6 %all_to_all.5.all_ref = f32[16,2,16,128]{3,2,1,0:T(8,128)S(1)} all-to-all(f32[16,2,16,128]{3,2,1,0:T(8,128)S(1)} %stats_pack.1), channel_id=1, replica_groups={{0,2,4,6,8,10,12,14,64,66,68,70,72,74,76,78},{1,3,5,7,9,11,13,15,65,67,..., dimensions={0} | all-to-all | bytes 524288 | tf_op jit(solution)/shard_map/all_to_all | solution.py:458
  49.4 0.1 stats_scale.1.refs_8_
  49.5 2.6 %sums_sib.2 = bf16[4,1056,128]{2,1,0:T(8,128)(2,1)S(1)} custom-call(bf16[2,1024,512]{2,1,0:T(8,128)(2,1)S(1)} %get-tuple-element.48.refs_0_, bf16[2,1024,512]{2,1,0:T(8,128)(2,1)S(1)} %get-tuple-element.53.refs_1_, bf16[2,1024,512]{2,1,0:T(8,128)(2,1)S(1)} %get-tuple-element.55.refs_2_, bf16[2,1024,512]{2,1,0:T(8,128)(2,1)S(1)} %get-tuple-element.57.refs_3_, ...), custom_call_target="tpu_custom_call" | custom-call | flops 1024 | bytes 1024 | tf_op jit(solution)/shard_map/sums_sib/pallas_call | solution.py:257
  52.1 3.7 %collective-permute-start.10 = (bf16[4,1056,128]{2,1,0:T(8,128)(2,1)S(1)}, bf16[4,1056,128]{2,1,0:T(8,128)(2,1)S(1)}, u32[]{:S(2)}, u32[]{:S(2)}) collective-permute-start(bf16[4,1056,128]{2,1,0:T(8,128)(2,1)S(1)} %sums_sib.2), channel_id=1, source_target_pairs={{0,1},{1,0},{2,3},{3,2},{4,5},{5,4},{6,7},{7,6},{8,9},{9,8},{10,11... | collective-permute-start | bytes 3244040 | tf_op jit(solution)/shard_map/ppermute | solution.py:38
  55.8 2.6 %sums_own.2 = (f32[4,1024,128]{2,1,0:T(8,128)S(1)}, f32[8,128]{1,0:T(8,128)S(1)}) custom-call(bf16[2,1024,512]{2,1,0:T(8,128)(2,1)S(1)} %get-tuple-element.48.refs_0_, bf16[2,1024,512]{2,1,0:T(8,128)(2,1)S(1)} %get-tuple-element.53.refs_1_, bf16[2,1024,512]{2,1,0:T(8,128)(2,1)S(1)} %get-tuple-element.55.refs_2_, ...), custom_call_target="tpu_custom_call" | custom-call | flops 42949672960 | bytes 1024 | tf_op jit(solution)/shard_map/sums_own/pallas_call | solution.py:257
  58.4 0.2 mix.2
  58.6 3.7 %collective-permute-start.15 = (bf16[1056,128]{1,0:T(8,128)(2,1)S(1)}, bf16[1056,128]{1,0:T(8,128)(2,1)S(1)}, u32[]{:S(2)}, u32[]{:S(2)}) collective-permute-start(bf16[1056,128]{1,0:T(8,128)(2,1)S(1)} %get-tuple-element.74), channel_id=1, source_target_pairs={{0,32},{1,33},{2,34},{3,35},{4,36},{5,37},{6,38},{7,39},{8,40},{9,... | collective-permute-start | bytes 811016 | tf_op jit(solution)/shard_map/ppermute | solution.py:38
  62.2 0.7 collective-permute-start.16
  63.0 1.9 %collective-permute-start.17 = (bf16[1056,128]{1,0:T(8,128)(2,1)S(1)}, bf16[1056,128]{1,0:T(8,128)(2,1)S(1)}, u32[]{:S(2)}, u32[]{:S(2)}) collective-permute-start(bf16[1056,128]{1,0:T(8,128)(2,1)S(1)} %get-tuple-element.76), channel_id=1, source_target_pairs={{0,48},{1,49},{2,50},{3,51},{4,52},{5,53},{6,54},{7,55},{8,56},{9,... | collective-permute-start | bytes 811016 | tf_op jit(solution)/shard_map/ppermute | solution.py:38
  64.9 2.6 %sums_sib.3 = bf16[4,1056,128]{2,1,0:T(8,128)(2,1)S(1)} custom-call(bf16[2,1024,512]{2,1,0:T(8,128)(2,1)S(1)} %get-tuple-element.48.refs_0_, bf16[2,1024,512]{2,1,0:T(8,128)(2,1)S(1)} %get-tuple-element.53.refs_1_, bf16[2,1024,512]{2,1,0:T(8,128)(2,1)S(1)} %get-tuple-element.55.refs_2_, bf16[2,1024,512]{2,1,0:T(8,128)(2,1)S(1)} %get-tuple-element.57.refs_3_, ...), custom_call_target="tpu_custom_call" | custom-call | flops 1024 | bytes 1024 | tf_op jit(solution)/shard_map/sums_sib/pallas_call | solution.py:257
  67.6 1.1 %collective-permute-start.11 = (bf16[4,1056,128]{2,1,0:T(8,128)(2,1)S(1)}, bf16[4,1056,128]{2,1,0:T(8,128)(2,1)S(1)}, u32[]{:S(2)}, u32[]{:S(2)}) collective-permute-start(bf16[4,1056,128]{2,1,0:T(8,128)(2,1)S(1)} %sums_sib.3), channel_id=1, source_target_pairs={{0,1},{1,0},{2,3},{3,2},{4,5},{5,4},{6,7},{7,6},{8,9},{9,8},{10,11... | collective-permute-start | bytes 3244040 | tf_op jit(solution)/shard_map/ppermute | solution.py:38
  68.7 2.5 %sums_own.3 = (f32[4,1024,128]{2,1,0:T(8,128)S(1)}, f32[8,128]{1,0:T(8,128)S(1)}) custom-call(bf16[2,1024,512]{2,1,0:T(8,128)(2,1)S(1)} %get-tuple-element.48.refs_0_, bf16[2,1024,512]{2,1,0:T(8,128)(2,1)S(1)} %get-tuple-element.53.refs_1_, bf16[2,1024,512]{2,1,0:T(8,128)(2,1)S(1)} %get-tuple-element.55.refs_2_, ...), custom_call_target="tpu_custom_call" | custom-call | flops 42949672960 | bytes 1024 | tf_op jit(solution)/shard_map/sums_own/pallas_call | solution.py:257
  71.2 0.0 copy-start.1
  71.2 0.3 mix.3
  71.5 0.1 collective-permute-start.12
  71.6 0.3 collective-permute-start.13
  71.9 2.5 %collective-permute-start.14 = (bf16[1056,128]{1,0:T(8,128)(2,1)S(1)}, bf16[1056,128]{1,0:T(8,128)(2,1)S(1)}, u32[]{:S(2)}, u32[]{:S(2)}) collective-permute-start(bf16[1056,128]{1,0:T(8,128)(2,1)S(1)} %get-tuple-element.72), channel_id=1, source_target_pairs={{0,48},{1,49},{2,50},{3,51},{4,52},{5,53},{6,54},{7,55},{8,56},{9,... | collective-permute-start | bytes 811016 | tf_op jit(solution)/shard_map/ppermute | solution.py:38
  74.3 0.7 collective-permute-done.16.refs_1_
  75.0 0.3 collective-permute-done.17.refs_2_
  75.3 0.1 far_sum.1
  75.4 1.1 %collective-permute-start.18 = (bf16[1056,128]{1,0:T(8,128)(2,1)S(1)}, bf16[1056,128]{1,0:T(8,128)(2,1)S(1)}, u32[]{:S(2)}, u32[]{:S(2)}) collective-permute-start(bf16[1056,128]{1,0:T(8,128)(2,1)S(1)} %far_sum.1), channel_id=1, source_target_pairs={{0,64},{1,65},{2,66},{3,67},{4,68},{5,69},{6,70},{7,71},{8,72},{9,... | collective-permute-start | bytes 811016 | tf_op jit(solution)/shard_map/ppermute | solution.py:38
  76.6 4.5 %collective-permute-done.12.refs_0_ = bf16[1056,128]{1,0:T(8,128)(2,1)S(1)} collective-permute-done((bf16[1056,128]{1,0:T(8,128)(2,1)S(1)}, bf16[1056,128]{1,0:T(8,128)(2,1)S(1)}, u32[]{:S(2)}, u32[]{:S(2)}) %collective-permute-start.12) | collective-permute-done | bytes 270368 | tf_op jit(solution)/shard_map/ppermute | solution.py:38
  81.1 5.8 %collective-permute-done.13.refs_1_ = bf16[1056,128]{1,0:T(8,128)(2,1)S(1)} collective-permute-done((bf16[1056,128]{1,0:T(8,128)(2,1)S(1)}, bf16[1056,128]{1,0:T(8,128)(2,1)S(1)}, u32[]{:S(2)}, u32[]{:S(2)}) %collective-permute-start.13) | collective-permute-done | bytes 270368 | tf_op jit(solution)/shard_map/ppermute | solution.py:38
  86.8 0.1 collective-permute-done.14.refs_2_
  86.9 1.4 %finish.1 = f32[128,2048]{1,0:T(8,128)} custom-call(s32[1]{0:T(128)} %bitcast.id_ref, f32[1024,128]{1,0:T(8,128)S(1)} %get-tuple-element.68.keep_ref, f32[8,128]{1,0:T(8,128)S(1)} %get-tuple-element.69.refs_3_.cnt_ref, bf16[1056,128]{1,0:T(8,128)(2,1)S(1)} %collective-permute-done.12.refs_0_, bf16[1056,128]{1,0:T(8,128)(2,1)S(1)} %collective-permute-done.13.refs_1_, ...), custom_call_target="tpu_custom_call" | custom-call | tf_op jit(solution)/shard_map/finish/pallas_call | solution.py:334
  (15 shorter events, 0.1 us)
Async XLA Ops:
  0.0 16.3 %collective-permute-start.3 = (bf16[2048,1024]{1,0:T(8,128)(2,1)}, bf16[2048,1024]{1,0:T(8,128)(2,1)S(1)}, u32[]{:S(2)}, u32[]{:S(2)}) collective-permute-start(bf16[2048,1024]{1,0:T(8,128)(2,1)} %refs_4_.1), channel_id=1, source_target_pairs={{0,1},{1,0},{2,3},{3,2},{4,5},{5,4},{6,7},{7,6},{8,9},{9,8},{10,11... | collective-permute-start | bytes 12582920 | tf_op jit(solution)/shard_map/ppermute | solution.py:38
  1.4 7.8 %collective-permute-start = (bf16[128,1024]{1,0:T(8,128)(2,1)}, bf16[128,1024]{1,0:T(8,128)(2,1)S(1)}, u32[]{:S(2)}, u32[]{:S(2)}) collective-permute-start(bf16[128,1024]{1,0:T(8,128)(2,1)} %refs_0_.1), channel_id=1, source_target_pairs={{0,2},{1,9},{2,4},{3,11},{4,6},{5,13},{6,0},{7,15},{8,10},{9,65},{... | collective-permute-start | bytes 786440 | tf_op jit(solution)/shard_map/ppermute | solution.py:38
  2.7 7.9 %collective-permute-start.2 = (bf16[128,1024]{1,0:T(8,128)(2,1)}, bf16[128,1024]{1,0:T(8,128)(2,1)S(1)}, u32[]{:S(2)}, u32[]{:S(2)}) collective-permute-start(bf16[128,1024]{1,0:T(8,128)(2,1)} %refs_0_.1), channel_id=1, source_target_pairs={{0,6},{1,73},{2,0},{3,75},{4,2},{5,77},{6,4},{7,79},{8,14},{9,1},{... | collective-permute-start | bytes 786440 | tf_op jit(solution)/shard_map/ppermute | solution.py:38
  4.1 8.1 %collective-permute-start.1 = (bf16[128,1024]{1,0:T(8,128)(2,1)}, bf16[128,1024]{1,0:T(8,128)(2,1)S(1)}, u32[]{:S(2)}, u32[]{:S(2)}) collective-permute-start(bf16[128,1024]{1,0:T(8,128)(2,1)} %refs_0_.1), channel_id=1, source_target_pairs={{0,4},{1,65},{2,6},{3,67},{4,0},{5,69},{6,2},{7,71},{8,12},{9,73},... | collective-permute-start | bytes 786440 | tf_op jit(solution)/shard_map/ppermute | solution.py:38
  5.7 2.2 %copy-start = (bf16[2048,1024]{1,0:T(8,128)(2,1)S(1)}, bf16[2048,1024]{1,0:T(8,128)(2,1)}, u32[]{:S(2)}) copy-start(bf16[2048,1024]{1,0:T(8,128)(2,1)} %refs_4_.1) | copy-start | bytes 12582916
  7.9 1.3 %copy-start.2 = (bf16[128,1024]{1,0:T(8,128)(2,1)S(1)}, bf16[128,1024]{1,0:T(8,128)(2,1)}, u32[]{:S(2)}) copy-start(bf16[128,1024]{1,0:T(8,128)(2,1)} %refs_0_.1) | copy-start | bytes 786436
  9.3 9.7 %collective-permute-start.4 = (bf16[256,1024]{1,0:T(8,128)(2,1)S(1)}, bf16[256,1024]{1,0:T(8,128)(2,1)S(1)}, u32[]{:S(2)}, u32[]{:S(2)}) collective-permute-start(bf16[256,1024]{1,0:T(8,128)(2,1)S(1)} %join.2.refs_0_), channel_id=1, source_target_pairs={{0,8},{1,3},{2,10},{3,5},{4,12},{5,7},{6,14},{7,1},{8,64},{9,11},{... | collective-permute-start | bytes 1572872 | tf_op jit(solution)/shard_map/ppermute | solution.py:38
  12.3 10.1 %collective-permute-start.5 = (bf16[256,1024]{1,0:T(8,128)(2,1)S(1)}, bf16[256,1024]{1,0:T(8,128)(2,1)S(1)}, u32[]{:S(2)}, u32[]{:S(2)}) collective-permute-start(bf16[256,1024]{1,0:T(8,128)(2,1)S(1)} %join.3.refs_1_), channel_id=1, source_target_pairs={{0,72},{1,7},{2,74},{3,1},{4,76},{5,3},{6,78},{7,5},{8,0},{9,15},{... | collective-permute-start | bytes 1572872 | tf_op jit(solution)/shard_map/ppermute | solution.py:38
  14.8 14.0 %collective-permute-start.7 = (bf16[256,1024]{1,0:T(8,128)(2,1)S(1)}, bf16[256,1024]{1,0:T(8,128)(2,1)S(1)}, u32[]{:S(2)}, u32[]{:S(2)}) collective-permute-start(bf16[256,1024]{1,0:T(8,128)(2,1)S(1)} %join.2.refs_0_), channel_id=1, source_target_pairs={{0,72},{1,7},{2,74},{3,1},{4,76},{5,3},{6,78},{7,5},{8,0},{9,15},{... | collective-permute-start | bytes 1572872 | tf_op jit(solution)/shard_map/ppermute | solution.py:38
  15.2 13.5 %collective-permute-start.6 = (bf16[256,1024]{1,0:T(8,128)(2,1)S(1)}, bf16[256,1024]{1,0:T(8,128)(2,1)S(1)}, u32[]{:S(2)}, u32[]{:S(2)}) collective-permute-start(bf16[256,1024]{1,0:T(8,128)(2,1)S(1)} %join.3.refs_1_), channel_id=1, source_target_pairs={{0,8},{1,3},{2,10},{3,5},{4,12},{5,7},{6,14},{7,1},{8,64},{9,11},{... | collective-permute-start | bytes 1572872 | tf_op jit(solution)/shard_map/ppermute | solution.py:38
  18.9 13.3 %collective-permute-start.8 = (bf16[256,1024]{1,0:T(8,128)(2,1)S(1)}, bf16[256,1024]{1,0:T(8,128)(2,1)S(1)}, u32[]{:S(2)}, u32[]{:S(2)}) collective-permute-start(bf16[256,1024]{1,0:T(8,128)(2,1)S(1)} %collective-permute-done.4.refs_0_), channel_id=1, source_target_pairs={{0,8},{1,3},{2,10},{3,5},{4,12},{5,7},{6,14},{7,1},{8,64},{9,11},{... | collective-permute-start | bytes 1572872 | tf_op jit(solution)/shard_map/ppermute | solution.py:38
  22.4 9.8 %collective-permute-start.9 = (bf16[256,1024]{1,0:T(8,128)(2,1)S(1)}, bf16[256,1024]{1,0:T(8,128)(2,1)S(1)}, u32[]{:S(2)}, u32[]{:S(2)}) collective-permute-start(bf16[256,1024]{1,0:T(8,128)(2,1)S(1)} %collective-permute-done.5.refs_1_), channel_id=1, source_target_pairs={{0,72},{1,7},{2,74},{3,1},{4,76},{5,3},{6,78},{7,5},{8,0},{9,15},{... | collective-permute-start | bytes 1572872 | tf_op jit(solution)/shard_map/ppermute | solution.py:38
  52.1 6.3 %collective-permute-start.10 = (bf16[4,1056,128]{2,1,0:T(8,128)(2,1)S(1)}, bf16[4,1056,128]{2,1,0:T(8,128)(2,1)S(1)}, u32[]{:S(2)}, u32[]{:S(2)}) collective-permute-start(bf16[4,1056,128]{2,1,0:T(8,128)(2,1)S(1)} %sums_sib.2), channel_id=1, source_target_pairs={{0,1},{1,0},{2,3},{3,2},{4,5},{5,4},{6,7},{7,6},{8,9},{9,8},{10,11... | collective-permute-start | bytes 3244040 | tf_op jit(solution)/shard_map/ppermute | solution.py:38
  58.6 13.3 %collective-permute-start.15 = (bf16[1056,128]{1,0:T(8,128)(2,1)S(1)}, bf16[1056,128]{1,0:T(8,128)(2,1)S(1)}, u32[]{:S(2)}, u32[]{:S(2)}) collective-permute-start(bf16[1056,128]{1,0:T(8,128)(2,1)S(1)} %get-tuple-element.74), channel_id=1, source_target_pairs={{0,32},{1,33},{2,34},{3,35},{4,36},{5,37},{6,38},{7,39},{8,40},{9,... | collective-permute-start | bytes 811016 | tf_op jit(solution)/shard_map/ppermute | solution.py:38
  62.2 12.7 %collective-permute-start.16 = (bf16[1056,128]{1,0:T(8,128)(2,1)S(1)}, bf16[1056,128]{1,0:T(8,128)(2,1)S(1)}, u32[]{:S(2)}, u32[]{:S(2)}) collective-permute-start(bf16[1056,128]{1,0:T(8,128)(2,1)S(1)} %get-tuple-element.75), channel_id=1, source_target_pairs={{0,16},{1,17},{2,18},{3,19},{4,20},{5,21},{6,22},{7,23},{8,24},{9,... | collective-permute-start | bytes 811016 | tf_op jit(solution)/shard_map/ppermute | solution.py:38
  63.0 12.3 %collective-permute-start.17 = (bf16[1056,128]{1,0:T(8,128)(2,1)S(1)}, bf16[1056,128]{1,0:T(8,128)(2,1)S(1)}, u32[]{:S(2)}, u32[]{:S(2)}) collective-permute-start(bf16[1056,128]{1,0:T(8,128)(2,1)S(1)} %get-tuple-element.76), channel_id=1, source_target_pairs={{0,48},{1,49},{2,50},{3,51},{4,52},{5,53},{6,54},{7,55},{8,56},{9,... | collective-permute-start | bytes 811016 | tf_op jit(solution)/shard_map/ppermute | solution.py:38
  67.6 3.6 %collective-permute-start.11 = (bf16[4,1056,128]{2,1,0:T(8,128)(2,1)S(1)}, bf16[4,1056,128]{2,1,0:T(8,128)(2,1)S(1)}, u32[]{:S(2)}, u32[]{:S(2)}) collective-permute-start(bf16[4,1056,128]{2,1,0:T(8,128)(2,1)S(1)} %sums_sib.3), channel_id=1, source_target_pairs={{0,1},{1,0},{2,3},{3,2},{4,5},{5,4},{6,7},{7,6},{8,9},{9,8},{10,11... | collective-permute-start | bytes 3244040 | tf_op jit(solution)/shard_map/ppermute | solution.py:38
  71.2 15.7 %copy-start.1 = (bf16[2048,1024]{1,0:T(8,128)(2,1)S(1)}, bf16[2048,1024]{1,0:T(8,128)(2,1)}, u32[]{:S(2)}) copy-start(bf16[2048,1024]{1,0:T(8,128)(2,1)} %refs_4_.1) | copy-start | bytes 12582916
  71.5 9.6 %collective-permute-start.12 = (bf16[1056,128]{1,0:T(8,128)(2,1)S(1)}, bf16[1056,128]{1,0:T(8,128)(2,1)S(1)}, u32[]{:S(2)}, u32[]{:S(2)}) collective-permute-start(bf16[1056,128]{1,0:T(8,128)(2,1)S(1)} %get-tuple-element.70), channel_id=1, source_target_pairs={{0,32},{1,33},{2,34},{3,35},{4,36},{5,37},{6,38},{7,39},{8,40},{9,... | collective-permute-start | bytes 811016 | tf_op jit(solution)/shard_map/ppermute | solution.py:38
  71.6 15.3 %collective-permute-start.13 = (bf16[1056,128]{1,0:T(8,128)(2,1)S(1)}, bf16[1056,128]{1,0:T(8,128)(2,1)S(1)}, u32[]{:S(2)}, u32[]{:S(2)}) collective-permute-start(bf16[1056,128]{1,0:T(8,128)(2,1)S(1)} %get-tuple-element.71), channel_id=1, source_target_pairs={{0,16},{1,17},{2,18},{3,19},{4,20},{5,21},{6,22},{7,23},{8,24},{9,... | collective-permute-start | bytes 811016 | tf_op jit(solution)/shard_map/ppermute | solution.py:38
  71.9 15.1 %collective-permute-start.14 = (bf16[1056,128]{1,0:T(8,128)(2,1)S(1)}, bf16[1056,128]{1,0:T(8,128)(2,1)S(1)}, u32[]{:S(2)}, u32[]{:S(2)}) collective-permute-start(bf16[1056,128]{1,0:T(8,128)(2,1)S(1)} %get-tuple-element.72), channel_id=1, source_target_pairs={{0,48},{1,49},{2,50},{3,51},{4,52},{5,53},{6,54},{7,55},{8,56},{9,... | collective-permute-start | bytes 811016 | tf_op jit(solution)/shard_map/ppermute | solution.py:38
  75.4 11.5 %collective-permute-start.18 = (bf16[1056,128]{1,0:T(8,128)(2,1)S(1)}, bf16[1056,128]{1,0:T(8,128)(2,1)S(1)}, u32[]{:S(2)}, u32[]{:S(2)}) collective-permute-start(bf16[1056,128]{1,0:T(8,128)(2,1)S(1)} %far_sum.1), channel_id=1, source_target_pairs={{0,64},{1,65},{2,66},{3,67},{4,68},{5,69},{6,70},{7,71},{8,72},{9,... | collective-permute-start | bytes 811016 | tf_op jit(solution)/shard_map/ppermute | solution.py:38

commit v6 on v5

--- a/solution.py
+++ b/solution.py
@@ -203,15 +203,17 @@
     w_refs, x_refs, sc_ref = refs[:n_arr], refs[n_arr : 2 * n_arr], refs[2 * n_arr]
     packed = half == 1
     out_ref, cnt_ref = refs[-2:]
-    k, r = w_refs[0].shape[1:]
+    k = w_refs[0].shape[1]
     kb = 256
     per = kb // 128
     cols = slice(group * NZ * 128, (group + 1) * NZ * 128)
     for j in range(k // kb):
         rows = slice(j * kb, (j + 1) * kb)
-        acc, lanes = None, None
+        acc, lanes, pos = None, None, 0
         for a in range(n_arr):
-            sc = sc_ref[half : half + 1, a * r : (a + 1) * r]
+            r = w_refs[a].shape[2]
+            sc = sc_ref[half : half + 1, pos : pos + r]
+            pos += r
             w = (w_refs[a][half, rows, :].astype(F32) * sc).astype(BF16)
             wf = w.astype(F32)
             for t in range(r // 128):
@@ -345,7 +347,7 @@
     place = {}
     for a in range(4):
         place[0, a] = (0, a * 128)
-        place[2, a] = (3, a * 128)
+        place[2, a] = (3 + a // 2, (a % 2) * 128)
         place[1, a] = (1 if a < 2 else 2, (a % 2) * 128)
         place[3, a] = (1 if a >= 2 else 2, 256 + (a % 2) * 128)
     return [place[b, a] for b in range(4) for a in range(4)]
@@ -372,7 +374,7 @@
 
 
 def _pack_kernel(gain, id_ref, *refs):
-    stats, o_ref, t_ref = refs[:4], refs[-2], refs[-1]
+    stats, o_ref, t_ref = refs[:-2], refs[-2], refs[-1]
     pairs = [(_gather_slots(stats, 2 * b), _gather_slots(stats, 2 * b + 1)) for b in range(2)]
     m, s = _merge(pairs, gain)
     for i, n in enumerate(_absolute(id_ref)):
@@ -384,18 +386,19 @@
 
 
 def _scale_kernel(gain, id_ref, all_ref, *refs):
-    stats, o_ref, t_ref = refs[:4], refs[-2], refs[-1]
+    stats, o_ref, t_ref = refs[:-2], refs[-2], refs[-1]
     top, total = _merge([(all_ref[j, 0], all_ref[j, 1]) for j in range(all_ref.shape[0])], gain)
     t_ref[0], t_ref[1] = top, total
     order = _absolute(id_ref)
     top, total = [
         jnp.concatenate([t_ref[q, pl.ds(n, 1), :] for n in order], axis=0) for q in range(2)
     ]
-    r = stats[0].shape[1]
+    base = [sum(st.shape[1] for st in stats[:n]) for n in range(len(stats))]
     for b in range(2):
         q = jnp.exp2((_gather_slots(stats, 2 * b) - top) * gain) / total
         for i, (n, off) in enumerate(_slots()):
-            o_ref[b : b + 1, n * r + off : n * r + off + 128] = q[i : i + 1, :]
+            lane = base[n] + off
+            o_ref[b : b + 1, lane : lane + 128] = q[i : i + 1, :]
 
 
 def _statistics(kernel, shape, ident, args, name):
@@ -451,7 +454,8 @@
     far_b = send_second(down_b, 3)
     run(up_a, down_b)
     run(up_b, down_a)
-    run(far_a, far_b)
+    run(far_a)
+    run(far_b)
 
     shape = (NX * NY, 2, 16, 128)
     packs = _statistics(functools.partial(_pack_kernel, gain), shape, ident, stats, "stats_pack")

time: 88.5 us -> 86.8 us (0.981)
  blocking collectives: 13.6 us -> 11.8 us
    all_to_all x1, blocking collectives: 13.6 us -> 11.8 us  [local(): lax.all_to_all(packs, AXES, 0, 0, tiled=True, axis_index_groups=_plane_gr...]
    pallas_call x4 -> x5, Pallas kernels: 13.7 us -> 13.9 us  [score(): pl.pallas_call(functools.partial(_score_kernel, gain, len(xs)), out_shape...]
  transfers between devices with their start and end apart: 19 -> 19, of which waited for: 7 -> 7; matrix products, arithmetic and copies ran while one was open for 0% -> 0% of each run, Pallas kernels for 24% -> 26%
where the time goes in v6:
time: 86.8 us; the launch traced here: 86.6 us
  starting transfers between devices  29.1 us (34%)
  Pallas kernels  28.9 us (33%)
  waiting for transfers between devices  14.4 us (17%)
  blocking collectives  11.8 us (14%)
  local copies, waits for them, and re-layouts  2.2 us (3%)
    ppermute x19, starting transfers between devices, _send(): return lax.ppermute(a, AXES, pairs)  29.1 us
    ppermute x19, waiting for transfers between devices, _send(): return lax.ppermute(a, AXES, pairs)  14.4 us
    pallas_call x5, Pallas kernels, score(): pl.pallas_call(functools.partial(_score_kernel, gain, len(xs)), out_shape...  13.9 us
    all_to_all x1, blocking collectives, local(): lax.all_to_all(packs, AXES, 0, 0, tiled=True, axis_index_groups=_plane_gr...  11.8 us
    pallas_call x4, Pallas kernels, weighted_sums(): pl.pallas_call(functools.partial(_sum_kernel, half, group, n_arr), out_sh...  10.3 us
    pallas_call x2, Pallas kernels, load_half(): pl.pallas_call(_load_kernel, out_shape=(jax.ShapeDtypeStruct((k, d), BF16...  2.55 us
    unnamed x6, local copies, waits for them, and re-layouts  2.2 us
  transfers between devices with their start and end apart: 19, of which 7 were waited for; matrix products, arithmetic and copies ran while one was open for 0% of the time, Pallas kernels for 26%

profile of v6, /device:TPU:1, one launch (start us, length us, event | category | flops | bytes accessed | tf_op | source)
XLA Modules:
  0.0 86.6 jit_solution(13443795486534284029)
XLA Ops:
  0.0 1.4 %collective-permute-start.3 = (bf16[2048,1024]{1,0:T(8,128)(2,1)}, bf16[2048,1024]{1,0:T(8,128)(2,1)S(1)}, u32[]{:S(2)}, u32[]{:S(2)}) collective-permute-start(bf16[2048,1024]{1,0:T(8,128)(2,1)} %refs_4_.1), channel_id=1, source_target_pairs={{0,1},{1,0},{2,3},{3,2},{4,5},{5,4},{6,7},{7,6},{8,9},{9,8},{10,11... | collective-permute-start | bytes 12582920 | tf_op jit(solution)/shard_map/ppermute | solution.py:38
  1.4 1.3 %collective-permute-start = (bf16[128,1024]{1,0:T(8,128)(2,1)}, bf16[128,1024]{1,0:T(8,128)(2,1)S(1)}, u32[]{:S(2)}, u32[]{:S(2)}) collective-permute-start(bf16[128,1024]{1,0:T(8,128)(2,1)} %refs_0_.1), channel_id=1, source_target_pairs={{0,2},{1,9},{2,4},{3,11},{4,6},{5,13},{6,0},{7,15},{8,10},{9,65},{... | collective-permute-start | bytes 786440 | tf_op jit(solution)/shard_map/ppermute | solution.py:38
  2.7 1.4 %collective-permute-start.2 = (bf16[128,1024]{1,0:T(8,128)(2,1)}, bf16[128,1024]{1,0:T(8,128)(2,1)S(1)}, u32[]{:S(2)}, u32[]{:S(2)}) collective-permute-start(bf16[128,1024]{1,0:T(8,128)(2,1)} %refs_0_.1), channel_id=1, source_target_pairs={{0,6},{1,73},{2,0},{3,75},{4,2},{5,77},{6,4},{7,79},{8,14},{9,1},{... | collective-permute-start | bytes 786440 | tf_op jit(solution)/shard_map/ppermute | solution.py:38
  4.1 1.6 %collective-permute-start.1 = (bf16[128,1024]{1,0:T(8,128)(2,1)}, bf16[128,1024]{1,0:T(8,128)(2,1)S(1)}, u32[]{:S(2)}, u32[]{:S(2)}) collective-permute-start(bf16[128,1024]{1,0:T(8,128)(2,1)} %refs_0_.1), channel_id=1, source_target_pairs={{0,4},{1,65},{2,6},{3,67},{4,0},{5,69},{6,2},{7,71},{8,12},{9,73},... | collective-permute-start | bytes 786440 | tf_op jit(solution)/shard_map/ppermute | solution.py:38
  5.7 2.2 %copy-done = bf16[2048,1024]{1,0:T(8,128)(2,1)S(1)} copy-done((bf16[2048,1024]{1,0:T(8,128)(2,1)S(1)}, bf16[2048,1024]{1,0:T(8,128)(2,1)}, u32[]{:S(2)}) %copy-start) | copy-done | bytes 4194328
  7.9 1.3 %load_half.2 = (bf16[1024,1024]{1,0:T(8,128)(2,1)S(1)}, f32[1024,128]{1,0:T(8,128)S(1)}) custom-call(s32[1]{0:T(128)} %bitcast.id_ref, bf16[2048,1024]{1,0:T(8,128)(2,1)S(1)} %copy-done), custom_call_target="tpu_custom_call" | custom-call | flops 1024 | bytes 1024 | tf_op jit(solution)/shard_map/load_half/pallas_call | solution.py:86
  9.2 0.0 collective-permute-done.refs_1_
  9.3 1.4 %collective-permute-start.4 = (bf16[256,1024]{1,0:T(8,128)(2,1)S(1)}, bf16[256,1024]{1,0:T(8,128)(2,1)S(1)}, u32[]{:S(2)}, u32[]{:S(2)}) collective-permute-start(bf16[256,1024]{1,0:T(8,128)(2,1)S(1)} %join.2.refs_0_), channel_id=1, source_target_pairs={{0,8},{1,3},{2,10},{3,5},{4,12},{5,7},{6,14},{7,1},{8,64},{9,11},{... | collective-permute-start | bytes 1572872 | tf_op jit(solution)/shard_map/ppermute | solution.py:38
  10.6 0.0 collective-permute-done.2.refs_1_
  10.6 1.6 %collective-permute-done.1.refs_0_ = bf16[128,1024]{1,0:T(8,128)(2,1)S(1)} collective-permute-done((bf16[128,1024]{1,0:T(8,128)(2,1)}, bf16[128,1024]{1,0:T(8,128)(2,1)S(1)}, u32[]{:S(2)}, u32[]{:S(2)}) %collective-permute-start.1) | collective-permute-done | bytes 262176 | tf_op jit(solution)/shard_map/ppermute | solution.py:38
  12.3 2.5 %collective-permute-start.5 = (bf16[256,1024]{1,0:T(8,128)(2,1)S(1)}, bf16[256,1024]{1,0:T(8,128)(2,1)S(1)}, u32[]{:S(2)}, u32[]{:S(2)}) collective-permute-start(bf16[256,1024]{1,0:T(8,128)(2,1)S(1)} %join.3.refs_1_), channel_id=1, source_target_pairs={{0,72},{1,7},{2,74},{3,1},{4,76},{5,3},{6,78},{7,5},{8,0},{9,15},{... | collective-permute-start | bytes 1572872 | tf_op jit(solution)/shard_map/ppermute | solution.py:38
  14.8 0.5 collective-permute-start.7
  15.2 1.0 %collective-permute-start.6 = (bf16[256,1024]{1,0:T(8,128)(2,1)S(1)}, bf16[256,1024]{1,0:T(8,128)(2,1)S(1)}, u32[]{:S(2)}, u32[]{:S(2)}) collective-permute-start(bf16[256,1024]{1,0:T(8,128)(2,1)S(1)} %join.3.refs_1_), channel_id=1, source_target_pairs={{0,8},{1,3},{2,10},{3,5},{4,12},{5,7},{6,14},{7,1},{8,64},{9,11},{... | collective-permute-start | bytes 1572872 | tf_op jit(solution)/shard_map/ppermute | solution.py:38
  16.3 1.3 %load_half.3 = (bf16[1024,1024]{1,0:T(8,128)(2,1)S(1)}, f32[1024,128]{1,0:T(8,128)S(1)}) custom-call(s32[1]{0:T(128)} %bitcast.id_ref, bf16[2048,1024]{1,0:T(8,128)(2,1)S(1)} %collective-permute-done.3.c_ref), custom_call_target="tpu_custom_call" | custom-call | flops 1024 | bytes 1024 | tf_op jit(solution)/shard_map/load_half/pallas_call | solution.py:86
  17.5 1.4 %collective-permute-done.4.refs_0_ = bf16[256,1024]{1,0:T(8,128)(2,1)S(1)} collective-permute-done((bf16[256,1024]{1,0:T(8,128)(2,1)S(1)}, bf16[256,1024]{1,0:T(8,128)(2,1)S(1)}, u32[]{:S(2)}, u32[]{:S(2)}) %collective-permute-start.4) | collective-permute-done | bytes 524320 | tf_op jit(solution)/shard_map/ppermute | solution.py:38
  18.9 0.0 collective-permute-start.8
  18.9 3.4 %score.5 = (bf16[2,1024,512]{2,1,0:T(8,128)(2,1)S(1)}, f32[8,512]{1,0:T(8,128)S(1)}, bf16[512,1024]{1,0:T(8,128)(2,1)S(1)}) custom-call(s32[1]{0:T(128)} %bitcast.id_ref, bf16[256,1024]{1,0:T(8,128)(2,1)S(1)} %join.2.refs_0_, bf16[256,1024]{1,0:T(8,128)(2,1)S(1)} %join.3.refs_1_, bf16[1024,1024]{1,0:T(8,128)(2,1)S(1)} %get-tuple-element.46.refs_2_.refs_1_, ...), custom_call_target="tpu_custom_call" | custom-call | flops 1024 | bytes 1024 | tf_op jit(solution)/shard_map/score/pallas_call | solution.py:186
  22.4 2.9 %collective-permute-start.9 = (bf16[256,1024]{1,0:T(8,128)(2,1)S(1)}, bf16[256,1024]{1,0:T(8,128)(2,1)S(1)}, u32[]{:S(2)}, u32[]{:S(2)}) collective-permute-start(bf16[256,1024]{1,0:T(8,128)(2,1)S(1)} %collective-permute-done.5.refs_1_), channel_id=1, source_target_pairs={{0,72},{1,7},{2,74},{3,1},{4,76},{5,3},{6,78},{7,5},{8,0},{9,15},{... | collective-permute-start | bytes 1572872 | tf_op jit(solution)/shard_map/ppermute | solution.py:38
  25.3 3.4 %score.6 = (bf16[2,1024,512]{2,1,0:T(8,128)(2,1)S(1)}, f32[8,512]{1,0:T(8,128)S(1)}, bf16[512,1024]{1,0:T(8,128)(2,1)S(1)}) custom-call(s32[1]{0:T(128)} %bitcast.id_ref, bf16[256,1024]{1,0:T(8,128)(2,1)S(1)} %collective-permute-done.4.refs_0_, bf16[256,1024]{1,0:T(8,128)(2,1)S(1)} %collective-permute-done.5.refs_1_, ...), custom_call_target="tpu_custom_call" | custom-call | flops 1024 | bytes 1024 | tf_op jit(solution)/shard_map/score/pallas_call | solution.py:186
  28.8 3.4 %score.7 = (bf16[2,1024,512]{2,1,0:T(8,128)(2,1)S(1)}, f32[8,512]{1,0:T(8,128)S(1)}, bf16[512,1024]{1,0:T(8,128)(2,1)S(1)}) custom-call(s32[1]{0:T(128)} %bitcast.id_ref, bf16[256,1024]{1,0:T(8,128)(2,1)S(1)} %collective-permute-done.6.refs_0_, bf16[256,1024]{1,0:T(8,128)(2,1)S(1)} %collective-permute-done.7.refs_1_, ...), custom_call_target="tpu_custom_call" | custom-call | flops 1024 | bytes 1024 | tf_op jit(solution)/shard_map/score/pallas_call | solution.py:186
  32.2 1.8 %score.8 = (bf16[2,1024,256]{2,1,0:T(8,128)(2,1)S(1)}, f32[8,256]{1,0:T(8,128)S(1)}, bf16[256,1024]{1,0:T(8,128)(2,1)S(1)}) custom-call(s32[1]{0:T(128)} %bitcast.id_ref, bf16[256,1024]{1,0:T(8,128)(2,1)S(1)} %collective-permute-done.8.refs_0_, bf16[1024,1024]{1,0:T(8,128)(2,1)S(1)} %get-tuple-element.46.refs_2_.refs_1_, ...), custom_call_target="tpu_custom_call" | custom-call | flops 1024 | bytes 1024 | tf_op jit(solution)/shard_map/score/pallas_call | solution.py:186
  34.0 1.8 %score.9 = (bf16[2,1024,256]{2,1,0:T(8,128)(2,1)S(1)}, f32[8,256]{1,0:T(8,128)S(1)}, bf16[256,1024]{1,0:T(8,128)(2,1)S(1)}) custom-call(s32[1]{0:T(128)} %bitcast.id_ref, bf16[256,1024]{1,0:T(8,128)(2,1)S(1)} %collective-permute-done.9.refs_0_, bf16[1024,1024]{1,0:T(8,128)(2,1)S(1)} %get-tuple-element.46.refs_2_.refs_1_, ...), custom_call_target="tpu_custom_call" | custom-call | flops 1024 | bytes 1024 | tf_op jit(solution)/shard_map/score/pallas_call | solution.py:186
  35.8 0.1 stats_pack.1
  35.9 11.8 %all_to_all.5.all_ref = f32[16,2,16,128]{3,2,1,0:T(8,128)S(1)} all-to-all(f32[16,2,16,128]{3,2,1,0:T(8,128)S(1)} %stats_pack.1), channel_id=1, replica_groups={{0,2,4,6,8,10,12,14,64,66,68,70,72,74,76,78},{1,3,5,7,9,11,13,15,65,67,..., dimensions={0} | all-to-all | bytes 524288 | tf_op jit(solution)/shard_map/all_to_all | solution.py:462
  47.8 0.1 stats_scale.1.refs_10_
  47.9 2.6 %sums_sib.2 = bf16[4,1056,128]{2,1,0:T(8,128)(2,1)S(1)} custom-call(bf16[2,1024,512]{2,1,0:T(8,128)(2,1)S(1)} %get-tuple-element.51.refs_0_, bf16[2,1024,512]{2,1,0:T(8,128)(2,1)S(1)} %get-tuple-element.56.refs_1_, bf16[2,1024,512]{2,1,0:T(8,128)(2,1)S(1)} %get-tuple-element.58.refs_2_, bf16[2,1024,256]{2,1,0:T(8,128)(2,1)S(1)} %get-tuple-element.60.refs_3_, ...), custom_call_target="tpu_custom_call" | custom-call | flops 1024 | bytes 1024 | tf_op jit(solution)/shard_map/sums_sib/pallas_call | solution.py:259
  50.5 3.7 %collective-permute-start.10 = (bf16[4,1056,128]{2,1,0:T(8,128)(2,1)S(1)}, bf16[4,1056,128]{2,1,0:T(8,128)(2,1)S(1)}, u32[]{:S(2)}, u32[]{:S(2)}) collective-permute-start(bf16[4,1056,128]{2,1,0:T(8,128)(2,1)S(1)} %sums_sib.2), channel_id=1, source_target_pairs={{0,1},{1,0},{2,3},{3,2},{4,5},{5,4},{6,7},{7,6},{8,9},{9,8},{10,11... | collective-permute-start | bytes 3244040 | tf_op jit(solution)/shard_map/ppermute | solution.py:38
  54.2 2.5 %sums_own.2 = (f32[4,1024,128]{2,1,0:T(8,128)S(1)}, f32[8,128]{1,0:T(8,128)S(1)}) custom-call(bf16[2,1024,512]{2,1,0:T(8,128)(2,1)S(1)} %get-tuple-element.51.refs_0_, bf16[2,1024,512]{2,1,0:T(8,128)(2,1)S(1)} %get-tuple-element.56.refs_1_, bf16[2,1024,512]{2,1,0:T(8,128)(2,1)S(1)} %get-tuple-element.58.refs_2_, ...), custom_call_target="tpu_custom_call" | custom-call | flops 42949672960 | bytes 1024 | tf_op jit(solution)/shard_map/sums_own/pallas_call | solution.py:259
  56.7 0.2 mix.2
  56.9 3.7 %collective-permute-start.15 = (bf16[1056,128]{1,0:T(8,128)(2,1)S(1)}, bf16[1056,128]{1,0:T(8,128)(2,1)S(1)}, u32[]{:S(2)}, u32[]{:S(2)}) collective-permute-start(bf16[1056,128]{1,0:T(8,128)(2,1)S(1)} %get-tuple-element.80), channel_id=1, source_target_pairs={{0,32},{1,33},{2,34},{3,35},{4,36},{5,37},{6,38},{7,39},{8,40},{9,... | collective-permute-start | bytes 811016 | tf_op jit(solution)/shard_map/ppermute | solution.py:38
  60.6 0.7 collective-permute-start.16
  61.3 1.9 %collective-permute-start.17 = (bf16[1056,128]{1,0:T(8,128)(2,1)S(1)}, bf16[1056,128]{1,0:T(8,128)(2,1)S(1)}, u32[]{:S(2)}, u32[]{:S(2)}) collective-permute-start(bf16[1056,128]{1,0:T(8,128)(2,1)S(1)} %get-tuple-element.82), channel_id=1, source_target_pairs={{0,48},{1,49},{2,50},{3,51},{4,52},{5,53},{6,54},{7,55},{8,56},{9,... | collective-permute-start | bytes 811016 | tf_op jit(solution)/shard_map/ppermute | solution.py:38
  63.3 2.6 %sums_sib.3 = bf16[4,1056,128]{2,1,0:T(8,128)(2,1)S(1)} custom-call(bf16[2,1024,512]{2,1,0:T(8,128)(2,1)S(1)} %get-tuple-element.51.refs_0_, bf16[2,1024,512]{2,1,0:T(8,128)(2,1)S(1)} %get-tuple-element.56.refs_1_, bf16[2,1024,512]{2,1,0:T(8,128)(2,1)S(1)} %get-tuple-element.58.refs_2_, bf16[2,1024,256]{2,1,0:T(8,128)(2,1)S(1)} %get-tuple-element.60.refs_3_, ...), custom_call_target="tpu_custom_call" | custom-call | flops 1024 | bytes 1024 | tf_op jit(solution)/shard_map/sums_sib/pallas_call | solution.py:259
  65.9 1.1 %collective-permute-start.11 = (bf16[4,1056,128]{2,1,0:T(8,128)(2,1)S(1)}, bf16[4,1056,128]{2,1,0:T(8,128)(2,1)S(1)}, u32[]{:S(2)}, u32[]{:S(2)}) collective-permute-start(bf16[4,1056,128]{2,1,0:T(8,128)(2,1)S(1)} %sums_sib.3), channel_id=1, source_target_pairs={{0,1},{1,0},{2,3},{3,2},{4,5},{5,4},{6,7},{7,6},{8,9},{9,8},{10,11... | collective-permute-start | bytes 3244040 | tf_op jit(solution)/shard_map/ppermute | solution.py:38
  67.0 2.5 %sums_own.3 = (f32[4,1024,128]{2,1,0:T(8,128)S(1)}, f32[8,128]{1,0:T(8,128)S(1)}) custom-call(bf16[2,1024,512]{2,1,0:T(8,128)(2,1)S(1)} %get-tuple-element.51.refs_0_, bf16[2,1024,512]{2,1,0:T(8,128)(2,1)S(1)} %get-tuple-element.56.refs_1_, bf16[2,1024,512]{2,1,0:T(8,128)(2,1)S(1)} %get-tuple-element.58.refs_2_, ...), custom_call_target="tpu_custom_call" | custom-call | flops 42949672960 | bytes 1024 | tf_op jit(solution)/shard_map/sums_own/pallas_call | solution.py:259
  69.5 0.0 copy-start.1
  69.5 0.2 mix.3
  69.7 0.1 collective-permute-start.12
  69.8 0.3 collective-permute-start.13
  70.1 2.5 %collective-permute-start.14 = (bf16[1056,128]{1,0:T(8,128)(2,1)S(1)}, bf16[1056,128]{1,0:T(8,128)(2,1)S(1)}, u32[]{:S(2)}, u32[]{:S(2)}) collective-permute-start(bf16[1056,128]{1,0:T(8,128)(2,1)S(1)} %get-tuple-element.78), channel_id=1, source_target_pairs={{0,48},{1,49},{2,50},{3,51},{4,52},{5,53},{6,54},{7,55},{8,56},{9,... | collective-permute-start | bytes 811016 | tf_op jit(solution)/shard_map/ppermute | solution.py:38
  72.6 0.8 collective-permute-done.16.refs_1_
  73.3 0.3 collective-permute-done.17.refs_2_
  73.6 0.1 far_sum.1
  73.8 1.1 %collective-permute-start.18 = (bf16[1056,128]{1,0:T(8,128)(2,1)S(1)}, bf16[1056,128]{1,0:T(8,128)(2,1)S(1)}, u32[]{:S(2)}, u32[]{:S(2)}) collective-permute-start(bf16[1056,128]{1,0:T(8,128)(2,1)S(1)} %far_sum.1), channel_id=1, source_target_pairs={{0,64},{1,65},{2,66},{3,67},{4,68},{5,69},{6,70},{7,71},{8,72},{9,... | collective-permute-start | bytes 811016 | tf_op jit(solution)/shard_map/ppermute | solution.py:38
  74.9 4.4 %collective-permute-done.12.refs_0_ = bf16[1056,128]{1,0:T(8,128)(2,1)S(1)} collective-permute-done((bf16[1056,128]{1,0:T(8,128)(2,1)S(1)}, bf16[1056,128]{1,0:T(8,128)(2,1)S(1)}, u32[]{:S(2)}, u32[]{:S(2)}) %collective-permute-start.12) | collective-permute-done | bytes 270368 | tf_op jit(solution)/shard_map/ppermute | solution.py:38
  79.3 5.8 %collective-permute-done.13.refs_1_ = bf16[1056,128]{1,0:T(8,128)(2,1)S(1)} collective-permute-done((bf16[1056,128]{1,0:T(8,128)(2,1)S(1)}, bf16[1056,128]{1,0:T(8,128)(2,1)S(1)}, u32[]{:S(2)}, u32[]{:S(2)}) %collective-permute-start.13) | collective-permute-done | bytes 270368 | tf_op jit(solution)/shard_map/ppermute | solution.py:38
  85.1 0.2 collective-permute-done.14.refs_2_
  85.3 1.4 %finish.1 = f32[128,2048]{1,0:T(8,128)} custom-call(s32[1]{0:T(128)} %bitcast.id_ref, f32[1024,128]{1,0:T(8,128)S(1)} %get-tuple-element.74.keep_ref, f32[8,128]{1,0:T(8,128)S(1)} %get-tuple-element.75.refs_3_.cnt_ref, bf16[1056,128]{1,0:T(8,128)(2,1)S(1)} %collective-permute-done.12.refs_0_, bf16[1056,128]{1,0:T(8,128)(2,1)S(1)} %collective-permute-done.13.refs_1_, ...), custom_call_target="tpu_custom_call" | custom-call | tf_op jit(solution)/shard_map/finish/pallas_call | solution.py:336
  (16 shorter events, 0.1 us)
Async XLA Ops:
  0.0 16.3 %collective-permute-start.3 = (bf16[2048,1024]{1,0:T(8,128)(2,1)}, bf16[2048,1024]{1,0:T(8,128)(2,1)S(1)}, u32[]{:S(2)}, u32[]{:S(2)}) collective-permute-start(bf16[2048,1024]{1,0:T(8,128)(2,1)} %refs_4_.1), channel_id=1, source_target_pairs={{0,1},{1,0},{2,3},{3,2},{4,5},{5,4},{6,7},{7,6},{8,9},{9,8},{10,11... | collective-permute-start | bytes 12582920 | tf_op jit(solution)/shard_map/ppermute | solution.py:38
  1.4 7.8 %collective-permute-start = (bf16[128,1024]{1,0:T(8,128)(2,1)}, bf16[128,1024]{1,0:T(8,128)(2,1)S(1)}, u32[]{:S(2)}, u32[]{:S(2)}) collective-permute-start(bf16[128,1024]{1,0:T(8,128)(2,1)} %refs_0_.1), channel_id=1, source_target_pairs={{0,2},{1,9},{2,4},{3,11},{4,6},{5,13},{6,0},{7,15},{8,10},{9,65},{... | collective-permute-start | bytes 786440 | tf_op jit(solution)/shard_map/ppermute | solution.py:38
  2.7 7.9 %collective-permute-start.2 = (bf16[128,1024]{1,0:T(8,128)(2,1)}, bf16[128,1024]{1,0:T(8,128)(2,1)S(1)}, u32[]{:S(2)}, u32[]{:S(2)}) collective-permute-start(bf16[128,1024]{1,0:T(8,128)(2,1)} %refs_0_.1), channel_id=1, source_target_pairs={{0,6},{1,73},{2,0},{3,75},{4,2},{5,77},{6,4},{7,79},{8,14},{9,1},{... | collective-permute-start | bytes 786440 | tf_op jit(solution)/shard_map/ppermute | solution.py:38
  4.1 8.1 %collective-permute-start.1 = (bf16[128,1024]{1,0:T(8,128)(2,1)}, bf16[128,1024]{1,0:T(8,128)(2,1)S(1)}, u32[]{:S(2)}, u32[]{:S(2)}) collective-permute-start(bf16[128,1024]{1,0:T(8,128)(2,1)} %refs_0_.1), channel_id=1, source_target_pairs={{0,4},{1,65},{2,6},{3,67},{4,0},{5,69},{6,2},{7,71},{8,12},{9,73},... | collective-permute-start | bytes 786440 | tf_op jit(solution)/shard_map/ppermute | solution.py:38
  5.7 2.2 %copy-start = (bf16[2048,1024]{1,0:T(8,128)(2,1)S(1)}, bf16[2048,1024]{1,0:T(8,128)(2,1)}, u32[]{:S(2)}) copy-start(bf16[2048,1024]{1,0:T(8,128)(2,1)} %refs_4_.1) | copy-start | bytes 12582916
  7.9 1.3 %copy-start.2 = (bf16[128,1024]{1,0:T(8,128)(2,1)S(1)}, bf16[128,1024]{1,0:T(8,128)(2,1)}, u32[]{:S(2)}) copy-start(bf16[128,1024]{1,0:T(8,128)(2,1)} %refs_0_.1) | copy-start | bytes 786436
  9.3 9.7 %collective-permute-start.4 = (bf16[256,1024]{1,0:T(8,128)(2,1)S(1)}, bf16[256,1024]{1,0:T(8,128)(2,1)S(1)}, u32[]{:S(2)}, u32[]{:S(2)}) collective-permute-start(bf16[256,1024]{1,0:T(8,128)(2,1)S(1)} %join.2.refs_0_), channel_id=1, source_target_pairs={{0,8},{1,3},{2,10},{3,5},{4,12},{5,7},{6,14},{7,1},{8,64},{9,11},{... | collective-permute-start | bytes 1572872 | tf_op jit(solution)/shard_map/ppermute | solution.py:38
  12.3 10.1 %collective-permute-start.5 = (bf16[256,1024]{1,0:T(8,128)(2,1)S(1)}, bf16[256,1024]{1,0:T(8,128)(2,1)S(1)}, u32[]{:S(2)}, u32[]{:S(2)}) collective-permute-start(bf16[256,1024]{1,0:T(8,128)(2,1)S(1)} %join.3.refs_1_), channel_id=1, source_target_pairs={{0,72},{1,7},{2,74},{3,1},{4,76},{5,3},{6,78},{7,5},{8,0},{9,15},{... | collective-permute-start | bytes 1572872 | tf_op jit(solution)/shard_map/ppermute | solution.py:38
  14.8 14.0 %collective-permute-start.7 = (bf16[256,1024]{1,0:T(8,128)(2,1)S(1)}, bf16[256,1024]{1,0:T(8,128)(2,1)S(1)}, u32[]{:S(2)}, u32[]{:S(2)}) collective-permute-start(bf16[256,1024]{1,0:T(8,128)(2,1)S(1)} %join.2.refs_0_), channel_id=1, source_target_pairs={{0,72},{1,7},{2,74},{3,1},{4,76},{5,3},{6,78},{7,5},{8,0},{9,15},{... | collective-permute-start | bytes 1572872 | tf_op jit(solution)/shard_map/ppermute | solution.py:38
  15.2 13.5 %collective-permute-start.6 = (bf16[256,1024]{1,0:T(8,128)(2,1)S(1)}, bf16[256,1024]{1,0:T(8,128)(2,1)S(1)}, u32[]{:S(2)}, u32[]{:S(2)}) collective-permute-start(bf16[256,1024]{1,0:T(8,128)(2,1)S(1)} %join.3.refs_1_), channel_id=1, source_target_pairs={{0,8},{1,3},{2,10},{3,5},{4,12},{5,7},{6,14},{7,1},{8,64},{9,11},{... | collective-permute-start | bytes 1572872 | tf_op jit(solution)/shard_map/ppermute | solution.py:38
  18.9 13.3 %collective-permute-start.8 = (bf16[256,1024]{1,0:T(8,128)(2,1)S(1)}, bf16[256,1024]{1,0:T(8,128)(2,1)S(1)}, u32[]{:S(2)}, u32[]{:S(2)}) collective-permute-start(bf16[256,1024]{1,0:T(8,128)(2,1)S(1)} %collective-permute-done.4.refs_0_), channel_id=1, source_target_pairs={{0,8},{1,3},{2,10},{3,5},{4,12},{5,7},{6,14},{7,1},{8,64},{9,11},{... | collective-permute-start | bytes 1572872 | tf_op jit(solution)/shard_map/ppermute | solution.py:38
  22.4 11.6 %collective-permute-start.9 = (bf16[256,1024]{1,0:T(8,128)(2,1)S(1)}, bf16[256,1024]{1,0:T(8,128)(2,1)S(1)}, u32[]{:S(2)}, u32[]{:S(2)}) collective-permute-start(bf16[256,1024]{1,0:T(8,128)(2,1)S(1)} %collective-permute-done.5.refs_1_), channel_id=1, source_target_pairs={{0,72},{1,7},{2,74},{3,1},{4,76},{5,3},{6,78},{7,5},{8,0},{9,15},{... | collective-permute-start | bytes 1572872 | tf_op jit(solution)/shard_map/ppermute | solution.py:38
  50.5 6.2 %collective-permute-start.10 = (bf16[4,1056,128]{2,1,0:T(8,128)(2,1)S(1)}, bf16[4,1056,128]{2,1,0:T(8,128)(2,1)S(1)}, u32[]{:S(2)}, u32[]{:S(2)}) collective-permute-start(bf16[4,1056,128]{2,1,0:T(8,128)(2,1)S(1)} %sums_sib.2), channel_id=1, source_target_pairs={{0,1},{1,0},{2,3},{3,2},{4,5},{5,4},{6,7},{7,6},{8,9},{9,8},{10,11... | collective-permute-start | bytes 3244040 | tf_op jit(solution)/shard_map/ppermute | solution.py:38
  56.9 13.2 %collective-permute-start.15 = (bf16[1056,128]{1,0:T(8,128)(2,1)S(1)}, bf16[1056,128]{1,0:T(8,128)(2,1)S(1)}, u32[]{:S(2)}, u32[]{:S(2)}) collective-permute-start(bf16[1056,128]{1,0:T(8,128)(2,1)S(1)} %get-tuple-element.80), channel_id=1, source_target_pairs={{0,32},{1,33},{2,34},{3,35},{4,36},{5,37},{6,38},{7,39},{8,40},{9,... | collective-permute-start | bytes 811016 | tf_op jit(solution)/shard_map/ppermute | solution.py:38
  60.6 12.7 %collective-permute-start.16 = (bf16[1056,128]{1,0:T(8,128)(2,1)S(1)}, bf16[1056,128]{1,0:T(8,128)(2,1)S(1)}, u32[]{:S(2)}, u32[]{:S(2)}) collective-permute-start(bf16[1056,128]{1,0:T(8,128)(2,1)S(1)} %get-tuple-element.81), channel_id=1, source_target_pairs={{0,16},{1,17},{2,18},{3,19},{4,20},{5,21},{6,22},{7,23},{8,24},{9,... | collective-permute-start | bytes 811016 | tf_op jit(solution)/shard_map/ppermute | solution.py:38
  61.3 12.3 %collective-permute-start.17 = (bf16[1056,128]{1,0:T(8,128)(2,1)S(1)}, bf16[1056,128]{1,0:T(8,128)(2,1)S(1)}, u32[]{:S(2)}, u32[]{:S(2)}) collective-permute-start(bf16[1056,128]{1,0:T(8,128)(2,1)S(1)} %get-tuple-element.82), channel_id=1, source_target_pairs={{0,48},{1,49},{2,50},{3,51},{4,52},{5,53},{6,54},{7,55},{8,56},{9,... | collective-permute-start | bytes 811016 | tf_op jit(solution)/shard_map/ppermute | solution.py:38
  65.9 3.6 %collective-permute-start.11 = (bf16[4,1056,128]{2,1,0:T(8,128)(2,1)S(1)}, bf16[4,1056,128]{2,1,0:T(8,128)(2,1)S(1)}, u32[]{:S(2)}, u32[]{:S(2)}) collective-permute-start(bf16[4,1056,128]{2,1,0:T(8,128)(2,1)S(1)} %sums_sib.3), channel_id=1, source_target_pairs={{0,1},{1,0},{2,3},{3,2},{4,5},{5,4},{6,7},{7,6},{8,9},{9,8},{10,11... | collective-permute-start | bytes 3244040 | tf_op jit(solution)/shard_map/ppermute | solution.py:38
  69.5 15.7 %copy-start.1 = (bf16[2048,1024]{1,0:T(8,128)(2,1)S(1)}, bf16[2048,1024]{1,0:T(8,128)(2,1)}, u32[]{:S(2)}) copy-start(bf16[2048,1024]{1,0:T(8,128)(2,1)} %refs_4_.1) | copy-start | bytes 12582916
  69.7 9.6 %collective-permute-start.12 = (bf16[1056,128]{1,0:T(8,128)(2,1)S(1)}, bf16[1056,128]{1,0:T(8,128)(2,1)S(1)}, u32[]{:S(2)}, u32[]{:S(2)}) collective-permute-start(bf16[1056,128]{1,0:T(8,128)(2,1)S(1)} %get-tuple-element.76), channel_id=1, source_target_pairs={{0,32},{1,33},{2,34},{3,35},{4,36},{5,37},{6,38},{7,39},{8,40},{9,... | collective-permute-start | bytes 811016 | tf_op jit(solution)/shard_map/ppermute | solution.py:38
  69.8 15.3 %collective-permute-start.13 = (bf16[1056,128]{1,0:T(8,128)(2,1)S(1)}, bf16[1056,128]{1,0:T(8,128)(2,1)S(1)}, u32[]{:S(2)}, u32[]{:S(2)}) collective-permute-start(bf16[1056,128]{1,0:T(8,128)(2,1)S(1)} %get-tuple-element.77), channel_id=1, source_target_pairs={{0,16},{1,17},{2,18},{3,19},{4,20},{5,21},{6,22},{7,23},{8,24},{9,... | collective-permute-start | bytes 811016 | tf_op jit(solution)/shard_map/ppermute | solution.py:38
  70.1 15.2 %collective-permute-start.14 = (bf16[1056,128]{1,0:T(8,128)(2,1)S(1)}, bf16[1056,128]{1,0:T(8,128)(2,1)S(1)}, u32[]{:S(2)}, u32[]{:S(2)}) collective-permute-start(bf16[1056,128]{1,0:T(8,128)(2,1)S(1)} %get-tuple-element.78), channel_id=1, source_target_pairs={{0,48},{1,49},{2,50},{3,51},{4,52},{5,53},{6,54},{7,55},{8,56},{9,... | collective-permute-start | bytes 811016 | tf_op jit(solution)/shard_map/ppermute | solution.py:38
  73.8 11.5 %collective-permute-start.18 = (bf16[1056,128]{1,0:T(8,128)(2,1)S(1)}, bf16[1056,128]{1,0:T(8,128)(2,1)S(1)}, u32[]{:S(2)}, u32[]{:S(2)}) collective-permute-start(bf16[1056,128]{1,0:T(8,128)(2,1)S(1)} %far_sum.1), channel_id=1, source_target_pairs={{0,64},{1,65},{2,66},{3,67},{4,68},{5,69},{6,70},{7,71},{8,72},{9,... | collective-permute-start | bytes 811016 | tf_op jit(solution)/shard_map/ppermute | solution.py:38

commit v7 on v6

--- a/solution.py
+++ b/solution.py
@@ -62,7 +62,7 @@
     return pltpu.CompilerParams(vmem_limit_bytes=mib << 20)
 
 
-def _load_kernel(id_ref, c_ref, half_ref, o_ref, sems):
+def _load_kernel(gain, id_ref, c_ref, half_ref, o_ref, sems):
     k = half_ref.shape[0]
     n = sems.shape[0]
     step = k // n
@@ -77,14 +77,14 @@
         copies[j].wait()
         rows = slice(j * step, (j + 1) * step)
         v = half_ref[rows, :].astype(F32)
-        s = 0.5 * jnp.sum(v * v, axis=1, keepdims=True)
+        s = (0.5 * gain) * jnp.sum(v * v, axis=1, keepdims=True)
         o_ref[rows, :] = jnp.broadcast_to(s, (step, 128))
 
 
-def load_half(ident, cents, mib):
+def load_half(ident, cents, mib, gain):
     k, d = cents.shape[0] // 2, cents.shape[1]
     return pl.pallas_call(
-        _load_kernel,
+        functools.partial(_load_kernel, gain),
         out_shape=(
             jax.ShapeDtypeStruct((k, d), BF16),
             jax.ShapeDtypeStruct((k, 128), F32),
@@ -146,13 +146,13 @@
         u = lax.dot_general(
             c_refs[b][rows, :], x_all_ref[...], (((1,), (1,)), ((), ())), preferred_element_type=F32
         )
-        u = u - jnp.tile(h_refs[b][rows, :], (1, r // 128))
+        u = u * gain - jnp.tile(h_refs[b][rows, :], (1, r // 128))
         u_ref[b, rows, :] = u
         return jnp.max(u, axis=0, keepdims=True)
 
     def weights(b, j, m):
         rows = slice(j * kb, (j + 1) * kb)
-        w = jnp.exp2((u_ref[b, rows, :] - m) * gain)
+        w = jnp.exp2(u_ref[b, rows, :] - m)
         w_ref[b, rows, :] = w.astype(BF16)
         return jnp.sum(w, axis=0, keepdims=True)
 
@@ -361,7 +361,7 @@
 
 def _merge(pairs, gain):
     m = functools.reduce(jnp.maximum, [p[0] for p in pairs])
-    s = sum(p[1] * jnp.exp2((p[0] - m) * gain) for p in pairs)
+    s = sum(p[1] * jnp.exp2(p[0] - m) for p in pairs)
     return m, s
 
 
@@ -395,7 +395,7 @@
     ]
     base = [sum(st.shape[1] for st in stats[:n]) for n in range(len(stats))]
     for b in range(2):
-        q = jnp.exp2((_gather_slots(stats, 2 * b) - top) * gain) / total
+        q = jnp.exp2(_gather_slots(stats, 2 * b) - top) / total
         for i, (n, off) in enumerate(_slots()):
             lane = base[n] + off
             o_ref[b : b + 1, lane : lane + 128] = q[i : i + 1, :]
@@ -430,11 +430,11 @@
     shards = [points] + [send_first(points, d) for d in (1, 2, 3)]
     shard, ident = lax.optimization_barrier((centroids, ident))
     whole = (centroids, send_core(shard))
-    own, own_norm = load_half(ident, whole[0], 4)
+    own, own_norm = load_half(ident, whole[0], 4, gain)
     line_a, line_b = join(shards[0], shards[1], own_norm), join(shards[2], shards[3], own_norm)
     half = line_a.shape[0]
     up_a, down_b = send_second(line_a, 1), send_second(line_b, 3)
-    sib, sib_norm = load_half(ident, whole[1], 4)
+    sib, sib_norm = load_half(ident, whole[1], 4, gain)
     cents = (own, sib)
     up_a, sib_norm = lax.optimization_barrier((up_a, sib_norm))
     far_a = send_second(up_a, 1)

time: 86.8 us -> 86.7 us (level)
  no operation moved by 1% of the time
where the time goes in v7:
time: 86.7 us; the launch traced here: 86.5 us
  starting transfers between devices  29.1 us (34%)
  Pallas kernels  28.2 us (33%)
  waiting for transfers between devices  14.5 us (17%)
  blocking collectives  12.4 us (14%)
  local copies, waits for them, and re-layouts  2.2 us (3%)
    ppermute x19, starting transfers between devices, _send(): return lax.ppermute(a, AXES, pairs)  29.1 us
    ppermute x19, waiting for transfers between devices, _send(): return lax.ppermute(a, AXES, pairs)  14.5 us
    pallas_call x5, Pallas kernels, score(): pl.pallas_call(functools.partial(_score_kernel, gain, len(xs)), out_shape...  13.2 us
    all_to_all x1, blocking collectives, local(): lax.all_to_all(packs, AXES, 0, 0, tiled=True, axis_index_groups=_plane_gr...  12.4 us
    pallas_call x4, Pallas kernels, weighted_sums(): pl.pallas_call(functools.partial(_sum_kernel, half, group, n_arr), out_sh...  10.3 us
    pallas_call x2, Pallas kernels, load_half(): pl.pallas_call(functools.partial(_load_kernel, gain), out_shape=(jax.Shap...  2.55 us
    unnamed x6, local copies, waits for them, and re-layouts  2.2 us
  transfers between devices with their start and end apart: 19, of which 7 were waited for; matrix products, arithmetic and copies ran while one was open for 0% of the time, Pallas kernels for 26%

profile of v7, /device:TPU:1, one launch (start us, length us, event | category | flops | bytes accessed | tf_op | source)
XLA Modules:
  0.0 86.5 jit_solution(17784828875604249028)
XLA Ops:
  0.0 1.4 %collective-permute-start.3 = (bf16[2048,1024]{1,0:T(8,128)(2,1)}, bf16[2048,1024]{1,0:T(8,128)(2,1)S(1)}, u32[]{:S(2)}, u32[]{:S(2)}) collective-permute-start(bf16[2048,1024]{1,0:T(8,128)(2,1)} %refs_4_.1), channel_id=1, source_target_pairs={{0,1},{1,0},{2,3},{3,2},{4,5},{5,4},{6,7},{7,6},{8,9},{9,8},{10,11... | collective-permute-start | bytes 12582920 | tf_op jit(solution)/shard_map/ppermute | solution.py:38
  1.4 1.3 %collective-permute-start = (bf16[128,1024]{1,0:T(8,128)(2,1)}, bf16[128,1024]{1,0:T(8,128)(2,1)S(1)}, u32[]{:S(2)}, u32[]{:S(2)}) collective-permute-start(bf16[128,1024]{1,0:T(8,128)(2,1)} %refs_0_.1), channel_id=1, source_target_pairs={{0,2},{1,9},{2,4},{3,11},{4,6},{5,13},{6,0},{7,15},{8,10},{9,65},{... | collective-permute-start | bytes 786440 | tf_op jit(solution)/shard_map/ppermute | solution.py:38
  2.7 1.4 %collective-permute-start.2 = (bf16[128,1024]{1,0:T(8,128)(2,1)}, bf16[128,1024]{1,0:T(8,128)(2,1)S(1)}, u32[]{:S(2)}, u32[]{:S(2)}) collective-permute-start(bf16[128,1024]{1,0:T(8,128)(2,1)} %refs_0_.1), channel_id=1, source_target_pairs={{0,6},{1,73},{2,0},{3,75},{4,2},{5,77},{6,4},{7,79},{8,14},{9,1},{... | collective-permute-start | bytes 786440 | tf_op jit(solution)/shard_map/ppermute | solution.py:38
  4.1 1.6 %collective-permute-start.1 = (bf16[128,1024]{1,0:T(8,128)(2,1)}, bf16[128,1024]{1,0:T(8,128)(2,1)S(1)}, u32[]{:S(2)}, u32[]{:S(2)}) collective-permute-start(bf16[128,1024]{1,0:T(8,128)(2,1)} %refs_0_.1), channel_id=1, source_target_pairs={{0,4},{1,65},{2,6},{3,67},{4,0},{5,69},{6,2},{7,71},{8,12},{9,73},... | collective-permute-start | bytes 786440 | tf_op jit(solution)/shard_map/ppermute | solution.py:38
  5.7 2.2 %copy-done = bf16[2048,1024]{1,0:T(8,128)(2,1)S(1)} copy-done((bf16[2048,1024]{1,0:T(8,128)(2,1)S(1)}, bf16[2048,1024]{1,0:T(8,128)(2,1)}, u32[]{:S(2)}) %copy-start) | copy-done | bytes 4194328
  7.9 1.3 %load_half.2 = (bf16[1024,1024]{1,0:T(8,128)(2,1)S(1)}, f32[1024,128]{1,0:T(8,128)S(1)}) custom-call(s32[1]{0:T(128)} %bitcast.id_ref, bf16[2048,1024]{1,0:T(8,128)(2,1)S(1)} %copy-done), custom_call_target="tpu_custom_call" | custom-call | flops 1024 | bytes 1024 | tf_op jit(solution)/shard_map/load_half/pallas_call | solution.py:86
  9.2 0.0 collective-permute-done.refs_1_
  9.3 1.4 %collective-permute-start.4 = (bf16[256,1024]{1,0:T(8,128)(2,1)S(1)}, bf16[256,1024]{1,0:T(8,128)(2,1)S(1)}, u32[]{:S(2)}, u32[]{:S(2)}) collective-permute-start(bf16[256,1024]{1,0:T(8,128)(2,1)S(1)} %join.2.refs_0_), channel_id=1, source_target_pairs={{0,8},{1,3},{2,10},{3,5},{4,12},{5,7},{6,14},{7,1},{8,64},{9,11},{... | collective-permute-start | bytes 1572872 | tf_op jit(solution)/shard_map/ppermute | solution.py:38
  10.6 0.0 collective-permute-done.2.refs_1_
  10.6 1.6 %collective-permute-done.1.refs_0_ = bf16[128,1024]{1,0:T(8,128)(2,1)S(1)} collective-permute-done((bf16[128,1024]{1,0:T(8,128)(2,1)}, bf16[128,1024]{1,0:T(8,128)(2,1)S(1)}, u32[]{:S(2)}, u32[]{:S(2)}) %collective-permute-start.1) | collective-permute-done | bytes 262176 | tf_op jit(solution)/shard_map/ppermute | solution.py:38
  12.3 2.5 %collective-permute-start.5 = (bf16[256,1024]{1,0:T(8,128)(2,1)S(1)}, bf16[256,1024]{1,0:T(8,128)(2,1)S(1)}, u32[]{:S(2)}, u32[]{:S(2)}) collective-permute-start(bf16[256,1024]{1,0:T(8,128)(2,1)S(1)} %join.3.refs_1_), channel_id=1, source_target_pairs={{0,72},{1,7},{2,74},{3,1},{4,76},{5,3},{6,78},{7,5},{8,0},{9,15},{... | collective-permute-start | bytes 1572872 | tf_op jit(solution)/shard_map/ppermute | solution.py:38
  14.8 0.5 collective-permute-start.7
  15.2 1.0 %collective-permute-start.6 = (bf16[256,1024]{1,0:T(8,128)(2,1)S(1)}, bf16[256,1024]{1,0:T(8,128)(2,1)S(1)}, u32[]{:S(2)}, u32[]{:S(2)}) collective-permute-start(bf16[256,1024]{1,0:T(8,128)(2,1)S(1)} %join.3.refs_1_), channel_id=1, source_target_pairs={{0,8},{1,3},{2,10},{3,5},{4,12},{5,7},{6,14},{7,1},{8,64},{9,11},{... | collective-permute-start | bytes 1572872 | tf_op jit(solution)/shard_map/ppermute | solution.py:38
  16.3 1.3 %load_half.3 = (bf16[1024,1024]{1,0:T(8,128)(2,1)S(1)}, f32[1024,128]{1,0:T(8,128)S(1)}) custom-call(s32[1]{0:T(128)} %bitcast.id_ref, bf16[2048,1024]{1,0:T(8,128)(2,1)S(1)} %collective-permute-done.3.c_ref), custom_call_target="tpu_custom_call" | custom-call | flops 1024 | bytes 1024 | tf_op jit(solution)/shard_map/load_half/pallas_call | solution.py:86
  17.5 1.4 %collective-permute-done.4.refs_0_ = bf16[256,1024]{1,0:T(8,128)(2,1)S(1)} collective-permute-done((bf16[256,1024]{1,0:T(8,128)(2,1)S(1)}, bf16[256,1024]{1,0:T(8,128)(2,1)S(1)}, u32[]{:S(2)}, u32[]{:S(2)}) %collective-permute-start.4) | collective-permute-done | bytes 524320 | tf_op jit(solution)/shard_map/ppermute | solution.py:38
  18.9 0.0 collective-permute-start.8
  18.9 3.3 %score.5 = (bf16[2,1024,512]{2,1,0:T(8,128)(2,1)S(1)}, f32[8,512]{1,0:T(8,128)S(1)}, bf16[512,1024]{1,0:T(8,128)(2,1)S(1)}) custom-call(s32[1]{0:T(128)} %bitcast.id_ref, bf16[256,1024]{1,0:T(8,128)(2,1)S(1)} %join.2.refs_0_, bf16[256,1024]{1,0:T(8,128)(2,1)S(1)} %join.3.refs_1_, bf16[1024,1024]{1,0:T(8,128)(2,1)S(1)} %get-tuple-element.46.refs_2_.refs_1_, ...), custom_call_target="tpu_custom_call" | custom-call | flops 1024 | bytes 1024 | tf_op jit(solution)/shard_map/score/pallas_call | solution.py:186
  22.2 2.9 %collective-permute-start.9 = (bf16[256,1024]{1,0:T(8,128)(2,1)S(1)}, bf16[256,1024]{1,0:T(8,128)(2,1)S(1)}, u32[]{:S(2)}, u32[]{:S(2)}) collective-permute-start(bf16[256,1024]{1,0:T(8,128)(2,1)S(1)} %collective-permute-done.5.refs_1_), channel_id=1, source_target_pairs={{0,72},{1,7},{2,74},{3,1},{4,76},{5,3},{6,78},{7,5},{8,0},{9,15},{... | collective-permute-start | bytes 1572872 | tf_op jit(solution)/shard_map/ppermute | solution.py:38
  25.2 3.3 %score.6 = (bf16[2,1024,512]{2,1,0:T(8,128)(2,1)S(1)}, f32[8,512]{1,0:T(8,128)S(1)}, bf16[512,1024]{1,0:T(8,128)(2,1)S(1)}) custom-call(s32[1]{0:T(128)} %bitcast.id_ref, bf16[256,1024]{1,0:T(8,128)(2,1)S(1)} %collective-permute-done.4.refs_0_, bf16[256,1024]{1,0:T(8,128)(2,1)S(1)} %collective-permute-done.5.refs_1_, ...), custom_call_target="tpu_custom_call" | custom-call | flops 1024 | bytes 1024 | tf_op jit(solution)/shard_map/score/pallas_call | solution.py:186
  28.4 3.3 %score.7 = (bf16[2,1024,512]{2,1,0:T(8,128)(2,1)S(1)}, f32[8,512]{1,0:T(8,128)S(1)}, bf16[512,1024]{1,0:T(8,128)(2,1)S(1)}) custom-call(s32[1]{0:T(128)} %bitcast.id_ref, bf16[256,1024]{1,0:T(8,128)(2,1)S(1)} %collective-permute-done.6.refs_0_, bf16[256,1024]{1,0:T(8,128)(2,1)S(1)} %collective-permute-done.7.refs_1_, ...), custom_call_target="tpu_custom_call" | custom-call | flops 1024 | bytes 1024 | tf_op jit(solution)/shard_map/score/pallas_call | solution.py:186
  31.8 1.7 %score.8 = (bf16[2,1024,256]{2,1,0:T(8,128)(2,1)S(1)}, f32[8,256]{1,0:T(8,128)S(1)}, bf16[256,1024]{1,0:T(8,128)(2,1)S(1)}) custom-call(s32[1]{0:T(128)} %bitcast.id_ref, bf16[256,1024]{1,0:T(8,128)(2,1)S(1)} %collective-permute-done.8.refs_0_, bf16[1024,1024]{1,0:T(8,128)(2,1)S(1)} %get-tuple-element.46.refs_2_.refs_1_, ...), custom_call_target="tpu_custom_call" | custom-call | flops 1024 | bytes 1024 | tf_op jit(solution)/shard_map/score/pallas_call | solution.py:186
  33.5 1.7 %score.9 = (bf16[2,1024,256]{2,1,0:T(8,128)(2,1)S(1)}, f32[8,256]{1,0:T(8,128)S(1)}, bf16[256,1024]{1,0:T(8,128)(2,1)S(1)}) custom-call(s32[1]{0:T(128)} %bitcast.id_ref, bf16[256,1024]{1,0:T(8,128)(2,1)S(1)} %collective-permute-done.9.refs_0_, bf16[1024,1024]{1,0:T(8,128)(2,1)S(1)} %get-tuple-element.46.refs_2_.refs_1_, ...), custom_call_target="tpu_custom_call" | custom-call | flops 1024 | bytes 1024 | tf_op jit(solution)/shard_map/score/pallas_call | solution.py:186
  35.2 0.1 stats_pack.1
  35.3 12.4 %all_to_all.5.all_ref = f32[16,2,16,128]{3,2,1,0:T(8,128)S(1)} all-to-all(f32[16,2,16,128]{3,2,1,0:T(8,128)S(1)} %stats_pack.1), channel_id=1, replica_groups={{0,2,4,6,8,10,12,14,64,66,68,70,72,74,76,78},{1,3,5,7,9,11,13,15,65,67,..., dimensions={0} | all-to-all | bytes 524288 | tf_op jit(solution)/shard_map/all_to_all | solution.py:462
  47.7 0.1 stats_scale.1.refs_10_
  47.7 2.6 %sums_sib.2 = bf16[4,1056,128]{2,1,0:T(8,128)(2,1)S(1)} custom-call(bf16[2,1024,512]{2,1,0:T(8,128)(2,1)S(1)} %get-tuple-element.51.refs_0_, bf16[2,1024,512]{2,1,0:T(8,128)(2,1)S(1)} %get-tuple-element.56.refs_1_, bf16[2,1024,512]{2,1,0:T(8,128)(2,1)S(1)} %get-tuple-element.58.refs_2_, bf16[2,1024,256]{2,1,0:T(8,128)(2,1)S(1)} %get-tuple-element.60.refs_3_, ...), custom_call_target="tpu_custom_call" | custom-call | flops 1024 | bytes 1024 | tf_op jit(solution)/shard_map/sums_sib/pallas_call | solution.py:259
  50.4 3.7 %collective-permute-start.10 = (bf16[4,1056,128]{2,1,0:T(8,128)(2,1)S(1)}, bf16[4,1056,128]{2,1,0:T(8,128)(2,1)S(1)}, u32[]{:S(2)}, u32[]{:S(2)}) collective-permute-start(bf16[4,1056,128]{2,1,0:T(8,128)(2,1)S(1)} %sums_sib.2), channel_id=1, source_target_pairs={{0,1},{1,0},{2,3},{3,2},{4,5},{5,4},{6,7},{7,6},{8,9},{9,8},{10,11... | collective-permute-start | bytes 3244040 | tf_op jit(solution)/shard_map/ppermute | solution.py:38
  54.1 2.5 %sums_own.2 = (f32[4,1024,128]{2,1,0:T(8,128)S(1)}, f32[8,128]{1,0:T(8,128)S(1)}) custom-call(bf16[2,1024,512]{2,1,0:T(8,128)(2,1)S(1)} %get-tuple-element.51.refs_0_, bf16[2,1024,512]{2,1,0:T(8,128)(2,1)S(1)} %get-tuple-element.56.refs_1_, bf16[2,1024,512]{2,1,0:T(8,128)(2,1)S(1)} %get-tuple-element.58.refs_2_, ...), custom_call_target="tpu_custom_call" | custom-call | flops 42949672960 | bytes 1024 | tf_op jit(solution)/shard_map/sums_own/pallas_call | solution.py:259
  56.6 0.2 mix.2
  56.8 3.7 %collective-permute-start.15 = (bf16[1056,128]{1,0:T(8,128)(2,1)S(1)}, bf16[1056,128]{1,0:T(8,128)(2,1)S(1)}, u32[]{:S(2)}, u32[]{:S(2)}) collective-permute-start(bf16[1056,128]{1,0:T(8,128)(2,1)S(1)} %get-tuple-element.80), channel_id=1, source_target_pairs={{0,32},{1,33},{2,34},{3,35},{4,36},{5,37},{6,38},{7,39},{8,40},{9,... | collective-permute-start | bytes 811016 | tf_op jit(solution)/shard_map/ppermute | solution.py:38
  60.5 0.7 collective-permute-start.16
  61.2 1.9 %collective-permute-start.17 = (bf16[1056,128]{1,0:T(8,128)(2,1)S(1)}, bf16[1056,128]{1,0:T(8,128)(2,1)S(1)}, u32[]{:S(2)}, u32[]{:S(2)}) collective-permute-start(bf16[1056,128]{1,0:T(8,128)(2,1)S(1)} %get-tuple-element.82), channel_id=1, source_target_pairs={{0,48},{1,49},{2,50},{3,51},{4,52},{5,53},{6,54},{7,55},{8,56},{9,... | collective-permute-start | bytes 811016 | tf_op jit(solution)/shard_map/ppermute | solution.py:38
  63.2 2.6 %sums_sib.3 = bf16[4,1056,128]{2,1,0:T(8,128)(2,1)S(1)} custom-call(bf16[2,1024,512]{2,1,0:T(8,128)(2,1)S(1)} %get-tuple-element.51.refs_0_, bf16[2,1024,512]{2,1,0:T(8,128)(2,1)S(1)} %get-tuple-element.56.refs_1_, bf16[2,1024,512]{2,1,0:T(8,128)(2,1)S(1)} %get-tuple-element.58.refs_2_, bf16[2,1024,256]{2,1,0:T(8,128)(2,1)S(1)} %get-tuple-element.60.refs_3_, ...), custom_call_target="tpu_custom_call" | custom-call | flops 1024 | bytes 1024 | tf_op jit(solution)/shard_map/sums_sib/pallas_call | solution.py:259
  65.8 1.1 %collective-permute-start.11 = (bf16[4,1056,128]{2,1,0:T(8,128)(2,1)S(1)}, bf16[4,1056,128]{2,1,0:T(8,128)(2,1)S(1)}, u32[]{:S(2)}, u32[]{:S(2)}) collective-permute-start(bf16[4,1056,128]{2,1,0:T(8,128)(2,1)S(1)} %sums_sib.3), channel_id=1, source_target_pairs={{0,1},{1,0},{2,3},{3,2},{4,5},{5,4},{6,7},{7,6},{8,9},{9,8},{10,11... | collective-permute-start | bytes 3244040 | tf_op jit(solution)/shard_map/ppermute | solution.py:38
  66.9 2.5 %sums_own.3 = (f32[4,1024,128]{2,1,0:T(8,128)S(1)}, f32[8,128]{1,0:T(8,128)S(1)}) custom-call(bf16[2,1024,512]{2,1,0:T(8,128)(2,1)S(1)} %get-tuple-element.51.refs_0_, bf16[2,1024,512]{2,1,0:T(8,128)(2,1)S(1)} %get-tuple-element.56.refs_1_, bf16[2,1024,512]{2,1,0:T(8,128)(2,1)S(1)} %get-tuple-element.58.refs_2_, ...), custom_call_target="tpu_custom_call" | custom-call | flops 42949672960 | bytes 1024 | tf_op jit(solution)/shard_map/sums_own/pallas_call | solution.py:259
  69.4 0.0 copy-start.1
  69.4 0.2 mix.3
  69.6 0.1 collective-permute-start.12
  69.7 0.3 collective-permute-start.13
  70.0 2.5 %collective-permute-start.14 = (bf16[1056,128]{1,0:T(8,128)(2,1)S(1)}, bf16[1056,128]{1,0:T(8,128)(2,1)S(1)}, u32[]{:S(2)}, u32[]{:S(2)}) collective-permute-start(bf16[1056,128]{1,0:T(8,128)(2,1)S(1)} %get-tuple-element.78), channel_id=1, source_target_pairs={{0,48},{1,49},{2,50},{3,51},{4,52},{5,53},{6,54},{7,55},{8,56},{9,... | collective-permute-start | bytes 811016 | tf_op jit(solution)/shard_map/ppermute | solution.py:38
  72.5 0.8 collective-permute-done.16.refs_1_
  73.2 0.3 collective-permute-done.17.refs_2_
  73.5 0.1 far_sum.1
  73.7 1.1 %collective-permute-start.18 = (bf16[1056,128]{1,0:T(8,128)(2,1)S(1)}, bf16[1056,128]{1,0:T(8,128)(2,1)S(1)}, u32[]{:S(2)}, u32[]{:S(2)}) collective-permute-start(bf16[1056,128]{1,0:T(8,128)(2,1)S(1)} %far_sum.1), channel_id=1, source_target_pairs={{0,64},{1,65},{2,66},{3,67},{4,68},{5,69},{6,70},{7,71},{8,72},{9,... | collective-permute-start | bytes 811016 | tf_op jit(solution)/shard_map/ppermute | solution.py:38
  74.8 4.4 %collective-permute-done.12.refs_0_ = bf16[1056,128]{1,0:T(8,128)(2,1)S(1)} collective-permute-done((bf16[1056,128]{1,0:T(8,128)(2,1)S(1)}, bf16[1056,128]{1,0:T(8,128)(2,1)S(1)}, u32[]{:S(2)}, u32[]{:S(2)}) %collective-permute-start.12) | collective-permute-done | bytes 270368 | tf_op jit(solution)/shard_map/ppermute | solution.py:38
  79.2 5.8 %collective-permute-done.13.refs_1_ = bf16[1056,128]{1,0:T(8,128)(2,1)S(1)} collective-permute-done((bf16[1056,128]{1,0:T(8,128)(2,1)S(1)}, bf16[1056,128]{1,0:T(8,128)(2,1)S(1)}, u32[]{:S(2)}, u32[]{:S(2)}) %collective-permute-start.13) | collective-permute-done | bytes 270368 | tf_op jit(solution)/shard_map/ppermute | solution.py:38
  85.0 0.2 collective-permute-done.14.refs_2_
  85.2 1.4 %finish.1 = f32[128,2048]{1,0:T(8,128)} custom-call(s32[1]{0:T(128)} %bitcast.id_ref, f32[1024,128]{1,0:T(8,128)S(1)} %get-tuple-element.74.keep_ref, f32[8,128]{1,0:T(8,128)S(1)} %get-tuple-element.75.refs_3_.cnt_ref, bf16[1056,128]{1,0:T(8,128)(2,1)S(1)} %collective-permute-done.12.refs_0_, bf16[1056,128]{1,0:T(8,128)(2,1)S(1)} %collective-permute-done.13.refs_1_, ...), custom_call_target="tpu_custom_call" | custom-call | tf_op jit(solution)/shard_map/finish/pallas_call | solution.py:336
  (16 shorter events, 0.1 us)
Async XLA Ops:
  0.0 16.3 %collective-permute-start.3 = (bf16[2048,1024]{1,0:T(8,128)(2,1)}, bf16[2048,1024]{1,0:T(8,128)(2,1)S(1)}, u32[]{:S(2)}, u32[]{:S(2)}) collective-permute-start(bf16[2048,1024]{1,0:T(8,128)(2,1)} %refs_4_.1), channel_id=1, source_target_pairs={{0,1},{1,0},{2,3},{3,2},{4,5},{5,4},{6,7},{7,6},{8,9},{9,8},{10,11... | collective-permute-start | bytes 12582920 | tf_op jit(solution)/shard_map/ppermute | solution.py:38
  1.4 7.8 %collective-permute-start = (bf16[128,1024]{1,0:T(8,128)(2,1)}, bf16[128,1024]{1,0:T(8,128)(2,1)S(1)}, u32[]{:S(2)}, u32[]{:S(2)}) collective-permute-start(bf16[128,1024]{1,0:T(8,128)(2,1)} %refs_0_.1), channel_id=1, source_target_pairs={{0,2},{1,9},{2,4},{3,11},{4,6},{5,13},{6,0},{7,15},{8,10},{9,65},{... | collective-permute-start | bytes 786440 | tf_op jit(solution)/shard_map/ppermute | solution.py:38
  2.7 7.9 %collective-permute-start.2 = (bf16[128,1024]{1,0:T(8,128)(2,1)}, bf16[128,1024]{1,0:T(8,128)(2,1)S(1)}, u32[]{:S(2)}, u32[]{:S(2)}) collective-permute-start(bf16[128,1024]{1,0:T(8,128)(2,1)} %refs_0_.1), channel_id=1, source_target_pairs={{0,6},{1,73},{2,0},{3,75},{4,2},{5,77},{6,4},{7,79},{8,14},{9,1},{... | collective-permute-start | bytes 786440 | tf_op jit(solution)/shard_map/ppermute | solution.py:38
  4.1 8.1 %collective-permute-start.1 = (bf16[128,1024]{1,0:T(8,128)(2,1)}, bf16[128,1024]{1,0:T(8,128)(2,1)S(1)}, u32[]{:S(2)}, u32[]{:S(2)}) collective-permute-start(bf16[128,1024]{1,0:T(8,128)(2,1)} %refs_0_.1), channel_id=1, source_target_pairs={{0,4},{1,65},{2,6},{3,67},{4,0},{5,69},{6,2},{7,71},{8,12},{9,73},... | collective-permute-start | bytes 786440 | tf_op jit(solution)/shard_map/ppermute | solution.py:38
  5.7 2.2 %copy-start = (bf16[2048,1024]{1,0:T(8,128)(2,1)S(1)}, bf16[2048,1024]{1,0:T(8,128)(2,1)}, u32[]{:S(2)}) copy-start(bf16[2048,1024]{1,0:T(8,128)(2,1)} %refs_4_.1) | copy-start | bytes 12582916
  7.9 1.3 %copy-start.2 = (bf16[128,1024]{1,0:T(8,128)(2,1)S(1)}, bf16[128,1024]{1,0:T(8,128)(2,1)}, u32[]{:S(2)}) copy-start(bf16[128,1024]{1,0:T(8,128)(2,1)} %refs_0_.1) | copy-start | bytes 786436
  9.3 9.7 %collective-permute-start.4 = (bf16[256,1024]{1,0:T(8,128)(2,1)S(1)}, bf16[256,1024]{1,0:T(8,128)(2,1)S(1)}, u32[]{:S(2)}, u32[]{:S(2)}) collective-permute-start(bf16[256,1024]{1,0:T(8,128)(2,1)S(1)} %join.2.refs_0_), channel_id=1, source_target_pairs={{0,8},{1,3},{2,10},{3,5},{4,12},{5,7},{6,14},{7,1},{8,64},{9,11},{... | collective-permute-start | bytes 1572872 | tf_op jit(solution)/shard_map/ppermute | solution.py:38
  12.3 10.0 %collective-permute-start.5 = (bf16[256,1024]{1,0:T(8,128)(2,1)S(1)}, bf16[256,1024]{1,0:T(8,128)(2,1)S(1)}, u32[]{:S(2)}, u32[]{:S(2)}) collective-permute-start(bf16[256,1024]{1,0:T(8,128)(2,1)S(1)} %join.3.refs_1_), channel_id=1, source_target_pairs={{0,72},{1,7},{2,74},{3,1},{4,76},{5,3},{6,78},{7,5},{8,0},{9,15},{... | collective-permute-start | bytes 1572872 | tf_op jit(solution)/shard_map/ppermute | solution.py:38
  14.8 13.6 %collective-permute-start.7 = (bf16[256,1024]{1,0:T(8,128)(2,1)S(1)}, bf16[256,1024]{1,0:T(8,128)(2,1)S(1)}, u32[]{:S(2)}, u32[]{:S(2)}) collective-permute-start(bf16[256,1024]{1,0:T(8,128)(2,1)S(1)} %join.2.refs_0_), channel_id=1, source_target_pairs={{0,72},{1,7},{2,74},{3,1},{4,76},{5,3},{6,78},{7,5},{8,0},{9,15},{... | collective-permute-start | bytes 1572872 | tf_op jit(solution)/shard_map/ppermute | solution.py:38
  15.2 13.2 %collective-permute-start.6 = (bf16[256,1024]{1,0:T(8,128)(2,1)S(1)}, bf16[256,1024]{1,0:T(8,128)(2,1)S(1)}, u32[]{:S(2)}, u32[]{:S(2)}) collective-permute-start(bf16[256,1024]{1,0:T(8,128)(2,1)S(1)} %join.3.refs_1_), channel_id=1, source_target_pairs={{0,8},{1,3},{2,10},{3,5},{4,12},{5,7},{6,14},{7,1},{8,64},{9,11},{... | collective-permute-start | bytes 1572872 | tf_op jit(solution)/shard_map/ppermute | solution.py:38
  18.9 12.8 %collective-permute-start.8 = (bf16[256,1024]{1,0:T(8,128)(2,1)S(1)}, bf16[256,1024]{1,0:T(8,128)(2,1)S(1)}, u32[]{:S(2)}, u32[]{:S(2)}) collective-permute-start(bf16[256,1024]{1,0:T(8,128)(2,1)S(1)} %collective-permute-done.4.refs_0_), channel_id=1, source_target_pairs={{0,8},{1,3},{2,10},{3,5},{4,12},{5,7},{6,14},{7,1},{8,64},{9,11},{... | collective-permute-start | bytes 1572872 | tf_op jit(solution)/shard_map/ppermute | solution.py:38
  22.2 11.2 %collective-permute-start.9 = (bf16[256,1024]{1,0:T(8,128)(2,1)S(1)}, bf16[256,1024]{1,0:T(8,128)(2,1)S(1)}, u32[]{:S(2)}, u32[]{:S(2)}) collective-permute-start(bf16[256,1024]{1,0:T(8,128)(2,1)S(1)} %collective-permute-done.5.refs_1_), channel_id=1, source_target_pairs={{0,72},{1,7},{2,74},{3,1},{4,76},{5,3},{6,78},{7,5},{8,0},{9,15},{... | collective-permute-start | bytes 1572872 | tf_op jit(solution)/shard_map/ppermute | solution.py:38
  50.4 6.2 %collective-permute-start.10 = (bf16[4,1056,128]{2,1,0:T(8,128)(2,1)S(1)}, bf16[4,1056,128]{2,1,0:T(8,128)(2,1)S(1)}, u32[]{:S(2)}, u32[]{:S(2)}) collective-permute-start(bf16[4,1056,128]{2,1,0:T(8,128)(2,1)S(1)} %sums_sib.2), channel_id=1, source_target_pairs={{0,1},{1,0},{2,3},{3,2},{4,5},{5,4},{6,7},{7,6},{8,9},{9,8},{10,11... | collective-permute-start | bytes 3244040 | tf_op jit(solution)/shard_map/ppermute | solution.py:38
  56.8 13.2 %collective-permute-start.15 = (bf16[1056,128]{1,0:T(8,128)(2,1)S(1)}, bf16[1056,128]{1,0:T(8,128)(2,1)S(1)}, u32[]{:S(2)}, u32[]{:S(2)}) collective-permute-start(bf16[1056,128]{1,0:T(8,128)(2,1)S(1)} %get-tuple-element.80), channel_id=1, source_target_pairs={{0,32},{1,33},{2,34},{3,35},{4,36},{5,37},{6,38},{7,39},{8,40},{9,... | collective-permute-start | bytes 811016 | tf_op jit(solution)/shard_map/ppermute | solution.py:38
  60.5 12.7 %collective-permute-start.16 = (bf16[1056,128]{1,0:T(8,128)(2,1)S(1)}, bf16[1056,128]{1,0:T(8,128)(2,1)S(1)}, u32[]{:S(2)}, u32[]{:S(2)}) collective-permute-start(bf16[1056,128]{1,0:T(8,128)(2,1)S(1)} %get-tuple-element.81), channel_id=1, source_target_pairs={{0,16},{1,17},{2,18},{3,19},{4,20},{5,21},{6,22},{7,23},{8,24},{9,... | collective-permute-start | bytes 811016 | tf_op jit(solution)/shard_map/ppermute | solution.py:38
  61.2 12.3 %collective-permute-start.17 = (bf16[1056,128]{1,0:T(8,128)(2,1)S(1)}, bf16[1056,128]{1,0:T(8,128)(2,1)S(1)}, u32[]{:S(2)}, u32[]{:S(2)}) collective-permute-start(bf16[1056,128]{1,0:T(8,128)(2,1)S(1)} %get-tuple-element.82), channel_id=1, source_target_pairs={{0,48},{1,49},{2,50},{3,51},{4,52},{5,53},{6,54},{7,55},{8,56},{9,... | collective-permute-start | bytes 811016 | tf_op jit(solution)/shard_map/ppermute | solution.py:38
  65.8 3.6 %collective-permute-start.11 = (bf16[4,1056,128]{2,1,0:T(8,128)(2,1)S(1)}, bf16[4,1056,128]{2,1,0:T(8,128)(2,1)S(1)}, u32[]{:S(2)}, u32[]{:S(2)}) collective-permute-start(bf16[4,1056,128]{2,1,0:T(8,128)(2,1)S(1)} %sums_sib.3), channel_id=1, source_target_pairs={{0,1},{1,0},{2,3},{3,2},{4,5},{5,4},{6,7},{7,6},{8,9},{9,8},{10,11... | collective-permute-start | bytes 3244040 | tf_op jit(solution)/shard_map/ppermute | solution.py:38
  69.4 15.7 %copy-start.1 = (bf16[2048,1024]{1,0:T(8,128)(2,1)S(1)}, bf16[2048,1024]{1,0:T(8,128)(2,1)}, u32[]{:S(2)}) copy-start(bf16[2048,1024]{1,0:T(8,128)(2,1)} %refs_4_.1) | copy-start | bytes 12582916
  69.6 9.6 %collective-permute-start.12 = (bf16[1056,128]{1,0:T(8,128)(2,1)S(1)}, bf16[1056,128]{1,0:T(8,128)(2,1)S(1)}, u32[]{:S(2)}, u32[]{:S(2)}) collective-permute-start(bf16[1056,128]{1,0:T(8,128)(2,1)S(1)} %get-tuple-element.76), channel_id=1, source_target_pairs={{0,32},{1,33},{2,34},{3,35},{4,36},{5,37},{6,38},{7,39},{8,40},{9,... | collective-permute-start | bytes 811016 | tf_op jit(solution)/shard_map/ppermute | solution.py:38
  69.7 15.3 %collective-permute-start.13 = (bf16[1056,128]{1,0:T(8,128)(2,1)S(1)}, bf16[1056,128]{1,0:T(8,128)(2,1)S(1)}, u32[]{:S(2)}, u32[]{:S(2)}) collective-permute-start(bf16[1056,128]{1,0:T(8,128)(2,1)S(1)} %get-tuple-element.77), channel_id=1, source_target_pairs={{0,16},{1,17},{2,18},{3,19},{4,20},{5,21},{6,22},{7,23},{8,24},{9,... | collective-permute-start | bytes 811016 | tf_op jit(solution)/shard_map/ppermute | solution.py:38
  70.0 15.2 %collective-permute-start.14 = (bf16[1056,128]{1,0:T(8,128)(2,1)S(1)}, bf16[1056,128]{1,0:T(8,128)(2,1)S(1)}, u32[]{:S(2)}, u32[]{:S(2)}) collective-permute-start(bf16[1056,128]{1,0:T(8,128)(2,1)S(1)} %get-tuple-element.78), channel_id=1, source_target_pairs={{0,48},{1,49},{2,50},{3,51},{4,52},{5,53},{6,54},{7,55},{8,56},{9,... | collective-permute-start | bytes 811016 | tf_op jit(solution)/shard_map/ppermute | solution.py:38
  73.7 11.5 %collective-permute-start.18 = (bf16[1056,128]{1,0:T(8,128)(2,1)S(1)}, bf16[1056,128]{1,0:T(8,128)(2,1)S(1)}, u32[]{:S(2)}, u32[]{:S(2)}) collective-permute-start(bf16[1056,128]{1,0:T(8,128)(2,1)S(1)} %far_sum.1), channel_id=1, source_target_pairs={{0,64},{1,65},{2,66},{3,67},{4,68},{5,69},{6,70},{7,71},{8,72},{9,... | collective-permute-start | bytes 811016 | tf_op jit(solution)/shard_map/ppermute | solution.py:38

commit v8 on v7

--- a/solution.py
+++ b/solution.py
@@ -436,8 +436,6 @@
     up_a, down_b = send_second(line_a, 1), send_second(line_b, 3)
     sib, sib_norm = load_half(ident, whole[1], 4, gain)
     cents = (own, sib)
-    up_a, sib_norm = lax.optimization_barrier((up_a, sib_norm))
-    far_a = send_second(up_a, 1)
     norms = (own_norm, sib_norm)
     up_b, down_a = send_second(line_b, 1), send_second(line_a, 3)
 
@@ -450,8 +448,8 @@
         xs.append(xp)
 
     run(line_a, line_b)
-    down_b, stats[0] = lax.optimization_barrier((down_b, stats[0]))
-    far_b = send_second(down_b, 3)
+    up_a, down_b, stats[0] = lax.optimization_barrier((up_a, down_b, stats[0]))
+    far_b, far_a = send_second(down_b, 3), send_second(up_a, 1)
     run(up_a, down_b)
     run(up_b, down_a)
     run(far_a)

time: 86.7 us -> 86.7 us (level)
  waiting for transfers between devices: 14.5 us -> 13.4 us
    ppermute x19, waiting for transfers between devices: 14.5 us -> 13.4 us  [_send(): return lax.ppermute(a, AXES, pairs)]
  transfers between devices with their start and end apart: 19 -> 19, of which waited for: 7 -> 8; matrix products, arithmetic and copies ran while one was open for 0% -> 0% of each run, Pallas kernels for 26% -> 26%
where the time goes in v8:
time: 86.7 us; the launch traced here: 86.5 us
  starting transfers between devices  29.5 us (34%)
  Pallas kernels  28.2 us (33%)
  waiting for transfers between devices  13.4 us (15%)
  blocking collectives  13 us (15%)
  local copies, waits for them, and re-layouts  2.2 us (3%)
    ppermute x19, starting transfers between devices, _send(): return lax.ppermute(a, AXES, pairs)  29.5 us
    ppermute x19, waiting for transfers between devices, _send(): return lax.ppermute(a, AXES, pairs)  13.4 us
    pallas_call x5, Pallas kernels, score(): pl.pallas_call(functools.partial(_score_kernel, gain, len(xs)), out_shape...  13.2 us
    all_to_all x1, blocking collectives, local(): lax.all_to_all(packs, AXES, 0, 0, tiled=True, axis_index_groups=_plane_gr...  13 us
    pallas_call x4, Pallas kernels, weighted_sums(): pl.pallas_call(functools.partial(_sum_kernel, half, group, n_arr), out_sh...  10.3 us
    pallas_call x2, Pallas kernels, load_half(): pl.pallas_call(functools.partial(_load_kernel, gain), out_shape=(jax.Shap...  2.55 us
    unnamed x6, local copies, waits for them, and re-layouts  2.2 us
  transfers between devices with their start and end apart: 19, of which 8 were waited for; matrix products, arithmetic and copies ran while one was open for 0% of the time, Pallas kernels for 26%

profile of v8, /device:TPU:1, one launch (start us, length us, event | category | flops | bytes accessed | tf_op | source)
XLA Modules:
  0.0 86.5 jit_solution(12376579393647332470)
XLA Ops:
  0.0 1.4 %collective-permute-start.3 = (bf16[2048,1024]{1,0:T(8,128)(2,1)}, bf16[2048,1024]{1,0:T(8,128)(2,1)S(1)}, u32[]{:S(2)}, u32[]{:S(2)}) collective-permute-start(bf16[2048,1024]{1,0:T(8,128)(2,1)} %refs_4_.1), channel_id=1, source_target_pairs={{0,1},{1,0},{2,3},{3,2},{4,5},{5,4},{6,7},{7,6},{8,9},{9,8},{10,11... | collective-permute-start | bytes 12582920 | tf_op jit(solution)/shard_map/ppermute | solution.py:38
  1.4 1.3 %collective-permute-start = (bf16[128,1024]{1,0:T(8,128)(2,1)}, bf16[128,1024]{1,0:T(8,128)(2,1)S(1)}, u32[]{:S(2)}, u32[]{:S(2)}) collective-permute-start(bf16[128,1024]{1,0:T(8,128)(2,1)} %refs_0_.1), channel_id=1, source_target_pairs={{0,2},{1,9},{2,4},{3,11},{4,6},{5,13},{6,0},{7,15},{8,10},{9,65},{... | collective-permute-start | bytes 786440 | tf_op jit(solution)/shard_map/ppermute | solution.py:38
  2.7 1.4 %collective-permute-start.2 = (bf16[128,1024]{1,0:T(8,128)(2,1)}, bf16[128,1024]{1,0:T(8,128)(2,1)S(1)}, u32[]{:S(2)}, u32[]{:S(2)}) collective-permute-start(bf16[128,1024]{1,0:T(8,128)(2,1)} %refs_0_.1), channel_id=1, source_target_pairs={{0,6},{1,73},{2,0},{3,75},{4,2},{5,77},{6,4},{7,79},{8,14},{9,1},{... | collective-permute-start | bytes 786440 | tf_op jit(solution)/shard_map/ppermute | solution.py:38
  4.1 1.6 %collective-permute-start.1 = (bf16[128,1024]{1,0:T(8,128)(2,1)}, bf16[128,1024]{1,0:T(8,128)(2,1)S(1)}, u32[]{:S(2)}, u32[]{:S(2)}) collective-permute-start(bf16[128,1024]{1,0:T(8,128)(2,1)} %refs_0_.1), channel_id=1, source_target_pairs={{0,4},{1,65},{2,6},{3,67},{4,0},{5,69},{6,2},{7,71},{8,12},{9,73},... | collective-permute-start | bytes 786440 | tf_op jit(solution)/shard_map/ppermute | solution.py:38
  5.7 2.2 %copy-done = bf16[2048,1024]{1,0:T(8,128)(2,1)S(1)} copy-done((bf16[2048,1024]{1,0:T(8,128)(2,1)S(1)}, bf16[2048,1024]{1,0:T(8,128)(2,1)}, u32[]{:S(2)}) %copy-start) | copy-done | bytes 4194328
  7.9 1.3 %load_half.2 = (bf16[1024,1024]{1,0:T(8,128)(2,1)S(1)}, f32[1024,128]{1,0:T(8,128)S(1)}) custom-call(s32[1]{0:T(128)} %bitcast.id_ref, bf16[2048,1024]{1,0:T(8,128)(2,1)S(1)} %copy-done), custom_call_target="tpu_custom_call" | custom-call | flops 1024 | bytes 1024 | tf_op jit(solution)/shard_map/load_half/pallas_call | solution.py:86
  9.2 0.0 collective-permute-done.refs_1_
  9.3 1.4 %collective-permute-start.4 = (bf16[256,1024]{1,0:T(8,128)(2,1)S(1)}, bf16[256,1024]{1,0:T(8,128)(2,1)S(1)}, u32[]{:S(2)}, u32[]{:S(2)}) collective-permute-start(bf16[256,1024]{1,0:T(8,128)(2,1)S(1)} %join.2.refs_0_), channel_id=1, source_target_pairs={{0,8},{1,3},{2,10},{3,5},{4,12},{5,7},{6,14},{7,1},{8,64},{9,11},{... | collective-permute-start | bytes 1572872 | tf_op jit(solution)/shard_map/ppermute | solution.py:38
  10.6 1.6 %collective-permute-done.1.refs_0_ = bf16[128,1024]{1,0:T(8,128)(2,1)S(1)} collective-permute-done((bf16[128,1024]{1,0:T(8,128)(2,1)}, bf16[128,1024]{1,0:T(8,128)(2,1)S(1)}, u32[]{:S(2)}, u32[]{:S(2)}) %collective-permute-start.1) | collective-permute-done | bytes 262176 | tf_op jit(solution)/shard_map/ppermute | solution.py:38
  12.3 2.5 %collective-permute-start.5 = (bf16[256,1024]{1,0:T(8,128)(2,1)S(1)}, bf16[256,1024]{1,0:T(8,128)(2,1)S(1)}, u32[]{:S(2)}, u32[]{:S(2)}) collective-permute-start(bf16[256,1024]{1,0:T(8,128)(2,1)S(1)} %join.3.refs_1_), channel_id=1, source_target_pairs={{0,72},{1,7},{2,74},{3,1},{4,76},{5,3},{6,78},{7,5},{8,0},{9,15},{... | collective-permute-start | bytes 1572872 | tf_op jit(solution)/shard_map/ppermute | solution.py:38
  14.8 0.5 collective-permute-start.7
  15.2 1.0 %collective-permute-start.6 = (bf16[256,1024]{1,0:T(8,128)(2,1)S(1)}, bf16[256,1024]{1,0:T(8,128)(2,1)S(1)}, u32[]{:S(2)}, u32[]{:S(2)}) collective-permute-start(bf16[256,1024]{1,0:T(8,128)(2,1)S(1)} %join.3.refs_1_), channel_id=1, source_target_pairs={{0,8},{1,3},{2,10},{3,5},{4,12},{5,7},{6,14},{7,1},{8,64},{9,11},{... | collective-permute-start | bytes 1572872 | tf_op jit(solution)/shard_map/ppermute | solution.py:38
  16.3 1.3 %load_half.3 = (bf16[1024,1024]{1,0:T(8,128)(2,1)S(1)}, f32[1024,128]{1,0:T(8,128)S(1)}) custom-call(s32[1]{0:T(128)} %bitcast.id_ref, bf16[2048,1024]{1,0:T(8,128)(2,1)S(1)} %collective-permute-done.3.c_ref), custom_call_target="tpu_custom_call" | custom-call | flops 1024 | bytes 1024 | tf_op jit(solution)/shard_map/load_half/pallas_call | solution.py:86
  17.5 3.3 %score.5 = (bf16[2,1024,512]{2,1,0:T(8,128)(2,1)S(1)}, f32[8,512]{1,0:T(8,128)S(1)}, bf16[512,1024]{1,0:T(8,128)(2,1)S(1)}) custom-call(s32[1]{0:T(128)} %bitcast.id_ref, bf16[256,1024]{1,0:T(8,128)(2,1)S(1)} %join.2.refs_0_, bf16[256,1024]{1,0:T(8,128)(2,1)S(1)} %join.3.refs_1_, bf16[1024,1024]{1,0:T(8,128)(2,1)S(1)} %get-tuple-element.45.refs_2_.refs_1_, ...), custom_call_target="tpu_custom_call" | custom-call | flops 1024 | bytes 1024 | tf_op jit(solution)/shard_map/score/pallas_call | solution.py:186
  20.8 0.1 collective-permute-done.5.refs_1_
  20.9 0.8 collective-permute-start.8
  21.7 2.7 %collective-permute-start.9 = (bf16[256,1024]{1,0:T(8,128)(2,1)S(1)}, bf16[256,1024]{1,0:T(8,128)(2,1)S(1)}, u32[]{:S(2)}, u32[]{:S(2)}) collective-permute-start(bf16[256,1024]{1,0:T(8,128)(2,1)S(1)} %collective-permute-done.5.refs_1_), channel_id=1, source_target_pairs={{0,72},{1,7},{2,74},{3,1},{4,76},{5,3},{6,78},{7,5},{8,0},{9,15},{... | collective-permute-start | bytes 1572872 | tf_op jit(solution)/shard_map/ppermute | solution.py:38
  24.3 3.3 %score.6 = (bf16[2,1024,512]{2,1,0:T(8,128)(2,1)S(1)}, f32[8,512]{1,0:T(8,128)S(1)}, bf16[512,1024]{1,0:T(8,128)(2,1)S(1)}) custom-call(s32[1]{0:T(128)} %bitcast.id_ref, bf16[256,1024]{1,0:T(8,128)(2,1)S(1)} %collective-permute-done.4.refs_0_, bf16[256,1024]{1,0:T(8,128)(2,1)S(1)} %collective-permute-done.5.refs_1_, ...), custom_call_target="tpu_custom_call" | custom-call | flops 1024 | bytes 1024 | tf_op jit(solution)/shard_map/score/pallas_call | solution.py:186
  27.6 3.3 %score.7 = (bf16[2,1024,512]{2,1,0:T(8,128)(2,1)S(1)}, f32[8,512]{1,0:T(8,128)S(1)}, bf16[512,1024]{1,0:T(8,128)(2,1)S(1)}) custom-call(s32[1]{0:T(128)} %bitcast.id_ref, bf16[256,1024]{1,0:T(8,128)(2,1)S(1)} %collective-permute-done.6.refs_0_, bf16[256,1024]{1,0:T(8,128)(2,1)S(1)} %collective-permute-done.7.refs_1_, ...), custom_call_target="tpu_custom_call" | custom-call | flops 1024 | bytes 1024 | tf_op jit(solution)/shard_map/score/pallas_call | solution.py:186
  30.9 0.3 collective-permute-done.8.refs_0_
  31.2 1.7 %score.8 = (bf16[2,1024,256]{2,1,0:T(8,128)(2,1)S(1)}, f32[8,256]{1,0:T(8,128)S(1)}, bf16[256,1024]{1,0:T(8,128)(2,1)S(1)}) custom-call(s32[1]{0:T(128)} %bitcast.id_ref, bf16[256,1024]{1,0:T(8,128)(2,1)S(1)} %collective-permute-done.8.refs_0_, bf16[1024,1024]{1,0:T(8,128)(2,1)S(1)} %get-tuple-element.45.refs_2_.refs_1_, ...), custom_call_target="tpu_custom_call" | custom-call | flops 1024 | bytes 1024 | tf_op jit(solution)/shard_map/score/pallas_call | solution.py:186
  32.9 1.7 %score.9 = (bf16[2,1024,256]{2,1,0:T(8,128)(2,1)S(1)}, f32[8,256]{1,0:T(8,128)S(1)}, bf16[256,1024]{1,0:T(8,128)(2,1)S(1)}) custom-call(s32[1]{0:T(128)} %bitcast.id_ref, bf16[256,1024]{1,0:T(8,128)(2,1)S(1)} %collective-permute-done.9.refs_0_, bf16[1024,1024]{1,0:T(8,128)(2,1)S(1)} %get-tuple-element.45.refs_2_.refs_1_, ...), custom_call_target="tpu_custom_call" | custom-call | flops 1024 | bytes 1024 | tf_op jit(solution)/shard_map/score/pallas_call | solution.py:186
  34.6 0.1 stats_pack.1
  34.7 13.0 %all_to_all.5.all_ref = f32[16,2,16,128]{3,2,1,0:T(8,128)S(1)} all-to-all(f32[16,2,16,128]{3,2,1,0:T(8,128)S(1)} %stats_pack.1), channel_id=1, replica_groups={{0,2,4,6,8,10,12,14,64,66,68,70,72,74,76,78},{1,3,5,7,9,11,13,15,65,67,..., dimensions={0} | all-to-all | bytes 524288 | tf_op jit(solution)/shard_map/all_to_all | solution.py:460
  47.7 0.1 stats_scale.1.refs_10_
  47.7 2.6 %sums_sib.2 = bf16[4,1056,128]{2,1,0:T(8,128)(2,1)S(1)} custom-call(bf16[2,1024,512]{2,1,0:T(8,128)(2,1)S(1)} %get-tuple-element.49.refs_0_, bf16[2,1024,512]{2,1,0:T(8,128)(2,1)S(1)} %get-tuple-element.54.refs_1_, bf16[2,1024,512]{2,1,0:T(8,128)(2,1)S(1)} %get-tuple-element.56.refs_2_, bf16[2,1024,256]{2,1,0:T(8,128)(2,1)S(1)} %get-tuple-element.58.refs_3_, ...), custom_call_target="tpu_custom_call" | custom-call | flops 1024 | bytes 1024 | tf_op jit(solution)/shard_map/sums_sib/pallas_call | solution.py:259
  50.4 3.7 %collective-permute-start.10 = (bf16[4,1056,128]{2,1,0:T(8,128)(2,1)S(1)}, bf16[4,1056,128]{2,1,0:T(8,128)(2,1)S(1)}, u32[]{:S(2)}, u32[]{:S(2)}) collective-permute-start(bf16[4,1056,128]{2,1,0:T(8,128)(2,1)S(1)} %sums_sib.2), channel_id=1, source_target_pairs={{0,1},{1,0},{2,3},{3,2},{4,5},{5,4},{6,7},{7,6},{8,9},{9,8},{10,11... | collective-permute-start | bytes 3244040 | tf_op jit(solution)/shard_map/ppermute | solution.py:38
  54.1 2.5 %sums_own.2 = (f32[4,1024,128]{2,1,0:T(8,128)S(1)}, f32[8,128]{1,0:T(8,128)S(1)}) custom-call(bf16[2,1024,512]{2,1,0:T(8,128)(2,1)S(1)} %get-tuple-element.49.refs_0_, bf16[2,1024,512]{2,1,0:T(8,128)(2,1)S(1)} %get-tuple-element.54.refs_1_, bf16[2,1024,512]{2,1,0:T(8,128)(2,1)S(1)} %get-tuple-element.56.refs_2_, ...), custom_call_target="tpu_custom_call" | custom-call | flops 42949672960 | bytes 1024 | tf_op jit(solution)/shard_map/sums_own/pallas_call | solution.py:259
  56.6 0.2 mix.2
  56.8 3.7 %collective-permute-start.15 = (bf16[1056,128]{1,0:T(8,128)(2,1)S(1)}, bf16[1056,128]{1,0:T(8,128)(2,1)S(1)}, u32[]{:S(2)}, u32[]{:S(2)}) collective-permute-start(bf16[1056,128]{1,0:T(8,128)(2,1)S(1)} %get-tuple-element.78), channel_id=1, source_target_pairs={{0,32},{1,33},{2,34},{3,35},{4,36},{5,37},{6,38},{7,39},{8,40},{9,... | collective-permute-start | bytes 811016 | tf_op jit(solution)/shard_map/ppermute | solution.py:38
  60.5 0.7 collective-permute-start.16
  61.2 1.9 %collective-permute-start.17 = (bf16[1056,128]{1,0:T(8,128)(2,1)S(1)}, bf16[1056,128]{1,0:T(8,128)(2,1)S(1)}, u32[]{:S(2)}, u32[]{:S(2)}) collective-permute-start(bf16[1056,128]{1,0:T(8,128)(2,1)S(1)} %get-tuple-element.80), channel_id=1, source_target_pairs={{0,48},{1,49},{2,50},{3,51},{4,52},{5,53},{6,54},{7,55},{8,56},{9,... | collective-permute-start | bytes 811016 | tf_op jit(solution)/shard_map/ppermute | solution.py:38
  63.2 2.6 %sums_sib.3 = bf16[4,1056,128]{2,1,0:T(8,128)(2,1)S(1)} custom-call(bf16[2,1024,512]{2,1,0:T(8,128)(2,1)S(1)} %get-tuple-element.49.refs_0_, bf16[2,1024,512]{2,1,0:T(8,128)(2,1)S(1)} %get-tuple-element.54.refs_1_, bf16[2,1024,512]{2,1,0:T(8,128)(2,1)S(1)} %get-tuple-element.56.refs_2_, bf16[2,1024,256]{2,1,0:T(8,128)(2,1)S(1)} %get-tuple-element.58.refs_3_, ...), custom_call_target="tpu_custom_call" | custom-call | flops 1024 | bytes 1024 | tf_op jit(solution)/shard_map/sums_sib/pallas_call | solution.py:259
  65.8 1.1 %collective-permute-start.11 = (bf16[4,1056,128]{2,1,0:T(8,128)(2,1)S(1)}, bf16[4,1056,128]{2,1,0:T(8,128)(2,1)S(1)}, u32[]{:S(2)}, u32[]{:S(2)}) collective-permute-start(bf16[4,1056,128]{2,1,0:T(8,128)(2,1)S(1)} %sums_sib.3), channel_id=1, source_target_pairs={{0,1},{1,0},{2,3},{3,2},{4,5},{5,4},{6,7},{7,6},{8,9},{9,8},{10,11... | collective-permute-start | bytes 3244040 | tf_op jit(solution)/shard_map/ppermute | solution.py:38
  66.9 2.5 %sums_own.3 = (f32[4,1024,128]{2,1,0:T(8,128)S(1)}, f32[8,128]{1,0:T(8,128)S(1)}) custom-call(bf16[2,1024,512]{2,1,0:T(8,128)(2,1)S(1)} %get-tuple-element.49.refs_0_, bf16[2,1024,512]{2,1,0:T(8,128)(2,1)S(1)} %get-tuple-element.54.refs_1_, bf16[2,1024,512]{2,1,0:T(8,128)(2,1)S(1)} %get-tuple-element.56.refs_2_, ...), custom_call_target="tpu_custom_call" | custom-call | flops 42949672960 | bytes 1024 | tf_op jit(solution)/shard_map/sums_own/pallas_call | solution.py:259
  69.4 0.0 copy-start.1
  69.4 0.2 mix.3
  69.6 0.1 collective-permute-start.12
  69.7 0.3 collective-permute-start.13
  70.0 2.5 %collective-permute-start.14 = (bf16[1056,128]{1,0:T(8,128)(2,1)S(1)}, bf16[1056,128]{1,0:T(8,128)(2,1)S(1)}, u32[]{:S(2)}, u32[]{:S(2)}) collective-permute-start(bf16[1056,128]{1,0:T(8,128)(2,1)S(1)} %get-tuple-element.76), channel_id=1, source_target_pairs={{0,48},{1,49},{2,50},{3,51},{4,52},{5,53},{6,54},{7,55},{8,56},{9,... | collective-permute-start | bytes 811016 | tf_op jit(solution)/shard_map/ppermute | solution.py:38
  72.5 0.8 collective-permute-done.16.refs_1_
  73.2 0.3 collective-permute-done.17.refs_2_
  73.5 0.1 far_sum.1
  73.7 1.1 %collective-permute-start.18 = (bf16[1056,128]{1,0:T(8,128)(2,1)S(1)}, bf16[1056,128]{1,0:T(8,128)(2,1)S(1)}, u32[]{:S(2)}, u32[]{:S(2)}) collective-permute-start(bf16[1056,128]{1,0:T(8,128)(2,1)S(1)} %far_sum.1), channel_id=1, source_target_pairs={{0,64},{1,65},{2,66},{3,67},{4,68},{5,69},{6,70},{7,71},{8,72},{9,... | collective-permute-start | bytes 811016 | tf_op jit(solution)/shard_map/ppermute | solution.py:38
  74.8 4.4 %collective-permute-done.12.refs_0_ = bf16[1056,128]{1,0:T(8,128)(2,1)S(1)} collective-permute-done((bf16[1056,128]{1,0:T(8,128)(2,1)S(1)}, bf16[1056,128]{1,0:T(8,128)(2,1)S(1)}, u32[]{:S(2)}, u32[]{:S(2)}) %collective-permute-start.12) | collective-permute-done | bytes 270368 | tf_op jit(solution)/shard_map/ppermute | solution.py:38
  79.2 5.8 %collective-permute-done.13.refs_1_ = bf16[1056,128]{1,0:T(8,128)(2,1)S(1)} collective-permute-done((bf16[1056,128]{1,0:T(8,128)(2,1)S(1)}, bf16[1056,128]{1,0:T(8,128)(2,1)S(1)}, u32[]{:S(2)}, u32[]{:S(2)}) %collective-permute-start.13) | collective-permute-done | bytes 270368 | tf_op jit(solution)/shard_map/ppermute | solution.py:38
  85.0 0.2 collective-permute-done.14.refs_2_
  85.2 1.4 %finish.1 = f32[128,2048]{1,0:T(8,128)} custom-call(s32[1]{0:T(128)} %bitcast.id_ref, f32[1024,128]{1,0:T(8,128)S(1)} %get-tuple-element.72.keep_ref, f32[8,128]{1,0:T(8,128)S(1)} %get-tuple-element.73.refs_3_.cnt_ref, bf16[1056,128]{1,0:T(8,128)(2,1)S(1)} %collective-permute-done.12.refs_0_, bf16[1056,128]{1,0:T(8,128)(2,1)S(1)} %collective-permute-done.13.refs_1_, ...), custom_call_target="tpu_custom_call" | custom-call | tf_op jit(solution)/shard_map/finish/pallas_call | solution.py:336
  (16 shorter events, 0.1 us)
Async XLA Ops:
  0.0 16.3 %collective-permute-start.3 = (bf16[2048,1024]{1,0:T(8,128)(2,1)}, bf16[2048,1024]{1,0:T(8,128)(2,1)S(1)}, u32[]{:S(2)}, u32[]{:S(2)}) collective-permute-start(bf16[2048,1024]{1,0:T(8,128)(2,1)} %refs_4_.1), channel_id=1, source_target_pairs={{0,1},{1,0},{2,3},{3,2},{4,5},{5,4},{6,7},{7,6},{8,9},{9,8},{10,11... | collective-permute-start | bytes 12582920 | tf_op jit(solution)/shard_map/ppermute | solution.py:38
  1.4 7.8 %collective-permute-start = (bf16[128,1024]{1,0:T(8,128)(2,1)}, bf16[128,1024]{1,0:T(8,128)(2,1)S(1)}, u32[]{:S(2)}, u32[]{:S(2)}) collective-permute-start(bf16[128,1024]{1,0:T(8,128)(2,1)} %refs_0_.1), channel_id=1, source_target_pairs={{0,2},{1,9},{2,4},{3,11},{4,6},{5,13},{6,0},{7,15},{8,10},{9,65},{... | collective-permute-start | bytes 786440 | tf_op jit(solution)/shard_map/ppermute | solution.py:38
  2.7 7.9 %collective-permute-start.2 = (bf16[128,1024]{1,0:T(8,128)(2,1)}, bf16[128,1024]{1,0:T(8,128)(2,1)S(1)}, u32[]{:S(2)}, u32[]{:S(2)}) collective-permute-start(bf16[128,1024]{1,0:T(8,128)(2,1)} %refs_0_.1), channel_id=1, source_target_pairs={{0,6},{1,73},{2,0},{3,75},{4,2},{5,77},{6,4},{7,79},{8,14},{9,1},{... | collective-permute-start | bytes 786440 | tf_op jit(solution)/shard_map/ppermute | solution.py:38
  4.1 8.1 %collective-permute-start.1 = (bf16[128,1024]{1,0:T(8,128)(2,1)}, bf16[128,1024]{1,0:T(8,128)(2,1)S(1)}, u32[]{:S(2)}, u32[]{:S(2)}) collective-permute-start(bf16[128,1024]{1,0:T(8,128)(2,1)} %refs_0_.1), channel_id=1, source_target_pairs={{0,4},{1,65},{2,6},{3,67},{4,0},{5,69},{6,2},{7,71},{8,12},{9,73},... | collective-permute-start | bytes 786440 | tf_op jit(solution)/shard_map/ppermute | solution.py:38
  5.7 2.2 %copy-start = (bf16[2048,1024]{1,0:T(8,128)(2,1)S(1)}, bf16[2048,1024]{1,0:T(8,128)(2,1)}, u32[]{:S(2)}) copy-start(bf16[2048,1024]{1,0:T(8,128)(2,1)} %refs_4_.1) | copy-start | bytes 12582916
  7.9 1.3 %copy-start.2 = (bf16[128,1024]{1,0:T(8,128)(2,1)S(1)}, bf16[128,1024]{1,0:T(8,128)(2,1)}, u32[]{:S(2)}) copy-start(bf16[128,1024]{1,0:T(8,128)(2,1)} %refs_0_.1) | copy-start | bytes 786436
  9.3 11.6 %collective-permute-start.4 = (bf16[256,1024]{1,0:T(8,128)(2,1)S(1)}, bf16[256,1024]{1,0:T(8,128)(2,1)S(1)}, u32[]{:S(2)}, u32[]{:S(2)}) collective-permute-start(bf16[256,1024]{1,0:T(8,128)(2,1)S(1)} %join.2.refs_0_), channel_id=1, source_target_pairs={{0,8},{1,3},{2,10},{3,5},{4,12},{5,7},{6,14},{7,1},{8,64},{9,11},{... | collective-permute-start | bytes 1572872 | tf_op jit(solution)/shard_map/ppermute | solution.py:38
  12.3 8.6 %collective-permute-start.5 = (bf16[256,1024]{1,0:T(8,128)(2,1)S(1)}, bf16[256,1024]{1,0:T(8,128)(2,1)S(1)}, u32[]{:S(2)}, u32[]{:S(2)}) collective-permute-start(bf16[256,1024]{1,0:T(8,128)(2,1)S(1)} %join.3.refs_1_), channel_id=1, source_target_pairs={{0,72},{1,7},{2,74},{3,1},{4,76},{5,3},{6,78},{7,5},{8,0},{9,15},{... | collective-permute-start | bytes 1572872 | tf_op jit(solution)/shard_map/ppermute | solution.py:38
  14.8 12.8 %collective-permute-start.7 = (bf16[256,1024]{1,0:T(8,128)(2,1)S(1)}, bf16[256,1024]{1,0:T(8,128)(2,1)S(1)}, u32[]{:S(2)}, u32[]{:S(2)}) collective-permute-start(bf16[256,1024]{1,0:T(8,128)(2,1)S(1)} %join.2.refs_0_), channel_id=1, source_target_pairs={{0,72},{1,7},{2,74},{3,1},{4,76},{5,3},{6,78},{7,5},{8,0},{9,15},{... | collective-permute-start | bytes 1572872 | tf_op jit(solution)/shard_map/ppermute | solution.py:38
  15.2 12.4 %collective-permute-start.6 = (bf16[256,1024]{1,0:T(8,128)(2,1)S(1)}, bf16[256,1024]{1,0:T(8,128)(2,1)S(1)}, u32[]{:S(2)}, u32[]{:S(2)}) collective-permute-start(bf16[256,1024]{1,0:T(8,128)(2,1)S(1)} %join.3.refs_1_), channel_id=1, source_target_pairs={{0,8},{1,3},{2,10},{3,5},{4,12},{5,7},{6,14},{7,1},{8,64},{9,11},{... | collective-permute-start | bytes 1572872 | tf_op jit(solution)/shard_map/ppermute | solution.py:38
  20.9 10.3 %collective-permute-start.8 = (bf16[256,1024]{1,0:T(8,128)(2,1)S(1)}, bf16[256,1024]{1,0:T(8,128)(2,1)S(1)}, u32[]{:S(2)}, u32[]{:S(2)}) collective-permute-start(bf16[256,1024]{1,0:T(8,128)(2,1)S(1)} %collective-permute-done.4.refs_0_), channel_id=1, source_target_pairs={{0,8},{1,3},{2,10},{3,5},{4,12},{5,7},{6,14},{7,1},{8,64},{9,11},{... | collective-permute-start | bytes 1572872 | tf_op jit(solution)/shard_map/ppermute | solution.py:38
  21.7 11.2 %collective-permute-start.9 = (bf16[256,1024]{1,0:T(8,128)(2,1)S(1)}, bf16[256,1024]{1,0:T(8,128)(2,1)S(1)}, u32[]{:S(2)}, u32[]{:S(2)}) collective-permute-start(bf16[256,1024]{1,0:T(8,128)(2,1)S(1)} %collective-permute-done.5.refs_1_), channel_id=1, source_target_pairs={{0,72},{1,7},{2,74},{3,1},{4,76},{5,3},{6,78},{7,5},{8,0},{9,15},{... | collective-permute-start | bytes 1572872 | tf_op jit(solution)/shard_map/ppermute | solution.py:38
  50.4 6.2 %collective-permute-start.10 = (bf16[4,1056,128]{2,1,0:T(8,128)(2,1)S(1)}, bf16[4,1056,128]{2,1,0:T(8,128)(2,1)S(1)}, u32[]{:S(2)}, u32[]{:S(2)}) collective-permute-start(bf16[4,1056,128]{2,1,0:T(8,128)(2,1)S(1)} %sums_sib.2), channel_id=1, source_target_pairs={{0,1},{1,0},{2,3},{3,2},{4,5},{5,4},{6,7},{7,6},{8,9},{9,8},{10,11... | collective-permute-start | bytes 3244040 | tf_op jit(solution)/shard_map/ppermute | solution.py:38
  56.8 13.2 %collective-permute-start.15 = (bf16[1056,128]{1,0:T(8,128)(2,1)S(1)}, bf16[1056,128]{1,0:T(8,128)(2,1)S(1)}, u32[]{:S(2)}, u32[]{:S(2)}) collective-permute-start(bf16[1056,128]{1,0:T(8,128)(2,1)S(1)} %get-tuple-element.78), channel_id=1, source_target_pairs={{0,32},{1,33},{2,34},{3,35},{4,36},{5,37},{6,38},{7,39},{8,40},{9,... | collective-permute-start | bytes 811016 | tf_op jit(solution)/shard_map/ppermute | solution.py:38
  60.5 12.7 %collective-permute-start.16 = (bf16[1056,128]{1,0:T(8,128)(2,1)S(1)}, bf16[1056,128]{1,0:T(8,128)(2,1)S(1)}, u32[]{:S(2)}, u32[]{:S(2)}) collective-permute-start(bf16[1056,128]{1,0:T(8,128)(2,1)S(1)} %get-tuple-element.79), channel_id=1, source_target_pairs={{0,16},{1,17},{2,18},{3,19},{4,20},{5,21},{6,22},{7,23},{8,24},{9,... | collective-permute-start | bytes 811016 | tf_op jit(solution)/shard_map/ppermute | solution.py:38
  61.2 12.3 %collective-permute-start.17 = (bf16[1056,128]{1,0:T(8,128)(2,1)S(1)}, bf16[1056,128]{1,0:T(8,128)(2,1)S(1)}, u32[]{:S(2)}, u32[]{:S(2)}) collective-permute-start(bf16[1056,128]{1,0:T(8,128)(2,1)S(1)} %get-tuple-element.80), channel_id=1, source_target_pairs={{0,48},{1,49},{2,50},{3,51},{4,52},{5,53},{6,54},{7,55},{8,56},{9,... | collective-permute-start | bytes 811016 | tf_op jit(solution)/shard_map/ppermute | solution.py:38
  65.8 3.6 %collective-permute-start.11 = (bf16[4,1056,128]{2,1,0:T(8,128)(2,1)S(1)}, bf16[4,1056,128]{2,1,0:T(8,128)(2,1)S(1)}, u32[]{:S(2)}, u32[]{:S(2)}) collective-permute-start(bf16[4,1056,128]{2,1,0:T(8,128)(2,1)S(1)} %sums_sib.3), channel_id=1, source_target_pairs={{0,1},{1,0},{2,3},{3,2},{4,5},{5,4},{6,7},{7,6},{8,9},{9,8},{10,11... | collective-permute-start | bytes 3244040 | tf_op jit(solution)/shard_map/ppermute | solution.py:38
  69.4 15.7 %copy-start.1 = (bf16[2048,1024]{1,0:T(8,128)(2,1)S(1)}, bf16[2048,1024]{1,0:T(8,128)(2,1)}, u32[]{:S(2)}) copy-start(bf16[2048,1024]{1,0:T(8,128)(2,1)} %refs_4_.1) | copy-start | bytes 12582916
  69.6 9.6 %collective-permute-start.12 = (bf16[1056,128]{1,0:T(8,128)(2,1)S(1)}, bf16[1056,128]{1,0:T(8,128)(2,1)S(1)}, u32[]{:S(2)}, u32[]{:S(2)}) collective-permute-start(bf16[1056,128]{1,0:T(8,128)(2,1)S(1)} %get-tuple-element.74), channel_id=1, source_target_pairs={{0,32},{1,33},{2,34},{3,35},{4,36},{5,37},{6,38},{7,39},{8,40},{9,... | collective-permute-start | bytes 811016 | tf_op jit(solution)/shard_map/ppermute | solution.py:38
  69.7 15.3 %collective-permute-start.13 = (bf16[1056,128]{1,0:T(8,128)(2,1)S(1)}, bf16[1056,128]{1,0:T(8,128)(2,1)S(1)}, u32[]{:S(2)}, u32[]{:S(2)}) collective-permute-start(bf16[1056,128]{1,0:T(8,128)(2,1)S(1)} %get-tuple-element.75), channel_id=1, source_target_pairs={{0,16},{1,17},{2,18},{3,19},{4,20},{5,21},{6,22},{7,23},{8,24},{9,... | collective-permute-start | bytes 811016 | tf_op jit(solution)/shard_map/ppermute | solution.py:38
  70.0 15.2 %collective-permute-start.14 = (bf16[1056,128]{1,0:T(8,128)(2,1)S(1)}, bf16[1056,128]{1,0:T(8,128)(2,1)S(1)}, u32[]{:S(2)}, u32[]{:S(2)}) collective-permute-start(bf16[1056,128]{1,0:T(8,128)(2,1)S(1)} %get-tuple-element.76), channel_id=1, source_target_pairs={{0,48},{1,49},{2,50},{3,51},{4,52},{5,53},{6,54},{7,55},{8,56},{9,... | collective-permute-start | bytes 811016 | tf_op jit(solution)/shard_map/ppermute | solution.py:38
  73.7 11.5 %collective-permute-start.18 = (bf16[1056,128]{1,0:T(8,128)(2,1)S(1)}, bf16[1056,128]{1,0:T(8,128)(2,1)S(1)}, u32[]{:S(2)}, u32[]{:S(2)}) collective-permute-start(bf16[1056,128]{1,0:T(8,128)(2,1)S(1)} %far_sum.1), channel_id=1, source_target_pairs={{0,64},{1,65},{2,66},{3,67},{4,68},{5,69},{6,70},{7,71},{8,72},{9,... | collective-permute-start | bytes 811016 | tf_op jit(solution)/shard_map/ppermute | solution.py:38
